TPU v7x, 32 devices: a whole 2x2x4 slice. The times are simulated.
32 devices in a mesh: seq: 8 (over z, y), win: 4 (over x, core).
Axes of the slice: x: 2, y: 2, z: 4, core: 2. Of those that a mesh axis runs over, the one named last changes fastest.
Arguments:
- queries: bfloat16 [4096, 1024], P(('win', 'seq')), parts along dimension 0, may hold values from -6 to 6
- key_rows: bfloat16 [4096, 1024], P(('win', 'seq')), parts along dimension 0, may hold values from -6 to 6
- value_rows: bfloat16 [4096, 2048], P(('win', 'seq')), parts along dimension 0, may hold values from -6 to 6
- residual: bfloat16 [4096, 1024], P(('win', 'seq')), parts along dimension 0, may hold values from -6 to 6
- out_weight: bfloat16 [2048, 1024], P(None, 'seq'), may hold values from -0.125 to 0.125
- expert_in: bfloat16 [8, 1024, 768], P('seq'), may hold values from -0.1875 to 0.1875
- expert_out: bfloat16 [8, 384, 1024], P('seq'), may hold values from -0.3125 to 0.3125
- expert_ids: int32 [4096, 2], P(('win', 'seq')), parts along dimension 0, may hold values from 0 to 7, all different within a row; in each aligned block of 128 rows (0 to 127, 128 to 255, ...) at most 64 rows name the same one
- gate_values: float32 [4096, 2], P(('win', 'seq')), parts along dimension 0, may hold values from 0.2 to 1
Outputs:
- layer_out: bfloat16 [4096, 1024], P(('win', 'seq')), parts along dimension 0
There are 4 independent parts, one for each index of `win`. A program takes and returns all parts, laid end to end along the dimension named above; an argument that names none is the same for every part. Nothing has to cross between parts.
Inputs may be any that keep to these rules, and one draw needn't show every extreme that they name: `expert_ids`: the 2 ids of a row differ. Within the rows of one block of 128 tokens no expert is named by more than 64 rows, a bound that some block reaches. Every expert is named somewhere.
All inputs are finite; a program needn't handle non-finite values.
Results may differ from a plain program's by a relative error of at most 0.013.
Values may be sent and summed in bfloat16 or wider, within the bound.
No kernel may reach another device: no remote copies, remote signals or barrier semaphores. Data moves between devices by JAX's collectives and lax.ppermute only.
A program may use at most 128 MiB of HBM per device.

v0:
```python
import jax
import jax.numpy as jnp
from jax import lax
from jax.sharding import PartitionSpec as P

D = 1024
H = 16
DK = 64
DV = 128
HE = 384
TOP = 2


def carried_in(x, axis, join, neutral):
    place = lax.axis_index(axis)
    gathered = lax.all_gather(x.astype(jnp.bfloat16), axis)
    state = jnp.zeros_like(x) + jnp.asarray(neutral, x.dtype)

    def one(step, state):
        return join(state, lax.dynamic_index_in_dim(gathered, step, 0, False).astype(x.dtype))

    return lax.fori_loop(0, place, one, state)


def add_states(earlier, later):
    return earlier + later


def per_device(
    queries,
    key_rows,
    value_rows,
    residual,
    out_weight,
    expert_in,
    expert_out,
    expert_ids,
    gate_values,
):
    length = queries.shape[0]
    q_heads = queries.reshape(length, H, DK)
    k_heads = key_rows.reshape(length, H, DK)
    v_heads = value_rows.reshape(length, H, DV)
    local_state = jnp.einsum("thd,the->hde", k_heads, v_heads, preferred_element_type=jnp.float32)
    prefix = carried_in(local_state, "seq", add_states, jnp.zeros_like(local_state))
    causal = jnp.arange(length)[:, None] >= jnp.arange(length)[None, :]
    scores = jnp.einsum("thd,shd->hts", q_heads, k_heads, preferred_element_type=jnp.float32)
    scores = jnp.where(causal[None], scores, 0.0).astype(jnp.bfloat16)
    intra_sum = jnp.einsum("hts,she->the", scores, v_heads, preferred_element_type=jnp.float32)
    inter_sum = jnp.einsum(
        "thd,hde->the", q_heads.astype(jnp.float32), prefix, precision=lax.Precision.HIGHEST
    )
    position = (lax.axis_index("seq") * length + jnp.arange(length)).astype(jnp.float32)
    scaling = lax.rsqrt((position + 1.0) * DK)
    attended = (
        ((intra_sum + inter_sum) * scaling[:, None, None])
        .astype(jnp.bfloat16)
        .reshape(length, H * DV)
    )
    projected = jnp.dot(
        attended,
        lax.all_gather(out_weight, "seq", axis=1, tiled=True),
        preferred_element_type=jnp.float32,
    )
    hidden = (residual.astype(jnp.float32) + projected).astype(jnp.bfloat16)
    hidden_float = hidden.astype(jnp.float32)
    normed = (
        hidden_float
        * lax.rsqrt(jnp.mean(hidden_float * hidden_float, axis=-1, keepdims=True) + 1e-06)
    ).astype(jnp.bfloat16)
    experts = lax.axis_size("seq") * expert_in.shape[0]
    capacity = max(2, 2 * length * TOP // experts)
    flat_ids = expert_ids.reshape(-1)
    one_hot = (flat_ids[:, None] == jnp.arange(experts)[None, :]).astype(jnp.int32)
    earlier = jnp.cumsum(one_hot, axis=0) - one_hot
    slot_index = jnp.sum(earlier * one_hot, axis=-1)
    dest_row = flat_ids * capacity + slot_index
    buffer = (
        jnp.zeros((experts * capacity, D), jnp.bfloat16)
        .at[dest_row]
        .set(jnp.repeat(normed, TOP, axis=0))
    )
    buffer = buffer.reshape(experts, 1, capacity, D)
    act = jnp.einsum(
        "ensd,edf->ensf",
        lax.all_to_all(buffer, "seq", split_axis=0, concat_axis=1, tiled=True),
        expert_in,
        preferred_element_type=jnp.float32,
    )
    inner = (jax.nn.silu(act[..., :HE]) * act[..., HE:]).astype(jnp.bfloat16)
    produced_all = jnp.einsum(
        "ensf,efd->ensd", inner, expert_out, preferred_element_type=jnp.float32
    ).astype(jnp.bfloat16)
    returned_rows = lax.all_to_all(produced_all, "seq", split_axis=1, concat_axis=0, tiled=True)
    picked = returned_rows.reshape(experts * capacity, D)[dest_row]
    combined = jnp.sum(
        picked.astype(jnp.float32).reshape(length, TOP, D) * gate_values[:, :, None], axis=1
    )
    return (hidden_float + combined).astype(jnp.bfloat16)


def solution(mesh):
    in_specs = (
        P(("win", "seq"), None),
        P(("win", "seq"), None),
        P(("win", "seq"), None),
        P(("win", "seq"), None),
        P(None, "seq"),
        P("seq", None, None),
        P("seq", None, None),
        P(("win", "seq"), None),
        P(("win", "seq"), None),
    )
    out_specs = P(("win", "seq"), None)
    return jax.shard_map(
        per_device, mesh=mesh, in_specs=in_specs, out_specs=out_specs, check_vma=False
    )
```

profile of v0, /device:TPU:0, one launch (start us, length us, event | category | flops | bytes accessed | tf_op | source)
XLA Modules:
  0.0 217.3 jit_solution(10166700806976817475)
XLA Ops:
  6.5 1.2 copy.24
  7.8 2.0 convolution_convert_fusion.1
  9.9 0.7 all-gather.4.cloned.1.call-update
  10.6 0.1 copy.28
  10.7 0.1 eq.29
  10.9 0.1 eq.25
  11.0 0.2 copy.23
  11.2 0.6 reduce-window.6
  11.8 0.2 slice_reduce_fusion
  12.1 0.1 copy.27
  12.2 0.1 mul.73
  12.4 0.1 fusion.26
  12.5 1.7 convolution_bitcast_fusion.1
  14.2 47.6 %all-gather.6.cloned.1.call-done = bf16[128,64,128]{2,1,0:T(8,128)(2,1)} async-done(((bf16[16,64,128]{2,1,0:T(8,128)(2,1)}), bf16[128,64,128]{2,1,0:T(8,128)(2,1)}) %all-gather.6.cloned.1.call-update) | async-done | bytes 2097168 | tf_op jit(solution)/shard_map/all_gather | solution.py:16
  61.9 1.8 fusion.8
  63.7 73.4 %all-gather.4.cloned.1.call-done = bf16[2048,1024]{1,0:T(8,128)(2,1)} async-done(((bf16[2048,128]{1,0:T(8,128)(2,1)}), bf16[2048,1024]{1,0:T(8,128)(2,1)}) %all-gather.4.cloned.1.call-update) | async-done | bytes 4194320 | tf_op jit(solution)/shard_map/all_gather | solution.py:62
  137.1 3.2 %multiply_reduce_fusion.1 = (f32[128]{0:T(128)S(1)}, f32[128,1024]{1,0:T(8,128)S(1)}) fusion(bf16[128,2048]{0,1:T(8,128)(2,1)} %bitcast.78, bf16[2048,1024]{1,0:T(8,128)(2,1)} %all-gather.4.cloned.1.call-done, bf16[128,1024]{1,0:T(8,128)(2,1)} %param.14), kind=kOutput, calls=%fused_computation.28 | convolution fusion | flops 537657216 | bytes 5505536 | tf_op jit(solution)/shard_map/dot_general | solution.py:60
  140.3 0.1 multiply_convert_fusion
  140.4 0.3 broadcast_in_dim.34
  140.7 1.0 reshape.151
  141.7 2.4 %scatter_custom_fusion = bf16[512,1024]{1,0:T(8,128)(2,1)S(1)} fusion(s32[256]{0:T(256)S(1)} %bitcast.80, bf16[256,1024]{1,0:T(8,128)(2,1)} %reshape.151, bf16[]{:T(256)} %constant.38.clone.1), kind=kCustom, calls=%fused_computation.29 | custom fusion | bytes 1049088 | tf_op jit(solution)/shard_map/scatter | solution.py:81
  144.1 28.4 %all_to_all.8 = bf16[8,1,64,1024]{3,2,1,0:T(8,128)(2,1)S(1)} all-to-all(bf16[8,1,64,1024]{3,2,1,0:T(8,128)(2,1)S(1)} %bitcast.73), channel_id=1, replica_groups=mesh['seq'=8,'win'=4] {'seq'}, dimensions={0} | all-to-all | bytes 2097152 | tf_op jit(solution)/shard_map/all_to_all | solution.py:86
  172.5 1.0 fusion.2
  173.5 0.2 copy-done.4
  173.6 1.7 fusion.5
  175.4 3.7 %all-to-all-start.1 = ((bf16[1,8,64,1024]{3,2,0,1:T(8,128)(2,1)}), bf16[1,8,64,1024]{3,2,0,1:T(8,128)(2,1)S(1)}, u32[]{:S(2)}, u32[]{:S(2)}) async-start(bf16[1,8,64,1024]{3,2,0,1:T(8,128)(2,1)} %fusion.5), calls=%async_computation.1 | async-start | bytes 2097152 | tf_op jit(solution)/shard_map/all_to_all | solution.py:94
  179.1 0.1 copy.31
  179.2 25.4 %all-to-all-done.1 = bf16[1,8,64,1024]{3,2,0,1:T(8,128)(2,1)S(1)} async-done(((bf16[1,8,64,1024]{3,2,0,1:T(8,128)(2,1)}), bf16[1,8,64,1024]{3,2,0,1:T(8,128)(2,1)S(1)}, u32[]{:S(2)}, u32[]{:S(2)}) %all-to-all-start.1) | async-done | bytes 1048608 | tf_op jit(solution)/shard_map/all_to_all | solution.py:94
  204.7 2.0 gather_fusion
  206.6 1.7 reshape.138
  208.3 1.3 multiply_reduce_fusion
  209.7 0.8 add_convert_fusion
  (23 shorter events, 0.2 us)
Async XLA Ops:
  6.5 166.0 %copy-start = (bf16[1,1024,768]{2,1,0:T(8,128)(2,1)S(1)}, bf16[1,1024,768]{2,1,0:T(8,128)(2,1)}, u32[]{:S(2)}) copy-start(bf16[1,1024,768]{2,1,0:T(8,128)(2,1)} %param.16) | copy-start | bytes 4718596
  6.5 4.1 %copy-start.2 = (s32[128,2]{0,1:T(2,128)S(1)}, s32[128,2]{0,1:T(2,128)}, u32[]{:S(2)}) copy-start(s32[128,2]{0,1:T(2,128)} %param.18) | copy-start | bytes 3076
  6.5 4.5 %copy-start.1 = (bf16[128,1024]{1,0:T(8,128)(2,1)S(1)}, bf16[128,1024]{1,0:T(8,128)(2,1)}, u32[]{:S(2)}) copy-start(bf16[128,1024]{1,0:T(8,128)(2,1)} %param.11) | copy-start | bytes 786436
  6.5 55.3 %all-gather.6.cloned.1.call-start = ((), (), s32[]{:S(2)}) async-start(), calls=%async_computation.3 | async-start | bytes 2359296 | tf_op jit(solution)/shard_map/all_gather | solution.py:16
  9.8 127.2 %all-gather.4.cloned.1.call-start = ((), (), s32[]{:S(2)}) async-start(), calls=%async_computation.2 | async-start | bytes 4718592 | tf_op jit(solution)/shard_map/all_gather | solution.py:62
  172.5 1.1 copy-start.4
  175.4 3.7 %copy-start.3 = (f32[128,2]{0,1:T(2,128)S(1)}, f32[128,2]{0,1:T(2,128)}, u32[]{:S(2)}) copy-start(f32[128,2]{0,1:T(2,128)} %param.19) | copy-start | bytes 3076
  175.4 29.3 %all-to-all-start.1 = ((bf16[1,8,64,1024]{3,2,0,1:T(8,128)(2,1)}), bf16[1,8,64,1024]{3,2,0,1:T(8,128)(2,1)S(1)}, u32[]{:S(2)}, u32[]{:S(2)}) async-start(bf16[1,8,64,1024]{3,2,0,1:T(8,128)(2,1)} %fusion.5), calls=%async_computation.1 | async-start | bytes 2097152 | tf_op jit(solution)/shard_map/all_to_all | solution.py:94
Sparse Core Ops, SparseCore 0:
  10.0 51.8 all-gather.5
  63.9 73.1 all-gather.3
where the time goes:
time: 218 us; the launch traced here: 217 us
  waiting for transfers between devices  147 us (67%)
  blocking collectives  28.4 us (13%)
  between operations  13.6 us (6%)
  matrix products  11.5 us (5%)
  local copies, waits for them, and re-layouts  9.93 us (5%)
  starting transfers between devices  3.78 us (2%)
  other arithmetic  3 us (1%)
    all_gather x1, waiting for transfers between devices, per_device(): lax.all_gather(out_weight, 'seq', axis=1, tiled=True)  73.4 us
    all_gather x1, waiting for transfers between devices, carried_in(): gathered = lax.all_gather(x.astype(jnp.bfloat16), axis)  47.6 us
    all_to_all x1, blocking collectives, per_device(): lax.all_to_all(buffer, 'seq', split_axis=0, concat_axis=1, tiled=True)  28.4 us
    all_to_all x1, waiting for transfers between devices, per_device(): lax.all_to_all(produced_all, 'seq', split_axis=1, concat_axis=0, tiled=True)  25.4 us
  transfers between devices with their start and end apart: 3, of which 3 were waited for; matrix products, arithmetic and copies ran while one was open for 3% of the time, Pallas kernels for 0%

commit v1 on v0

v1 whole, which is shorter than its diff:
```python
import functools

import jax
import jax.numpy as jnp
from jax import lax
from jax.experimental import pallas as pl
from jax.experimental.pallas import tpu as pltpu
from jax.sharding import PartitionSpec as P

D = 1024
H = 16
DK = 64
DV = 128
HE = 384
TOP = 2
UNROLL_LIMIT = 16
BF = jnp.bfloat16
F32 = jnp.float32
VMEM = pl.BlockSpec(memory_space=pltpu.VMEM)


def call(body, outs, n_in, scratch=(), name=None):
    return pl.pallas_call(
        body,
        out_shape=outs,
        in_specs=[VMEM] * n_in,
        out_specs=jax.tree.map(lambda _: VMEM, outs),
        scratch_shapes=scratch,
        name=name,
    )


def sds(shape, dtype):
    return jax.ShapeDtypeStruct(shape, dtype)


def dot(a, b, dims=((1,), (0,))):
    return lax.dot_general(a, b, (dims, ((), ())), preferred_element_type=F32)


def states_body(k_ref, v_ref, mine_ref, send_ref, full):
    half = full.shape[0] // 2
    for p in range(H // 2):
        r = dot(k_ref[:, 2 * DK * p : 2 * DK * (p + 1)], v_ref[:, 2 * DV * p : 2 * DV * (p + 1)], ((0,), (0,)))
        full[2 * DK * p : 2 * DK * p + DK, :] = r[:DK, :DV]
        full[2 * DK * p + DK : 2 * DK * (p + 1), :] = r[DK:, DV:]
    y = lax.rem(lax.axis_index("seq"), 2)
    mine_ref[...] = full[pl.ds(pl.multiple_of(y * half, half), half), :]
    send_ref[...] = full[pl.ds(pl.multiple_of((1 - y) * half, half), half), :].astype(BF)


def intra_body(q_ref, k_ref, v_ref, out_ref):
    length = q_ref.shape[0]
    lane = lax.broadcasted_iota(jnp.int32, (length, 2 * DK), 1)
    row = lax.broadcasted_iota(jnp.int32, (length, length), 0)
    col = lax.broadcasted_iota(jnp.int32, (length, length), 1)
    causal = row >= col
    for p in range(H // 2):
        q = q_ref[:, 2 * DK * p : 2 * DK * (p + 1)]
        k = k_ref[:, 2 * DK * p : 2 * DK * (p + 1)]
        for i in range(2):
            mine = (lane < DK) if i == 0 else (lane >= DK)
            s = dot(jnp.where(mine, q, jnp.zeros_like(q)), k, ((1,), (1,)))
            s = jnp.where(causal, s, 0.0).astype(BF)
            c = (2 * p + i) * DV
            out_ref[:, c : c + DV] = dot(s, v_ref[:, c : c + DV])


def keys_of(meta, experts):
    length = meta.shape[1]
    e = lax.broadcasted_iota(jnp.int32, (experts, length), 0).astype(F32)
    first, second = meta[0:1, :] == e, meta[1:2, :] == e
    named = jnp.logical_or(first, second)
    a = lax.broadcasted_iota(jnp.int32, (length, length), 0)
    b = lax.broadcasted_iota(jnp.int32, (length, length), 1)
    before = jnp.where(a < b, 1.0, 0.0).astype(BF)
    count = dot(jnp.where(named, 1.0, 0.0).astype(BF), before)
    key = jnp.where(named, count, -1.0)
    gate = jnp.where(first, meta[2:3, :], jnp.where(second, meta[3:4, :], 0.0))
    return key, gate


def deal(key_ref, normed, outs, cap):
    s = lax.axis_index("seq")
    length = normed.shape[0]
    c = lax.broadcasted_iota(jnp.int32, (cap, length), 0).astype(F32)
    picks = [
        jnp.where(c == key_ref[pl.ds(jnp.bitwise_xor(s, k), 1), :], 1.0, 0.0).astype(BF)
        for k in range(len(outs))
    ]
    rows = dot(jnp.concatenate(picks, axis=0), normed).astype(BF)
    for k, out in enumerate(outs):
        out[...] = rows[k * cap : (k + 1) * cap, :]


def project_body(n, q_ref, intra_ref, pm_ref, po_ref, wown_ref, res_ref, meta_ref, *refs):
    fwd, bwd = n // 2, n // 2 - 1
    pieces, refs = refs[: 2 * (fwd + bwd)], refs[2 * (fwd + bwd) :]
    fm, refs_f = pieces[:fwd], pieces[fwd : 2 * fwd]
    bm, refs_b = pieces[2 * fwd : 2 * fwd + bwd], pieces[2 * fwd + bwd :]
    hidden_ref, normed_ref = refs[:2]
    outs = refs[2 : 2 + n // 2]
    prefix, att, hid, key_ref = refs[2 + n // 2 :]
    s = lax.axis_index("seq")
    c = lax.rem(lax.axis_index("win"), 2)
    y = lax.rem(s, 2)
    length = q_ref.shape[0]
    half = prefix.shape[0] // 2
    prefix[pl.ds(pl.multiple_of(y * half, half), half), :] = pm_ref[...]
    prefix[pl.ds(pl.multiple_of((1 - y) * half, half), half), :] = po_ref[...]
    place = (s * length + lax.broadcasted_iota(jnp.int32, (length, 1), 0)).astype(F32)
    scaling = lax.rsqrt((place + 1.0) * DK)
    zero = jnp.zeros((DK, DV), BF)
    for p in range(H // 2):
        top = jnp.concatenate([prefix[2 * DK * p : 2 * DK * p + DK, :], zero], axis=1)
        low = jnp.concatenate([zero, prefix[2 * DK * p + DK : 2 * DK * (p + 1), :]], axis=1)
        inter = dot(q_ref[:, 2 * DK * p : 2 * DK * (p + 1)], jnp.concatenate([top, low], axis=0))
        cols = slice(2 * DV * p, 2 * DV * (p + 1))
        att[:, cols] = ((intra_ref[:, cols] + inter) * scaling).astype(BF)
    rows = att.shape[1] // 2
    width = wown_ref.shape[1]
    att_m = att[:, pl.ds(pl.multiple_of(c * rows, rows), rows)]
    att_p = att[:, pl.ds(pl.multiple_of((1 - c) * rows, rows), rows)]
    pos = jnp.where(y == 0, s // 2, n - 1 - s // 2)

    def source(shift):
        at = lax.rem(pos + shift + n, n)
        return jnp.where(at < n // 2, 2 * at, 2 * (n - 1 - at) + 1)

    def put(shift, value):
        hid[:, pl.ds(pl.multiple_of(source(shift) * width, width), width)] = value

    put(0, dot(att[...], wown_ref[...]))
    for j in range(fwd):
        if j < bwd:
            m = jnp.concatenate([fm[j][...], bm[j][...]], axis=1)
            o = jnp.concatenate([refs_f[j][...], refs_b[j][...]], axis=1)
            both = dot(att_m, m) + dot(att_p, o)
            put(-(j + 1), both[:, :width])
            put(j + 1, both[:, width:])
        else:
            put(-(j + 1), dot(att_m, fm[j][...]) + dot(att_p, refs_f[j][...]))
    hidden = (res_ref[...].astype(F32) + hid[...]).astype(BF)
    hidden_ref[...] = hidden
    h = hidden.astype(F32)
    normed = (h * lax.rsqrt(jnp.mean(h * h, axis=-1, keepdims=True) + 1e-06)).astype(BF)
    normed_ref[...] = normed
    key_ref[...] = keys_of(meta_ref[...], n)[0]
    deal(key_ref, normed, outs, outs[0].shape[0])


def deal_body(n, normed_ref, meta_ref, *refs):
    outs, key_ref = refs[:-1], refs[-1]
    key_ref[...] = keys_of(meta_ref[...], n)[0]
    deal(key_ref, normed_ref[...], outs, outs[0].shape[0])


def expert_body(parts, win_ref, wout_ref, *refs):
    ins, outs = refs[:parts], refs[parts:]
    cap = ins[0].shape[0]
    x = jnp.concatenate([r[...] for r in ins], axis=0)
    act = dot(x, win_ref[0])
    gate = act[:, :HE]
    inner = (gate / (1.0 + jnp.exp(-gate)) * act[:, HE:]).astype(BF)
    rows = dot(inner, wout_ref[0]).astype(BF)
    for k in range(parts):
        outs[k][...] = rows[k * cap : (k + 1) * cap, :]


def gather_rows(n, meta, ins, key_ref, gate_ref):
    key, gate = keys_of(meta, n)
    key_ref[...] = key
    gate_ref[...] = gate
    s = lax.axis_index("seq")
    cap = ins[0].shape[0]
    length = meta.shape[1]
    c = lax.broadcasted_iota(jnp.int32, (cap, length), 0).astype(F32)
    high, low = [], []
    for k in range(len(ins)):
        e = pl.ds(jnp.bitwise_xor(s, k), 1)
        w = jnp.where(c == key_ref[e, :], gate_ref[e, :], 0.0)
        h = w.astype(BF)
        high.append(h)
        low.append((w - h.astype(F32)).astype(BF))
    rows = jnp.concatenate([r[...] for r in ins], axis=0)
    dims = ((0,), (0,))
    return dot(jnp.concatenate(high, axis=0), rows, dims) + dot(jnp.concatenate(low, axis=0), rows, dims)


def partial_body(n, meta_ref, *refs):
    ins, out_ref, key_ref, gate_ref = refs[:-3], refs[-3], refs[-2], refs[-1]
    out_ref[...] = gather_rows(n, meta_ref[...], ins, key_ref, gate_ref).astype(BF)


def final_body(n, meta_ref, hidden_ref, other_ref, *refs):
    ins, out_ref, key_ref, gate_ref = refs[:-3], refs[-3], refs[-2], refs[-1]
    total = gather_rows(n, meta_ref[...], ins, key_ref, gate_ref)
    total = total + other_ref[...].astype(F32) + hidden_ref[...].astype(F32)
    out_ref[...] = total.astype(BF)


def small_group(
    queries,
    key_rows,
    value_rows,
    residual,
    out_weight,
    expert_in,
    expert_out,
    expert_ids,
    gate_values,
):
    n = lax.axis_size("seq")
    length = queries.shape[0]
    s = lax.axis_index("seq")
    c = lax.rem(lax.axis_index("win"), 2)
    y = lax.rem(s, 2)
    near = n // 2
    cap = max(2, 2 * length * TOP // n)
    half = H * DK // 2
    order = [2 * i for i in range(n // 2)] + [2 * i + 1 for i in reversed(range(n // 2))]
    ahead = [(order[i], order[(i + 1) % n]) for i in range(n)]
    back = [(b, a) for a, b in ahead]

    def flip(x, k):
        return lax.ppermute(x, "seq", [(i, i ^ k) for i in range(n)])

    def swap_core(x):
        return lax.ppermute(x, "win", [(i, i ^ 1) for i in range(lax.axis_size("win"))])

    mine, sent = call(
        states_body,
        (sds((half, DV), F32), sds((half, DV), BF)),
        2,
        [pltpu.VMEM((2 * half, DV), F32)],
        name="states",
    )(key_rows, value_rows)
    got = flip(sent, 1).astype(F32)
    run = mine + got
    before = jnp.zeros_like(mine)
    step = 1
    while step < n // 2:
        hop = [(i, i + 2 * step) for i in range(n - 2 * step)]
        came = lax.ppermute(run.astype(BF), "seq", hop).astype(F32)
        before, run = before + came, run + came
        step *= 2
    prefix_mine = (before + jnp.where(y == 0, 0.0, got)).astype(BF)
    prefix_other = flip((before + jnp.where(y == 0, mine, 0.0)).astype(BF), 1)

    rows = H * DV // 2
    piece = lax.dynamic_slice_in_dim(out_weight, c * rows, rows, 0)
    fm, bm = [], []
    f = b = piece
    for j in range(near):
        f = lax.ppermute(f, "seq", ahead)
        fm.append(f)
        if j < near - 1:
            b = lax.ppermute(b, "seq", back)
            bm.append(b)
    fp = [swap_core(x) for x in fm]
    bp = [swap_core(x) for x in bm]

    meta = jnp.concatenate([expert_ids.astype(F32), gate_values], axis=1).T
    meta_far = flip(meta, near)

    intra = call(intra_body, sds((length, H * DV), F32), 3, name="intra")(queries, key_rows, value_rows)

    ins = [queries, intra, prefix_mine, prefix_other, out_weight, residual, meta, *fm, *fp, *bm, *bp]
    row_buf = sds((cap, D), BF)
    hidden, normed, *deal_own = call(
        functools.partial(project_body, n),
        (sds((length, D), BF), sds((length, D), BF), *[row_buf] * near),
        len(ins),
        [
            pltpu.VMEM((2 * half, DV), BF),
            pltpu.VMEM((length, H * DV), BF),
            pltpu.VMEM((length, D), F32),
            pltpu.VMEM((n, length), F32),
        ],
        name="project",
    )(*ins)
    normed_far = flip(normed, near)
    own_in = [deal_own[0]] + [flip(deal_own[k], k) for k in range(1, near)]
    deal_far = call(
        functools.partial(deal_body, n),
        tuple([row_buf] * near),
        2,
        [pltpu.VMEM((n, length), F32)],
        name="deal",
    )(normed_far, meta_far)
    far_in = [deal_far[0]] + [flip(deal_far[k], k) for k in range(1, near)]

    experts = call(
        functools.partial(expert_body, near), tuple([row_buf] * near), 2 + near, name="experts"
    )
    own_out = experts(expert_in, expert_out, *own_in)
    far_out = experts(expert_in, expert_out, *far_in)
    own_back = [own_out[0]] + [flip(own_out[k], k) for k in range(1, near)]
    far_back = [far_out[0]] + [flip(far_out[k], k) for k in range(1, near)]
    scratch = [pltpu.VMEM((n, length), F32), pltpu.VMEM((n, length), F32)]
    part_far = call(
        functools.partial(partial_body, n), sds((length, D), BF), 1 + near, scratch, name="partial"
    )(meta_far, *far_back)
    part_own = flip(part_far, near)
    return call(
        functools.partial(final_body, n), sds((length, D), BF), 3 + near, scratch, name="final"
    )(meta, hidden, part_own, *own_back)


def large_group(
    queries,
    key_rows,
    value_rows,
    residual,
    out_weight,
    expert_in,
    expert_out,
    expert_ids,
    gate_values,
):
    length = queries.shape[0]
    q_heads = queries.reshape(length, H, DK)
    k_heads = key_rows.reshape(length, H, DK)
    v_heads = value_rows.reshape(length, H, DV)
    local_state = jnp.einsum("thd,the->hde", k_heads, v_heads, preferred_element_type=F32)
    gathered = lax.all_gather(local_state.astype(BF), "seq")
    prefix = lax.fori_loop(
        0,
        lax.axis_index("seq"),
        lambda i, total: total + lax.dynamic_index_in_dim(gathered, i, 0, False).astype(F32),
        jnp.zeros_like(local_state),
    )
    causal = jnp.arange(length)[:, None] >= jnp.arange(length)[None, :]
    scores = jnp.einsum("thd,shd->hts", q_heads, k_heads, preferred_element_type=F32)
    scores = jnp.where(causal[None], scores, 0.0).astype(BF)
    intra_sum = jnp.einsum("hts,she->the", scores, v_heads, preferred_element_type=F32)
    inter_sum = jnp.einsum(
        "thd,hde->the", q_heads.astype(F32), prefix, precision=lax.Precision.HIGHEST
    )
    position = (lax.axis_index("seq") * length + jnp.arange(length)).astype(F32)
    scaling = lax.rsqrt((position + 1.0) * DK)
    attended = ((intra_sum + inter_sum) * scaling[:, None, None]).astype(BF).reshape(length, H * DV)
    projected = jnp.dot(
        attended,
        lax.all_gather(out_weight, "seq", axis=1, tiled=True),
        preferred_element_type=F32,
    )
    hidden = (residual.astype(F32) + projected).astype(BF)
    hidden_float = hidden.astype(F32)
    normed = (
        hidden_float
        * lax.rsqrt(jnp.mean(hidden_float * hidden_float, axis=-1, keepdims=True) + 1e-06)
    ).astype(BF)
    experts = lax.axis_size("seq") * expert_in.shape[0]
    capacity = max(2, 2 * length * TOP // experts)
    flat_ids = expert_ids.reshape(-1)
    one_hot = (flat_ids[:, None] == jnp.arange(experts)[None, :]).astype(jnp.int32)
    earlier = jnp.cumsum(one_hot, axis=0) - one_hot
    slot_index = jnp.sum(earlier * one_hot, axis=-1)
    dest_row = flat_ids * capacity + slot_index
    buffer = (
        jnp.zeros((experts * capacity, D), BF).at[dest_row].set(jnp.repeat(normed, TOP, axis=0))
    )
    buffer = buffer.reshape(experts, 1, capacity, D)
    act = jnp.einsum(
        "ensd,edf->ensf",
        lax.all_to_all(buffer, "seq", split_axis=0, concat_axis=1, tiled=True),
        expert_in,
        preferred_element_type=F32,
    )
    inner = (jax.nn.silu(act[..., :HE]) * act[..., HE:]).astype(BF)
    produced_all = jnp.einsum(
        "ensf,efd->ensd", inner, expert_out, preferred_element_type=F32
    ).astype(BF)
    returned_rows = lax.all_to_all(produced_all, "seq", split_axis=1, concat_axis=0, tiled=True)
    picked = returned_rows.reshape(experts * capacity, D)[dest_row]
    combined = jnp.sum(
        picked.astype(F32).reshape(length, TOP, D) * gate_values[:, :, None], axis=1
    )
    return (hidden_float + combined).astype(BF)


def solution(mesh):
    n = mesh.shape["seq"]
    even_win = mesh.shape["win"] % 2 == 0
    small = 4 <= n <= UNROLL_LIMIT and n & (n - 1) == 0 and even_win
    in_specs = (
        P(("win", "seq"), None),
        P(("win", "seq"), None),
        P(("win", "seq"), None),
        P(("win", "seq"), None),
        P(None, "seq"),
        P("seq", None, None),
        P("seq", None, None),
        P(("win", "seq"), None),
        P(("win", "seq"), None),
    )
    out_specs = P(("win", "seq"), None)
    return jax.shard_map(
        small_group if small else large_group,
        mesh=mesh,
        in_specs=in_specs,
        out_specs=out_specs,
        check_vma=False,
    )
```

time: 218 us -> 118 us (0.54)
  waiting for transfers between devices: 147 us -> 43.7 us
  starting transfers between devices: 3.78 us -> 36.8 us
  blocking collectives: 28.4 us -> 0 us
  Pallas kernels: 0 us -> 26.2 us
  between operations: 13.6 us -> 0.34 us
  matrix products: 11.5 us -> 0 us
  local copies, waits for them, and re-layouts: 9.93 us -> 5.82 us
    all_gather x2 -> x0, waiting for transfers between devices: 121 us -> none  [the longest x1 73.4 us: per_device(): lax.all_gather(out_weight, 'seq', axis=1, tiled=True)]
    ppermute x0 -> x33, waiting for transfers between devices: none -> 43.7 us  [the longest x17 39.2 us: flip(): return lax.ppermute(x, 'seq', [(i, i ^ k) for i in range(n)])]
    ppermute x0 -> x33, starting transfers between devices: none -> 36.8 us  [the longest x17 16.7 us: flip(): return lax.ppermute(x, 'seq', [(i, i ^ k) for i in range(n)])]
    all_to_all x1 -> x0, blocking collectives: 28.4 us -> none  [per_device(): lax.all_to_all(buffer, 'seq', split_axis=0, concat_axis=1, tiled=True)]
    pallas_call x0 -> x8, Pallas kernels: none -> 26.2 us  [the longest x1 4.93 us: small_group(): call(functools.partial(project_body, n), (sds((length, D), BF), sds((leng...]
    all_to_all x1 -> x0, waiting for transfers between devices: 25.4 us -> none  [per_device(): lax.all_to_all(produced_all, 'seq', split_axis=1, concat_axis=0, tiled=True)]
    dot_general x6 -> x0, matrix products: 11.5 us -> none  [the longest x1 3.18 us: per_device(): jnp.dot(attended, lax.all_gather(out_weight, 'seq', axis=1, tiled=True),...]
    all_to_all x1 -> x0, starting transfers between devices: 3.73 us -> none  [per_device(): lax.all_to_all(produced_all, 'seq', split_axis=1, concat_axis=0, tiled=True)]
  transfers between devices with their start and end apart: 3 -> 33, of which waited for: 3 -> 14; matrix products, arithmetic and copies ran while one was open for 3% -> 4% of each run, Pallas kernels for 0% -> 11%
where the time goes in v1:
time: 118 us; the launch traced here: 117 us
  waiting for transfers between devices  43.7 us (37%)
  starting transfers between devices  36.8 us (31%)
  Pallas kernels  26.2 us (22%)
  local copies, waits for them, and re-layouts  5.82 us (5%)
  other arithmetic  4.27 us (4%)
    ppermute x17, waiting for transfers between devices, flip(): return lax.ppermute(x, 'seq', [(i, i ^ k) for i in range(n)])  39.2 us
    ppermute x17, starting transfers between devices, flip(): return lax.ppermute(x, 'seq', [(i, i ^ k) for i in range(n)])  16.7 us
    ppermute x2, starting transfers between devices, small_group(): came = lax.ppermute(run.astype(BF), 'seq', hop).astype(F32)  7.04 us
    ppermute x4, starting transfers between devices, small_group(): f = lax.ppermute(f, 'seq', ahead)  6.54 us
    pallas_call x1, Pallas kernels, small_group(): call(functools.partial(project_body, n), (sds((length, D), BF), sds((leng...  4.93 us
    ppermute x3, starting transfers between devices, small_group(): b = lax.ppermute(b, 'seq', back)  4.87 us
    unnamed x68, local copies, waits for them, and re-layouts  4.85 us
    pallas_call x1, Pallas kernels, small_group(): call(intra_body, sds((length, H * DV), F32), 3, name='intra')  4.79 us
  transfers between devices with their start and end apart: 33, of which 14 were waited for; matrix products, arithmetic and copies ran while one was open for 4% of the time, Pallas kernels for 11%

profile of v1, /device:TPU:0, one launch (start us, length us, event | category | flops | bytes accessed | tf_op | source)
XLA Modules:
  0.0 117.2 jit_solution(837442891755684309)
XLA Ops:
  1.0 3.1 %collective-permute-start.4 = (bf16[1024,128]{1,0:T(8,128)(2,1)S(1)}, bf16[1024,128]{1,0:T(8,128)(2,1)S(1)}, u32[]{:S(2)}, u32[]{:S(2)}) collective-permute-start(bf16[1024,128]{1,0:T(8,128)(2,1)S(1)} %constant_dynamic-slice_fusion), channel_id=1, source_target_pairs={{0,8},{8,16},{16,24},{24,28},{28,20},{20,12},{12,4},{4,0},{1,9},{9... | collective-permute-start | bytes 786440 | tf_op jit(solution)/shard_map/ppermute | solution.py:255
  4.1 2.3 %states.1 = (f32[512,128]{1,0:T(8,128)}, bf16[512,128]{1,0:T(8,128)(2,1)}) custom-call(bf16[128,1024]{1,0:T(8,128)(2,1)} %k_ref.3, bf16[128,2048]{1,0:T(8,128)(2,1)} %v_ref.3), custom_call_target="tpu_custom_call" | custom-call | tf_op jit(solution)/shard_map/states/pallas_call | solution.py:231
  6.4 2.0 %collective-permute-start.12 = (bf16[1024,128]{1,0:T(8,128)(2,1)S(1)}, bf16[1024,128]{1,0:T(8,128)(2,1)S(1)}, u32[]{:S(2)}, u32[]{:S(2)}) collective-permute-start(bf16[1024,128]{1,0:T(8,128)(2,1)S(1)} %constant_dynamic-slice_fusion), channel_id=1, source_target_pairs={{8,0},{16,8},{24,16},{28,24},{20,28},{12,20},{4,12},{0,4},{9,1},{1... | collective-permute-start | bytes 786440 | tf_op jit(solution)/shard_map/ppermute | solution.py:258
  8.4 2.8 %collective-permute-done.4.refs_0_ = bf16[1024,128]{1,0:T(8,128)(2,1)S(1)} collective-permute-done((bf16[1024,128]{1,0:T(8,128)(2,1)S(1)}, bf16[1024,128]{1,0:T(8,128)(2,1)S(1)}, u32[]{:S(2)}, u32[]{:S(2)}) %collective-permute-start.4) | collective-permute-done | bytes 262176 | tf_op jit(solution)/shard_map/ppermute | solution.py:255
  12.1 1.9 %collective-permute-done = bf16[512,128]{1,0:T(8,128)(2,1)S(1)} collective-permute-done((bf16[512,128]{1,0:T(8,128)(2,1)}, bf16[512,128]{1,0:T(8,128)(2,1)S(1)}, u32[]{:S(2)}, u32[]{:S(2)}) %collective-permute-start) | collective-permute-done | bytes 131104 | tf_op jit(solution)/shard_map/ppermute | solution.py:226
  15.0 1.6 %collective-permute-start.1 = (bf16[512,128]{1,0:T(8,128)(2,1)S(1)}, bf16[512,128]{1,0:T(8,128)(2,1)S(1)}, u32[]{:S(2)}, u32[]{:S(2)}) collective-permute-start(bf16[512,128]{1,0:T(8,128)(2,1)S(1)} %fusion.3), channel_id=1, source_target_pairs={{0,8},{4,12},{8,16},{12,20},{16,24},{20,28},{1,9},{5,13},{9,17},{1... | collective-permute-start | bytes 393224 | tf_op jit(solution)/shard_map/ppermute | solution.py:244
  17.4 1.3 %collective-permute-done.5.refs_1_ = bf16[1024,128]{1,0:T(8,128)(2,1)S(1)} collective-permute-done((bf16[1024,128]{1,0:T(8,128)(2,1)S(1)}, bf16[1024,128]{1,0:T(8,128)(2,1)S(1)}, u32[]{:S(2)}, u32[]{:S(2)}) %collective-permute-start.5) | collective-permute-done | bytes 262176 | tf_op jit(solution)/shard_map/ppermute | solution.py:255
  18.8 2.0 %collective-permute-start.6 = (bf16[1024,128]{1,0:T(8,128)(2,1)S(1)}, bf16[1024,128]{1,0:T(8,128)(2,1)S(1)}, u32[]{:S(2)}, u32[]{:S(2)}) collective-permute-start(bf16[1024,128]{1,0:T(8,128)(2,1)S(1)} %collective-permute-done.5.refs_1_), channel_id=1, source_target_pairs={{0,8},{8,16},{16,24},{24,28},{28,20},{20,12},{12,4},{4,0},{1,9},{9... | collective-permute-start | bytes 786440 | tf_op jit(solution)/shard_map/ppermute | solution.py:255
  22.1 5.4 %collective-permute-start.2 = (bf16[512,128]{1,0:T(8,128)(2,1)S(1)}, bf16[512,128]{1,0:T(8,128)(2,1)S(1)}, u32[]{:S(2)}, u32[]{:S(2)}) collective-permute-start(bf16[512,128]{1,0:T(8,128)(2,1)S(1)} %fusion.2), channel_id=1, source_target_pairs={{0,16},{4,20},{8,24},{12,28},{1,17},{5,21},{9,25},{13,29},{2,18},{... | collective-permute-start | bytes 393224 | tf_op jit(solution)/shard_map/ppermute | solution.py:244
  28.1 2.0 %collective-permute-start.14 = (bf16[1024,128]{1,0:T(8,128)(2,1)S(1)}, bf16[1024,128]{1,0:T(8,128)(2,1)S(1)}, u32[]{:S(2)}, u32[]{:S(2)}) collective-permute-start(bf16[1024,128]{1,0:T(8,128)(2,1)S(1)} %collective-permute-done.13.refs_9_), channel_id=1, source_target_pairs={{8,0},{16,8},{24,16},{28,24},{20,28},{12,20},{4,12},{0,4},{9,1},{1... | collective-permute-start | bytes 786440 | tf_op jit(solution)/shard_map/ppermute | solution.py:258
  30.7 1.7 %add_convert_fusion = (bf16[512,128]{1,0:T(8,128)(2,1)S(1)}, bf16[512,128]{1,0:T(8,128)(2,1)}) fusion(f32[512,128]{1,0:T(8,128)} %get-tuple-element.25, bf16[512,128]{1,0:T(8,128)(2,1)S(1)} %collective-permute-done.2, bf16[512,128]{1,0:T(8,128)(2,1)S(1)} %collective-permute-done.1, pred[]{:T(512)S(6)} %eq.4, bf16[512,128]{1,0:T(8,128)(2,1)S(1)} %collective-permute-done), kind=kLoop, calls=%fused_computation.7 | loop fusion | flops 655360 | bytes 917505 | tf_op jit(solution)/shard_map/convert_element_type | solution.py:248
  34.0 7.8 %collective-permute-done.3.po_ref = bf16[512,128]{1,0:T(8,128)(2,1)S(1)} collective-permute-done((bf16[512,128]{1,0:T(8,128)(2,1)S(1)}, bf16[512,128]{1,0:T(8,128)(2,1)S(1)}, u32[]{:S(2)}, u32[]{:S(2)}) %collective-permute-start.3) | collective-permute-done | bytes 131104 | tf_op jit(solution)/shard_map/ppermute | solution.py:226
  42.3 4.8 %intra.1.intra_ref = f32[128,2048]{1,0:T(8,128)} custom-call(bf16[128,1024]{1,0:T(8,128)(2,1)} %q_ref.3, bf16[128,1024]{1,0:T(8,128)(2,1)} %k_ref.3, bf16[128,2048]{1,0:T(8,128)(2,1)} %v_ref.3), custom_call_target="tpu_custom_call" | custom-call | tf_op jit(solution)/shard_map/intra/pallas_call | solution.py:266
  48.7 4.9 %project.1 = (bf16[128,1024]{1,0:T(8,128)(2,1)}, bf16[128,1024]{1,0:T(8,128)(2,1)}, bf16[64,1024]{1,0:T(8,128)(2,1)}, bf16[64,1024]{1,0:T(8,128)(2,1)}, bf16[64,...) custom-call(bf16[128,1024]{1,0:T(8,128)(2,1)} %q_ref.3, f32[128,2048]{1,0:T(8,128)} %intra.1.intra_ref, ...), custom_call_target="tpu_custom_call" | custom-call | tf_op jit(solution)/shard_map/project/pallas_call | solution.py:270
  53.7 2.9 %collective-permute-start.18 = (f32[4,128]{1,0:T(4,128)S(1)}, f32[4,128]{1,0:T(4,128)S(1)}, u32[]{:S(2)}, u32[]{:S(2)}) collective-permute-start(f32[4,128]{1,0:T(4,128)S(1)} %copy-done.27), channel_id=1, source_target_pairs={{0,16},{4,20},{8,24},{12,28},{16,0},{20,4},{24,8},{28,12},{1,17},{... | collective-permute-start | bytes 6152 | tf_op jit(solution)/shard_map/ppermute | solution.py:226
  56.6 11.0 %collective-permute-done.18.meta_ref = f32[4,128]{1,0:T(4,128)S(1)} collective-permute-done((f32[4,128]{1,0:T(4,128)S(1)}, f32[4,128]{1,0:T(4,128)S(1)}, u32[]{:S(2)}, u32[]{:S(2)}) %collective-permute-start.18) | collective-permute-done | bytes 2080 | tf_op jit(solution)/shard_map/ppermute | solution.py:226
  68.9 2.1 %deal.1 = (bf16[64,1024]{1,0:T(8,128)(2,1)}, bf16[64,1024]{1,0:T(8,128)(2,1)}, bf16[64,1024]{1,0:T(8,128)(2,1)}, bf16[64,1024]{1,0:T(8,128)(2,1)}) custom-call(bf16[128,1024]{1,0:T(8,128)(2,1)} %copy-done.13, f32[4,128]{1,0:T(4,128)} %copy-done.28), custom_call_target="tpu_custom_call" | custom-call | tf_op jit(solution)/shard_map/deal/pallas_call | solution.py:284
  72.1 2.4 %collective-permute-start.22 = (bf16[64,1024]{1,0:T(8,128)(2,1)}, bf16[64,1024]{1,0:T(8,128)(2,1)S(1)}, u32[]{:S(2)}, u32[]{:S(2)}) collective-permute-start(bf16[64,1024]{1,0:T(8,128)(2,1)} %get-tuple-element.32), channel_id=1, source_target_pairs={{0,12},{4,8},{8,4},{12,0},{16,28},{20,24},{24,20},{28,16},{1,13},{... | collective-permute-start | bytes 393224 | tf_op jit(solution)/shard_map/ppermute | solution.py:226
  74.5 2.2 %collective-permute-done.20.refs_1_ = bf16[64,1024]{1,0:T(8,128)(2,1)S(1)} collective-permute-done((bf16[64,1024]{1,0:T(8,128)(2,1)}, bf16[64,1024]{1,0:T(8,128)(2,1)S(1)}, u32[]{:S(2)}, u32[]{:S(2)}) %collective-permute-start.20) | collective-permute-done | bytes 131104 | tf_op jit(solution)/shard_map/ppermute | solution.py:226
  76.7 1.7 %collective-permute-done.21.refs_2_ = bf16[64,1024]{1,0:T(8,128)(2,1)S(1)} collective-permute-done((bf16[64,1024]{1,0:T(8,128)(2,1)}, bf16[64,1024]{1,0:T(8,128)(2,1)S(1)}, u32[]{:S(2)}, u32[]{:S(2)}) %collective-permute-start.21) | collective-permute-done | bytes 131104 | tf_op jit(solution)/shard_map/ppermute | solution.py:226
  78.4 2.3 %collective-permute-done.22.refs_3_ = bf16[64,1024]{1,0:T(8,128)(2,1)S(1)} collective-permute-done((bf16[64,1024]{1,0:T(8,128)(2,1)}, bf16[64,1024]{1,0:T(8,128)(2,1)S(1)}, u32[]{:S(2)}, u32[]{:S(2)}) %collective-permute-start.22) | collective-permute-done | bytes 131104 | tf_op jit(solution)/shard_map/ppermute | solution.py:226
  81.3 3.7 %experts.2 = (bf16[64,1024]{1,0:T(8,128)(2,1)}, bf16[64,1024]{1,0:T(8,128)(2,1)}, bf16[64,1024]{1,0:T(8,128)(2,1)}, bf16[64,1024]{1,0:T(8,128)(2,1)}) custom-call(bf16[1,1024,768]{2,1,0:T(8,128)(2,1)} %win_ref.3, bf16[1,384,1024]{2,1,0:T(8,128)(2,1)} %wout_ref.3, bf16[64,1024]{1,0:T(8,128)(2,1)} %get-tuple-element.29.refs_0_, bf16[64,1024]{1,0:T(8,128)(2,1)} %copy-done.20, ...), custom_call_target="tpu_custom_call" | custom-call | tf_op jit(solution)/shard_map/experts/pallas_call | solution.py:297
  85.9 2.6 %collective-permute-start.25 = (bf16[64,1024]{1,0:T(8,128)(2,1)}, bf16[64,1024]{1,0:T(8,128)(2,1)S(1)}, u32[]{:S(2)}, u32[]{:S(2)}) collective-permute-start(bf16[64,1024]{1,0:T(8,128)(2,1)} %get-tuple-element.36), channel_id=1, source_target_pairs={{0,12},{4,8},{8,4},{12,0},{16,28},{20,24},{24,20},{28,16},{1,13},{... | collective-permute-start | bytes 393224 | tf_op jit(solution)/shard_map/ppermute | solution.py:226
  89.4 3.2 %collective-permute-done.23.refs_1_ = bf16[64,1024]{1,0:T(8,128)(2,1)S(1)} collective-permute-done((bf16[64,1024]{1,0:T(8,128)(2,1)}, bf16[64,1024]{1,0:T(8,128)(2,1)S(1)}, u32[]{:S(2)}, u32[]{:S(2)}) %collective-permute-start.23) | collective-permute-done | bytes 131104 | tf_op jit(solution)/shard_map/ppermute | solution.py:226
  92.7 3.3 %collective-permute-done.25.refs_3_ = bf16[64,1024]{1,0:T(8,128)(2,1)S(1)} collective-permute-done((bf16[64,1024]{1,0:T(8,128)(2,1)}, bf16[64,1024]{1,0:T(8,128)(2,1)S(1)}, u32[]{:S(2)}, u32[]{:S(2)}) %collective-permute-start.25) | collective-permute-done | bytes 131104 | tf_op jit(solution)/shard_map/ppermute | solution.py:226
  96.6 2.3 %partial.1 = bf16[128,1024]{1,0:T(8,128)(2,1)} custom-call(f32[4,128]{1,0:T(4,128)} %copy-done.28, bf16[64,1024]{1,0:T(8,128)(2,1)} %get-tuple-element.33.refs_0_, bf16[64,1024]{1,0:T(8,128)(2,1)} %copy-done.24, bf16[64,1024]{1,0:T(8,128)(2,1)} %copy-done.25, bf16[64,1024]{1,0:T(8,128)(2,1)} %copy-done.26), custom_call_target="tpu_custom_call" | custom-call | tf_op jit(solution)/shard_map/partial/pallas_call | solution.py:301
  98.9 1.3 %collective-permute-start.26 = (bf16[128,1024]{1,0:T(8,128)(2,1)}, bf16[128,1024]{1,0:T(8,128)(2,1)S(1)}, u32[]{:S(2)}, u32[]{:S(2)}) collective-permute-start(bf16[128,1024]{1,0:T(8,128)(2,1)} %partial.1), channel_id=1, source_target_pairs={{0,16},{4,20},{8,24},{12,28},{16,0},{20,4},{24,8},{28,12},{1,17},{... | collective-permute-start | bytes 786440 | tf_op jit(solution)/shard_map/ppermute | solution.py:226
  102.0 3.7 %experts.3 = (bf16[64,1024]{1,0:T(8,128)(2,1)}, bf16[64,1024]{1,0:T(8,128)(2,1)}, bf16[64,1024]{1,0:T(8,128)(2,1)}, bf16[64,1024]{1,0:T(8,128)(2,1)}) custom-call(bf16[1,1024,768]{2,1,0:T(8,128)(2,1)} %win_ref.3, bf16[1,384,1024]{2,1,0:T(8,128)(2,1)} %wout_ref.3, bf16[64,1024]{1,0:T(8,128)(2,1)} %get-tuple-element.37.refs_0_, bf16[64,1024]{1,0:T(8,128)(2,1)} %copy-done.15, ...), custom_call_target="tpu_custom_call" | custom-call | tf_op jit(solution)/shard_map/experts/pallas_call | solution.py:296
  106.7 2.4 %collective-permute-start.32 = (bf16[64,1024]{1,0:T(8,128)(2,1)}, bf16[64,1024]{1,0:T(8,128)(2,1)S(1)}, u32[]{:S(2)}, u32[]{:S(2)}) collective-permute-start(bf16[64,1024]{1,0:T(8,128)(2,1)} %get-tuple-element.44), channel_id=1, source_target_pairs={{0,12},{4,8},{8,4},{12,0},{16,28},{20,24},{24,20},{28,16},{1,13},{... | collective-permute-start | bytes 393224 | tf_op jit(solution)/shard_map/ppermute | solution.py:226
  109.2 3.1 %collective-permute-done.30.refs_1_ = bf16[64,1024]{1,0:T(8,128)(2,1)S(1)} collective-permute-done((bf16[64,1024]{1,0:T(8,128)(2,1)}, bf16[64,1024]{1,0:T(8,128)(2,1)S(1)}, u32[]{:S(2)}, u32[]{:S(2)}) %collective-permute-start.30) | collective-permute-done | bytes 131104 | tf_op jit(solution)/shard_map/ppermute | solution.py:226
  112.3 1.7 %collective-permute-done.32.refs_3_ = bf16[64,1024]{1,0:T(8,128)(2,1)S(1)} collective-permute-done((bf16[64,1024]{1,0:T(8,128)(2,1)}, bf16[64,1024]{1,0:T(8,128)(2,1)S(1)}, u32[]{:S(2)}, u32[]{:S(2)}) %collective-permute-start.32) | collective-permute-done | bytes 131104 | tf_op jit(solution)/shard_map/ppermute | solution.py:226
  114.8 2.4 %final.1 = bf16[128,1024]{1,0:T(8,128)(2,1)} custom-call(f32[4,128]{1,0:T(4,128)} %maximum_bitcast_fusion.meta_ref, bf16[128,1024]{1,0:T(8,128)(2,1)} %get-tuple-element.27.hidden_ref, bf16[128,1024]{1,0:T(8,128)(2,1)} %copy-done.12, bf16[64,1024]{1,0:T(8,128)(2,1)} %get-tuple-element.41.refs_0_, bf16[64,1024]{1,0:T(8,128)(2,1)} %copy-done.18, ...), custom_call_target="tpu_custom_call" | custom-call | tf_op jit(solution)/shard_map/final/pallas_call | solution.py:305
  (116 shorter events, 18.8 us)
Async XLA Ops:
  1.0 10.2 %collective-permute-start.4 = (bf16[1024,128]{1,0:T(8,128)(2,1)S(1)}, bf16[1024,128]{1,0:T(8,128)(2,1)S(1)}, u32[]{:S(2)}, u32[]{:S(2)}) collective-permute-start(bf16[1024,128]{1,0:T(8,128)(2,1)S(1)} %constant_dynamic-slice_fusion), channel_id=1, source_target_pairs={{0,8},{8,16},{16,24},{24,28},{28,20},{20,12},{12,4},{4,0},{1,9},{9... | collective-permute-start | bytes 786440 | tf_op jit(solution)/shard_map/ppermute | solution.py:255
  6.4 7.6 %collective-permute-start = (bf16[512,128]{1,0:T(8,128)(2,1)}, bf16[512,128]{1,0:T(8,128)(2,1)S(1)}, u32[]{:S(2)}, u32[]{:S(2)}) collective-permute-start(bf16[512,128]{1,0:T(8,128)(2,1)} %get-tuple-element.26), channel_id=1, source_target_pairs={{0,4},{4,0},{8,12},{12,8},{16,20},{20,16},{24,28},{28,24},{1,5},{5... | collective-permute-start | bytes 393224 | tf_op jit(solution)/shard_map/ppermute | solution.py:226
  6.4 10.3 %collective-permute-start.12 = (bf16[1024,128]{1,0:T(8,128)(2,1)S(1)}, bf16[1024,128]{1,0:T(8,128)(2,1)S(1)}, u32[]{:S(2)}, u32[]{:S(2)}) collective-permute-start(bf16[1024,128]{1,0:T(8,128)(2,1)S(1)} %constant_dynamic-slice_fusion), channel_id=1, source_target_pairs={{8,0},{16,8},{24,16},{28,24},{20,28},{12,20},{4,12},{0,4},{9,1},{1... | collective-permute-start | bytes 786440 | tf_op jit(solution)/shard_map/ppermute | solution.py:258
  11.2 7.6 %collective-permute-start.5 = (bf16[1024,128]{1,0:T(8,128)(2,1)S(1)}, bf16[1024,128]{1,0:T(8,128)(2,1)S(1)}, u32[]{:S(2)}, u32[]{:S(2)}) collective-permute-start(bf16[1024,128]{1,0:T(8,128)(2,1)S(1)} %collective-permute-done.4.refs_0_), channel_id=1, source_target_pairs={{0,8},{8,16},{16,24},{24,28},{28,20},{20,12},{12,4},{4,0},{1,9},{9... | collective-permute-start | bytes 786440 | tf_op jit(solution)/shard_map/ppermute | solution.py:255
  15.0 6.1 %collective-permute-start.1 = (bf16[512,128]{1,0:T(8,128)(2,1)S(1)}, bf16[512,128]{1,0:T(8,128)(2,1)S(1)}, u32[]{:S(2)}, u32[]{:S(2)}) collective-permute-start(bf16[512,128]{1,0:T(8,128)(2,1)S(1)} %fusion.3), channel_id=1, source_target_pairs={{0,8},{4,12},{8,16},{12,20},{16,24},{20,28},{1,9},{5,13},{9,17},{1... | collective-permute-start | bytes 393224 | tf_op jit(solution)/shard_map/ppermute | solution.py:244
  16.6 11.5 %collective-permute-start.13 = (bf16[1024,128]{1,0:T(8,128)(2,1)S(1)}, bf16[1024,128]{1,0:T(8,128)(2,1)S(1)}, u32[]{:S(2)}, u32[]{:S(2)}) collective-permute-start(bf16[1024,128]{1,0:T(8,128)(2,1)S(1)} %collective-permute-done.12.refs_8_), channel_id=1, source_target_pairs={{8,0},{16,8},{24,16},{28,24},{20,28},{12,20},{4,12},{0,4},{9,1},{1... | collective-permute-start | bytes 786440 | tf_op jit(solution)/shard_map/ppermute | solution.py:258
  18.8 11.4 %collective-permute-start.6 = (bf16[1024,128]{1,0:T(8,128)(2,1)S(1)}, bf16[1024,128]{1,0:T(8,128)(2,1)S(1)}, u32[]{:S(2)}, u32[]{:S(2)}) collective-permute-start(bf16[1024,128]{1,0:T(8,128)(2,1)S(1)} %collective-permute-done.5.refs_1_), channel_id=1, source_target_pairs={{0,8},{8,16},{16,24},{24,28},{28,20},{20,12},{12,4},{4,0},{1,9},{9... | collective-permute-start | bytes 786440 | tf_op jit(solution)/shard_map/ppermute | solution.py:255
  22.1 8.5 %collective-permute-start.2 = (bf16[512,128]{1,0:T(8,128)(2,1)S(1)}, bf16[512,128]{1,0:T(8,128)(2,1)S(1)}, u32[]{:S(2)}, u32[]{:S(2)}) collective-permute-start(bf16[512,128]{1,0:T(8,128)(2,1)S(1)} %fusion.2), channel_id=1, source_target_pairs={{0,16},{4,20},{8,24},{12,28},{1,17},{5,21},{9,25},{13,29},{2,18},{... | collective-permute-start | bytes 393224 | tf_op jit(solution)/shard_map/ppermute | solution.py:244
  27.5 5.9 %collective-permute-start.15 = (bf16[1024,128]{1,0:T(8,128)(2,1)S(1)}, bf16[1024,128]{1,0:T(8,128)(2,1)S(1)}, u32[]{:S(2)}, u32[]{:S(2)}) collective-permute-start(bf16[1024,128]{1,0:T(8,128)(2,1)S(1)} %collective-permute-done.12.refs_8_), channel_id=1, source_target_pairs={{0,1},{1,0},{2,3},{3,2},{4,5},{5,4},{6,7},{7,6},{8,9},{9,8},{10,11... | collective-permute-start | bytes 786440 | tf_op jit(solution)/shard_map/ppermute | solution.py:229
  27.6 5.8 %collective-permute-start.8 = (bf16[1024,128]{1,0:T(8,128)(2,1)S(1)}, bf16[1024,128]{1,0:T(8,128)(2,1)S(1)}, u32[]{:S(2)}, u32[]{:S(2)}) collective-permute-start(bf16[1024,128]{1,0:T(8,128)(2,1)S(1)} %collective-permute-done.4.refs_0_), channel_id=1, source_target_pairs={{0,1},{1,0},{2,3},{3,2},{4,5},{5,4},{6,7},{7,6},{8,9},{9,8},{10,11... | collective-permute-start | bytes 786440 | tf_op jit(solution)/shard_map/ppermute | solution.py:229
  28.1 13.6 %collective-permute-start.14 = (bf16[1024,128]{1,0:T(8,128)(2,1)S(1)}, bf16[1024,128]{1,0:T(8,128)(2,1)S(1)}, u32[]{:S(2)}, u32[]{:S(2)}) collective-permute-start(bf16[1024,128]{1,0:T(8,128)(2,1)S(1)} %collective-permute-done.13.refs_9_), channel_id=1, source_target_pairs={{8,0},{16,8},{24,16},{28,24},{20,28},{12,20},{4,12},{0,4},{9,1},{1... | collective-permute-start | bytes 786440 | tf_op jit(solution)/shard_map/ppermute | solution.py:258
  30.2 12.1 %collective-permute-start.7 = (bf16[1024,128]{1,0:T(8,128)(2,1)S(1)}, bf16[1024,128]{1,0:T(8,128)(2,1)S(1)}, u32[]{:S(2)}, u32[]{:S(2)}) collective-permute-start(bf16[1024,128]{1,0:T(8,128)(2,1)S(1)} %collective-permute-done.6.refs_2_), channel_id=1, source_target_pairs={{0,8},{8,16},{16,24},{24,28},{28,20},{20,12},{12,4},{4,0},{1,9},{9... | collective-permute-start | bytes 786440 | tf_op jit(solution)/shard_map/ppermute | solution.py:255
  32.4 9.4 %collective-permute-start.3 = (bf16[512,128]{1,0:T(8,128)(2,1)S(1)}, bf16[512,128]{1,0:T(8,128)(2,1)S(1)}, u32[]{:S(2)}, u32[]{:S(2)}) collective-permute-start(bf16[512,128]{1,0:T(8,128)(2,1)S(1)} %get-tuple-element.45), channel_id=1, source_target_pairs={{0,4},{4,0},{8,12},{12,8},{16,20},{20,16},{24,28},{28,24},{1,5},{5... | collective-permute-start | bytes 393224 | tf_op jit(solution)/shard_map/ppermute | solution.py:226
  33.4 14.3 %collective-permute-start.16 = (bf16[1024,128]{1,0:T(8,128)(2,1)S(1)}, bf16[1024,128]{1,0:T(8,128)(2,1)S(1)}, u32[]{:S(2)}, u32[]{:S(2)}) collective-permute-start(bf16[1024,128]{1,0:T(8,128)(2,1)S(1)} %collective-permute-done.13.refs_9_), channel_id=1, source_target_pairs={{0,1},{1,0},{2,3},{3,2},{4,5},{5,4},{6,7},{7,6},{8,9},{9,8},{10,11... | collective-permute-start | bytes 786440 | tf_op jit(solution)/shard_map/ppermute | solution.py:229
  33.5 14.3 %collective-permute-start.9 = (bf16[1024,128]{1,0:T(8,128)(2,1)S(1)}, bf16[1024,128]{1,0:T(8,128)(2,1)S(1)}, u32[]{:S(2)}, u32[]{:S(2)}) collective-permute-start(bf16[1024,128]{1,0:T(8,128)(2,1)S(1)} %collective-permute-done.5.refs_1_), channel_id=1, source_target_pairs={{0,1},{1,0},{2,3},{3,2},{4,5},{5,4},{6,7},{7,6},{8,9},{9,8},{10,11... | collective-permute-start | bytes 786440 | tf_op jit(solution)/shard_map/ppermute | solution.py:229
  41.7 6.0 %collective-permute-start.10 = (bf16[1024,128]{1,0:T(8,128)(2,1)S(1)}, bf16[1024,128]{1,0:T(8,128)(2,1)S(1)}, u32[]{:S(2)}, u32[]{:S(2)}) collective-permute-start(bf16[1024,128]{1,0:T(8,128)(2,1)S(1)} %collective-permute-done.6.refs_2_), channel_id=1, source_target_pairs={{0,1},{1,0},{2,3},{3,2},{4,5},{5,4},{6,7},{7,6},{8,9},{9,8},{10,11... | collective-permute-start | bytes 786440 | tf_op jit(solution)/shard_map/ppermute | solution.py:229
  41.7 6.1 %collective-permute-start.17 = (bf16[1024,128]{1,0:T(8,128)(2,1)S(1)}, bf16[1024,128]{1,0:T(8,128)(2,1)}, u32[]{:S(2)}, u32[]{:S(2)}) collective-permute-start(bf16[1024,128]{1,0:T(8,128)(2,1)S(1)} %collective-permute-done.14.refs_10_), channel_id=1, source_target_pairs={{0,1},{1,0},{2,3},{3,2},{4,5},{5,4},{6,7},{7,6},{8,9},{9,8},{10,11... | collective-permute-start | bytes 786440 | tf_op jit(solution)/shard_map/ppermute | solution.py:229
  53.6 14.0 %collective-permute-start.19 = (bf16[128,1024]{1,0:T(8,128)(2,1)}, bf16[128,1024]{1,0:T(8,128)(2,1)S(1)}, u32[]{:S(2)}, u32[]{:S(2)}) collective-permute-start(bf16[128,1024]{1,0:T(8,128)(2,1)} %get-tuple-element.28), channel_id=1, source_target_pairs={{0,16},{4,20},{8,24},{12,28},{16,0},{20,4},{24,8},{28,12},{1,17},{... | collective-permute-start | bytes 786440 | tf_op jit(solution)/shard_map/ppermute | solution.py:226
  53.7 13.9 %collective-permute-start.18 = (f32[4,128]{1,0:T(4,128)S(1)}, f32[4,128]{1,0:T(4,128)S(1)}, u32[]{:S(2)}, u32[]{:S(2)}) collective-permute-start(f32[4,128]{1,0:T(4,128)S(1)} %copy-done.27), channel_id=1, source_target_pairs={{0,16},{4,20},{8,24},{12,28},{16,0},{20,4},{24,8},{28,12},{1,17},{... | collective-permute-start | bytes 6152 | tf_op jit(solution)/shard_map/ppermute | solution.py:226
  71.0 5.7 %collective-permute-start.20 = (bf16[64,1024]{1,0:T(8,128)(2,1)}, bf16[64,1024]{1,0:T(8,128)(2,1)S(1)}, u32[]{:S(2)}, u32[]{:S(2)}) collective-permute-start(bf16[64,1024]{1,0:T(8,128)(2,1)} %get-tuple-element.30), channel_id=1, source_target_pairs={{0,4},{4,0},{8,12},{12,8},{16,20},{20,16},{24,28},{28,24},{1,5},{5... | collective-permute-start | bytes 393224 | tf_op jit(solution)/shard_map/ppermute | solution.py:226
  72.1 6.3 %collective-permute-start.21 = (bf16[64,1024]{1,0:T(8,128)(2,1)}, bf16[64,1024]{1,0:T(8,128)(2,1)S(1)}, u32[]{:S(2)}, u32[]{:S(2)}) collective-permute-start(bf16[64,1024]{1,0:T(8,128)(2,1)} %get-tuple-element.31), channel_id=1, source_target_pairs={{0,8},{4,12},{8,0},{12,4},{16,24},{20,28},{24,16},{28,20},{1,9},{5... | collective-permute-start | bytes 393224 | tf_op jit(solution)/shard_map/ppermute | solution.py:226
  72.1 8.6 %collective-permute-start.22 = (bf16[64,1024]{1,0:T(8,128)(2,1)}, bf16[64,1024]{1,0:T(8,128)(2,1)S(1)}, u32[]{:S(2)}, u32[]{:S(2)}) collective-permute-start(bf16[64,1024]{1,0:T(8,128)(2,1)} %get-tuple-element.32), channel_id=1, source_target_pairs={{0,12},{4,8},{8,4},{12,0},{16,28},{20,24},{24,20},{28,16},{1,13},{... | collective-permute-start | bytes 393224 | tf_op jit(solution)/shard_map/ppermute | solution.py:226
  85.0 7.6 %collective-permute-start.23 = (bf16[64,1024]{1,0:T(8,128)(2,1)}, bf16[64,1024]{1,0:T(8,128)(2,1)S(1)}, u32[]{:S(2)}, u32[]{:S(2)}) collective-permute-start(bf16[64,1024]{1,0:T(8,128)(2,1)} %get-tuple-element.34), channel_id=1, source_target_pairs={{0,4},{4,0},{8,12},{12,8},{16,20},{20,16},{24,28},{28,24},{1,5},{5... | collective-permute-start | bytes 393224 | tf_op jit(solution)/shard_map/ppermute | solution.py:226
  85.6 7.0 %collective-permute-start.24 = (bf16[64,1024]{1,0:T(8,128)(2,1)}, bf16[64,1024]{1,0:T(8,128)(2,1)S(1)}, u32[]{:S(2)}, u32[]{:S(2)}) collective-permute-start(bf16[64,1024]{1,0:T(8,128)(2,1)} %get-tuple-element.35), channel_id=1, source_target_pairs={{0,8},{4,12},{8,0},{12,4},{16,24},{20,28},{24,16},{28,20},{1,9},{5... | collective-permute-start | bytes 393224 | tf_op jit(solution)/shard_map/ppermute | solution.py:226
  85.9 10.1 %collective-permute-start.25 = (bf16[64,1024]{1,0:T(8,128)(2,1)}, bf16[64,1024]{1,0:T(8,128)(2,1)S(1)}, u32[]{:S(2)}, u32[]{:S(2)}) collective-permute-start(bf16[64,1024]{1,0:T(8,128)(2,1)} %get-tuple-element.36), channel_id=1, source_target_pairs={{0,12},{4,8},{8,4},{12,0},{16,28},{20,24},{24,20},{28,16},{1,13},{... | collective-permute-start | bytes 393224 | tf_op jit(solution)/shard_map/ppermute | solution.py:226
  88.5 11.7 %collective-permute-start.27 = (bf16[64,1024]{1,0:T(8,128)(2,1)S(1)}, bf16[64,1024]{1,0:T(8,128)(2,1)S(1)}, u32[]{:S(2)}, u32[]{:S(2)}) collective-permute-start(bf16[64,1024]{1,0:T(8,128)(2,1)S(1)} %copy-done.33), channel_id=1, source_target_pairs={{0,4},{4,0},{8,12},{12,8},{16,20},{20,16},{24,28},{28,24},{1,5},{5... | collective-permute-start | bytes 393224 | tf_op jit(solution)/shard_map/ppermute | solution.py:226
  89.1 11.1 %collective-permute-start.28 = (bf16[64,1024]{1,0:T(8,128)(2,1)S(1)}, bf16[64,1024]{1,0:T(8,128)(2,1)S(1)}, u32[]{:S(2)}, u32[]{:S(2)}) collective-permute-start(bf16[64,1024]{1,0:T(8,128)(2,1)S(1)} %copy-done.32), channel_id=1, source_target_pairs={{0,8},{4,12},{8,0},{12,4},{16,24},{20,28},{24,16},{28,20},{1,9},{5... | collective-permute-start | bytes 393224 | tf_op jit(solution)/shard_map/ppermute | solution.py:226
  92.6 8.7 %collective-permute-start.29 = (bf16[64,1024]{1,0:T(8,128)(2,1)S(1)}, bf16[64,1024]{1,0:T(8,128)(2,1)S(1)}, u32[]{:S(2)}, u32[]{:S(2)}) collective-permute-start(bf16[64,1024]{1,0:T(8,128)(2,1)S(1)} %copy-done.31), channel_id=1, source_target_pairs={{0,12},{4,8},{8,4},{12,0},{16,28},{20,24},{24,20},{28,16},{1,13},{... | collective-permute-start | bytes 393224 | tf_op jit(solution)/shard_map/ppermute | solution.py:226
  98.9 15.1 %collective-permute-start.26 = (bf16[128,1024]{1,0:T(8,128)(2,1)}, bf16[128,1024]{1,0:T(8,128)(2,1)S(1)}, u32[]{:S(2)}, u32[]{:S(2)}) collective-permute-start(bf16[128,1024]{1,0:T(8,128)(2,1)} %partial.1), channel_id=1, source_target_pairs={{0,16},{4,20},{8,24},{12,28},{16,0},{20,4},{24,8},{28,12},{1,17},{... | collective-permute-start | bytes 786440 | tf_op jit(solution)/shard_map/ppermute | solution.py:226
  105.7 6.6 %collective-permute-start.30 = (bf16[64,1024]{1,0:T(8,128)(2,1)}, bf16[64,1024]{1,0:T(8,128)(2,1)S(1)}, u32[]{:S(2)}, u32[]{:S(2)}) collective-permute-start(bf16[64,1024]{1,0:T(8,128)(2,1)} %get-tuple-element.42), channel_id=1, source_target_pairs={{0,4},{4,0},{8,12},{12,8},{16,20},{20,16},{24,28},{28,24},{1,5},{5... | collective-permute-start | bytes 393224 | tf_op jit(solution)/shard_map/ppermute | solution.py:226
  105.7 6.6 %collective-permute-start.31 = (bf16[64,1024]{1,0:T(8,128)(2,1)}, bf16[64,1024]{1,0:T(8,128)(2,1)S(1)}, u32[]{:S(2)}, u32[]{:S(2)}) collective-permute-start(bf16[64,1024]{1,0:T(8,128)(2,1)} %get-tuple-element.43), channel_id=1, source_target_pairs={{0,8},{4,12},{8,0},{12,4},{16,24},{20,28},{24,16},{28,20},{1,9},{5... | collective-permute-start | bytes 393224 | tf_op jit(solution)/shard_map/ppermute | solution.py:226
  106.7 7.3 %collective-permute-start.32 = (bf16[64,1024]{1,0:T(8,128)(2,1)}, bf16[64,1024]{1,0:T(8,128)(2,1)S(1)}, u32[]{:S(2)}, u32[]{:S(2)}) collective-permute-start(bf16[64,1024]{1,0:T(8,128)(2,1)} %get-tuple-element.44), channel_id=1, source_target_pairs={{0,12},{4,8},{8,4},{12,0},{16,28},{20,24},{24,20},{28,16},{1,13},{... | collective-permute-start | bytes 393224 | tf_op jit(solution)/shard_map/ppermute | solution.py:226
  (35 other events, 391.0 us)

commit v2 on v1

--- a/solution.py
+++ b/solution.py
@@ -6,6 +6,7 @@
 from jax.experimental import pallas as pl
 from jax.experimental.pallas import tpu as pltpu
 from jax.sharding import PartitionSpec as P
+
 
 D = 1024
 H = 16
@@ -14,24 +15,26 @@
 HE = 384
 TOP = 2
 UNROLL_LIMIT = 16
+KERNEL_VMEM = 24 * 1024 * 1024
 BF = jnp.bfloat16
 F32 = jnp.float32
 VMEM = pl.BlockSpec(memory_space=pltpu.VMEM)
 
 
-def call(body, outs, n_in, scratch=(), name=None):
-    return pl.pallas_call(
+def call(body, outs, n_in, scratch=()):
+    run = pl.pallas_call(
         body,
         out_shape=outs,
         in_specs=[VMEM] * n_in,
         out_specs=jax.tree.map(lambda _: VMEM, outs),
         scratch_shapes=scratch,
-        name=name,
-    )
+        compiler_params=pltpu.CompilerParams(vmem_limit_bytes=KERNEL_VMEM),
+    )
+    return lambda *xs: run(*[pltpu.with_memory_space_constraint(x, pltpu.VMEM) for x in xs])
 
 
 def sds(shape, dtype):
-    return jax.ShapeDtypeStruct(shape, dtype)
+    return pltpu.VMEM(shape, dtype)
 
 
 def dot(a, b, dims=((1,), (0,))):
@@ -49,13 +52,13 @@
     send_ref[...] = full[pl.ds(pl.multiple_of((1 - y) * half, half), half), :].astype(BF)
 
 
-def intra_body(q_ref, k_ref, v_ref, out_ref):
+def intra_body(first, q_ref, k_ref, v_ref, out_ref):
     length = q_ref.shape[0]
     lane = lax.broadcasted_iota(jnp.int32, (length, 2 * DK), 1)
     row = lax.broadcasted_iota(jnp.int32, (length, length), 0)
     col = lax.broadcasted_iota(jnp.int32, (length, length), 1)
     causal = row >= col
-    for p in range(H // 2):
+    for p in range(first, first + H // 4):
         q = q_ref[:, 2 * DK * p : 2 * DK * (p + 1)]
         k = k_ref[:, 2 * DK * p : 2 * DK * (p + 1)]
         for i in range(2):
@@ -63,7 +66,8 @@
             s = dot(jnp.where(mine, q, jnp.zeros_like(q)), k, ((1,), (1,)))
             s = jnp.where(causal, s, 0.0).astype(BF)
             c = (2 * p + i) * DV
-            out_ref[:, c : c + DV] = dot(s, v_ref[:, c : c + DV])
+            o = c - 2 * first * DV
+            out_ref[:, o : o + DV] = dot(s, v_ref[:, c : c + DV])
 
 
 def keys_of(meta, experts):
@@ -93,16 +97,18 @@
         out[...] = rows[k * cap : (k + 1) * cap, :]
 
 
-def project_body(n, q_ref, intra_ref, pm_ref, po_ref, wown_ref, res_ref, meta_ref, *refs):
+def project_body(n, offsets, q_ref, ia_ref, ib_ref, pm_ref, po_ref, wown_ref, res_ref, meta_ref, *refs):
     fwd, bwd = n // 2, n // 2 - 1
-    pieces, refs = refs[: 2 * (fwd + bwd)], refs[2 * (fwd + bwd) :]
-    fm, refs_f = pieces[:fwd], pieces[fwd : 2 * fwd]
-    bm, refs_b = pieces[2 * fwd : 2 * fwd + bwd], pieces[2 * fwd + bwd :]
+    copies = len(offsets)
+    fs = [refs[j * copies : (j + 1) * copies] for j in range(fwd)]
+    refs = refs[fwd * copies :]
+    bs = [refs[j * copies : (j + 1) * copies] for j in range(bwd)]
+    refs = refs[bwd * copies :]
     hidden_ref, normed_ref = refs[:2]
     outs = refs[2 : 2 + n // 2]
     prefix, att, hid, key_ref = refs[2 + n // 2 :]
     s = lax.axis_index("seq")
-    c = lax.rem(lax.axis_index("win"), 2)
+    w = lax.axis_index("win")
     y = lax.rem(s, 2)
     length = q_ref.shape[0]
     half = prefix.shape[0] // 2
@@ -116,11 +122,14 @@
         low = jnp.concatenate([zero, prefix[2 * DK * p + DK : 2 * DK * (p + 1), :]], axis=1)
         inter = dot(q_ref[:, 2 * DK * p : 2 * DK * (p + 1)], jnp.concatenate([top, low], axis=0))
         cols = slice(2 * DV * p, 2 * DV * (p + 1))
-        att[:, cols] = ((intra_ref[:, cols] + inter) * scaling).astype(BF)
-    rows = att.shape[1] // 2
+        src, at = (ia_ref, p) if p < H // 4 else (ib_ref, p - H // 4)
+        intra = src[:, 2 * DV * at : 2 * DV * (at + 1)]
+        att[:, cols] = ((intra + inter) * scaling).astype(BF)
+    rows = att.shape[1] // copies
     width = wown_ref.shape[1]
-    att_m = att[:, pl.ds(pl.multiple_of(c * rows, rows), rows)]
-    att_p = att[:, pl.ds(pl.multiple_of((1 - c) * rows, rows), rows)]
+    parts = [
+        att[:, pl.ds(pl.multiple_of(jnp.bitwise_xor(w, o) * rows, rows), rows)] for o in offsets
+    ]
     pos = jnp.where(y == 0, s // 2, n - 1 - s // 2)
 
     def source(shift):
@@ -132,14 +141,17 @@
 
     put(0, dot(att[...], wown_ref[...]))
     for j in range(fwd):
-        if j < bwd:
-            m = jnp.concatenate([fm[j][...], bm[j][...]], axis=1)
-            o = jnp.concatenate([refs_f[j][...], refs_b[j][...]], axis=1)
-            both = dot(att_m, m) + dot(att_p, o)
-            put(-(j + 1), both[:, :width])
-            put(j + 1, both[:, width:])
-        else:
-            put(-(j + 1), dot(att_m, fm[j][...]) + dot(att_p, refs_f[j][...]))
+        both = j < bwd
+        total = None
+        for i, part in enumerate(parts):
+            m = fs[j][i][...]
+            if both:
+                m = jnp.concatenate([m, bs[j][i][...]], axis=1)
+            r = dot(part, m)
+            total = r if total is None else total + r
+        put(-(j + 1), total[:, :width])
+        if both:
+            put(j + 1, total[:, width:])
     hidden = (res_ref[...].astype(F32) + hid[...]).astype(BF)
     hidden_ref[...] = hidden
     h = hidden.astype(F32)
@@ -211,10 +223,9 @@
     gate_values,
 ):
     n = lax.axis_size("seq")
+    copies = lax.axis_size("win")
     length = queries.shape[0]
-    s = lax.axis_index("seq")
-    c = lax.rem(lax.axis_index("win"), 2)
-    y = lax.rem(s, 2)
+    y = lax.rem(lax.axis_index("seq"), 2)
     near = n // 2
     cap = max(2, 2 * length * TOP // n)
     half = H * DK // 2
@@ -225,16 +236,35 @@
     def flip(x, k):
         return lax.ppermute(x, "seq", [(i, i ^ k) for i in range(n)])
 
-    def swap_core(x):
-        return lax.ppermute(x, "win", [(i, i ^ 1) for i in range(lax.axis_size("win"))])
-
-    mine, sent = call(
+    def kernel(body, outs, xs, scratch=()):
+        return call(body, outs, len(xs), scratch)(*xs)
+
+    def flips(xs):
+        return [xs[0]] + [flip(xs[k], k) for k in range(1, near)]
+
+    offsets = [0]
+    rows = H * DV // copies
+    piece = lax.dynamic_slice_in_dim(out_weight, lax.axis_index("win") * rows, rows, 0)
+    spread = []
+    bit = copies // 2
+    while bit:
+        spread.append(bit)
+        offsets = offsets + [o ^ bit for o in offsets]
+        bit //= 2
+
+    def share(x):
+        held = [x]
+        for k in spread:
+            pairs = [(i, i ^ k) for i in range(copies)]
+            held = held + [lax.ppermute(h, "win", pairs) for h in held]
+        return held
+
+    mine, sent = kernel(
         states_body,
         (sds((half, DV), F32), sds((half, DV), BF)),
-        2,
+        (key_rows, value_rows),
         [pltpu.VMEM((2 * half, DV), F32)],
-        name="states",
-    )(key_rows, value_rows)
+    )
     got = flip(sent, 1).astype(F32)
     run = mine + got
     before = jnp.zeros_like(mine)
@@ -247,64 +277,63 @@
     prefix_mine = (before + jnp.where(y == 0, 0.0, got)).astype(BF)
     prefix_other = flip((before + jnp.where(y == 0, mine, 0.0)).astype(BF), 1)
 
-    rows = H * DV // 2
-    piece = lax.dynamic_slice_in_dim(out_weight, c * rows, rows, 0)
-    fm, bm = [], []
+    fs, bs = [], []
     f = b = piece
     for j in range(near):
         f = lax.ppermute(f, "seq", ahead)
-        fm.append(f)
+        fs += share(f)
         if j < near - 1:
             b = lax.ppermute(b, "seq", back)
-            bm.append(b)
-    fp = [swap_core(x) for x in fm]
-    bp = [swap_core(x) for x in bm]
+            bs += share(b)
 
     meta = jnp.concatenate([expert_ids.astype(F32), gate_values], axis=1).T
     meta_far = flip(meta, near)
 
-    intra = call(intra_body, sds((length, H * DV), F32), 3, name="intra")(queries, key_rows, value_rows)
-
-    ins = [queries, intra, prefix_mine, prefix_other, out_weight, residual, meta, *fm, *fp, *bm, *bp]
+    tokens = (queries, key_rows, value_rows)
+    intra = [
+        kernel(functools.partial(intra_body, i * (H // 4)), sds((length, H * DV // 2), F32), tokens)
+        for i in range(2)
+    ]
     row_buf = sds((cap, D), BF)
-    hidden, normed, *deal_own = call(
-        functools.partial(project_body, n),
-        (sds((length, D), BF), sds((length, D), BF), *[row_buf] * near),
-        len(ins),
+    full = sds((length, D), BF)
+    keys = pltpu.VMEM((n, length), F32)
+    hidden, normed, *deal_own = kernel(
+        functools.partial(project_body, n, offsets),
+        (full, full, *[row_buf] * near),
+        (queries, *intra, prefix_mine, prefix_other, out_weight, residual, meta, *fs, *bs),
         [
             pltpu.VMEM((2 * half, DV), BF),
             pltpu.VMEM((length, H * DV), BF),
             pltpu.VMEM((length, D), F32),
-            pltpu.VMEM((n, length), F32),
+            keys,
         ],
-        name="project",
-    )(*ins)
+    )
     normed_far = flip(normed, near)
-    own_in = [deal_own[0]] + [flip(deal_own[k], k) for k in range(1, near)]
-    deal_far = call(
-        functools.partial(deal_body, n),
-        tuple([row_buf] * near),
-        2,
-        [pltpu.VMEM((n, length), F32)],
-        name="deal",
-    )(normed_far, meta_far)
-    far_in = [deal_far[0]] + [flip(deal_far[k], k) for k in range(1, near)]
-
-    experts = call(
-        functools.partial(expert_body, near), tuple([row_buf] * near), 2 + near, name="experts"
-    )
-    own_out = experts(expert_in, expert_out, *own_in)
-    far_out = experts(expert_in, expert_out, *far_in)
-    own_back = [own_out[0]] + [flip(own_out[k], k) for k in range(1, near)]
-    far_back = [far_out[0]] + [flip(far_out[k], k) for k in range(1, near)]
-    scratch = [pltpu.VMEM((n, length), F32), pltpu.VMEM((n, length), F32)]
-    part_far = call(
-        functools.partial(partial_body, n), sds((length, D), BF), 1 + near, scratch, name="partial"
-    )(meta_far, *far_back)
+    own_in = flips(deal_own)
+    deal_far = kernel(
+        functools.partial(deal_body, n), tuple([row_buf] * near), (normed_far, meta_far), [keys]
+    )
+    far_in = flips(deal_far)
+
+    def experts(xs):
+        return kernel(
+            functools.partial(expert_body, near),
+            tuple([row_buf] * near),
+            (expert_in, expert_out, *xs),
+        )
+
+    own_out = experts(own_in)
+    own_back = flips(own_out)
+    far_out = experts(far_in)
+    far_back = flips(far_out)
+    part_far = kernel(functools.partial(partial_body, n), full, (meta_far, *far_back), [keys, keys])
     part_own = flip(part_far, near)
-    return call(
-        functools.partial(final_body, n), sds((length, D), BF), 3 + near, scratch, name="final"
-    )(meta, hidden, part_own, *own_back)
+    return kernel(
+        functools.partial(final_body, n),
+        jax.ShapeDtypeStruct((length, D), BF),
+        (meta, hidden, part_own, *own_back),
+        [keys, keys],
+    )
 
 
 def large_group(
@@ -396,10 +425,11 @@
         P(("win", "seq"), None),
     )
     out_specs = P(("win", "seq"), None)
+    if not small:
+        return jax.shard_map(
+            large_group, mesh=mesh, in_specs=in_specs, out_specs=out_specs, check_vma=False
+        )
+
     return jax.shard_map(
-        small_group if small else large_group,
-        mesh=mesh,
-        in_specs=in_specs,
-        out_specs=out_specs,
-        check_vma=False,
-    )
+        small_group, mesh=mesh, in_specs=in_specs, out_specs=out_specs, check_vma=False
+    )

time: 118 us -> 106 us (0.90)
  Pallas kernels: 26.2 us -> 9.09 us
  starting transfers between devices: 36.8 us -> 44.7 us
  waiting for transfers between devices: 43.7 us -> 48.9 us
  other arithmetic: 4.27 us -> 0.18 us
  local copies, waits for them, and re-layouts: 5.82 us -> 2.94 us
    pallas_call x8 -> x9, Pallas kernels: 26.2 us -> 9.09 us  [call(): run(*[pltpu.with_memory_space_constraint(x, pltpu.VMEM) for x in xs])]
    ppermute x7 -> x21, waiting for transfers between devices: 0.02 us -> 7.04 us  [share(): held = held + [lax.ppermute(h, 'win', pairs) for h in held]]
    ppermute x7 -> x21, starting transfers between devices: 1.65 us -> 7.66 us  [share(): held = held + [lax.ppermute(h, 'win', pairs) for h in held]]
    ppermute x17, waiting for transfers between devices: 39.2 us -> 33.5 us  [flip(): return lax.ppermute(x, 'seq', [(i, i ^ k) for i in range(n)])]
    ppermute x17, starting transfers between devices: 16.7 us -> 22.1 us  [flip(): return lax.ppermute(x, 'seq', [(i, i ^ k) for i in range(n)])]
    ppermute x4, waiting for transfers between devices: 4.14 us -> 7.05 us  [small_group(): f = lax.ppermute(f, 'seq', ahead)]
    unnamed x68 -> x22, local copies, waits for them, and re-layouts: 4.85 us -> 2.03 us
    ppermute x3, starting transfers between devices: 4.87 us -> 2.19 us  [small_group(): b = lax.ppermute(b, 'seq', back)]
  transfers between devices with their start and end apart: 33 -> 47, of which waited for: 14 -> 23; matrix products, arithmetic and copies ran while one was open for 4% -> 1% of each run, Pallas kernels for 11% -> 4%
where the time goes in v2:
time: 106 us
  waiting for transfers between devices  48.9 us (46%)
  starting transfers between devices  44.7 us (42%)
  Pallas kernels  9.09 us (9%)
  local copies, waits for them, and re-layouts  2.94 us (3%)
    ppermute x17, waiting for transfers between devices, flip(): return lax.ppermute(x, 'seq', [(i, i ^ k) for i in range(n)])  33.5 us
    ppermute x17, starting transfers between devices, flip(): return lax.ppermute(x, 'seq', [(i, i ^ k) for i in range(n)])  22.1 us
    pallas_call x9, Pallas kernels, call(): run(*[pltpu.with_memory_space_constraint(x, pltpu.VMEM) for x in xs])  9.09 us
    ppermute x21, starting transfers between devices, share(): held = held + [lax.ppermute(h, 'win', pairs) for h in held]  7.66 us
    ppermute x4, waiting for transfers between devices, small_group(): f = lax.ppermute(f, 'seq', ahead)  7.05 us
    ppermute x21, waiting for transfers between devices, share(): held = held + [lax.ppermute(h, 'win', pairs) for h in held]  7.04 us
    ppermute x2, starting transfers between devices, small_group(): came = lax.ppermute(run.astype(BF), 'seq', hop).astype(F32)  6.95 us
    ppermute x4, starting transfers between devices, small_group(): f = lax.ppermute(f, 'seq', ahead)  5.78 us
  transfers between devices with their start and end apart: 47, of which 23 were waited for; matrix products, arithmetic and copies ran while one was open for 1% of the time, Pallas kernels for 4%

profile of v2, /device:TPU:0, one launch (start us, length us, event | category | flops | bytes accessed | tf_op | source)
XLA Modules:
  0.0 106.1 jit_solution(13884703329308030317)
XLA Ops:
  2.4 3.1 %collective-permute-start = (bf16[512,128]{1,0:T(8,128)(2,1)S(1)}, bf16[512,128]{1,0:T(8,128)(2,1)S(1)}, u32[]{:S(2)}, u32[]{:S(2)}) collective-permute-start(bf16[512,128]{1,0:T(8,128)(2,1)S(1)} %get-tuple-element.26), channel_id=1, source_target_pairs={{0,4},{4,0},{8,12},{12,8},{16,20},{20,16},{24,28},{28,24},{1,5},{5... | collective-permute-start | bytes 393224 | tf_op jit(solution)/shard_map/ppermute | solution.py:237
  6.4 1.6 %collective-permute-start.4 = (bf16[512,128]{1,0:T(8,128)(2,1)S(1)}, bf16[512,128]{1,0:T(8,128)(2,1)S(1)}, u32[]{:S(2)}, u32[]{:S(2)}) collective-permute-start(bf16[512,128]{1,0:T(8,128)(2,1)S(1)} %constant_dynamic-slice_fusion), channel_id=1, source_target_pairs={{0,8},{8,16},{16,24},{24,28},{28,20},{20,12},{12,4},{4,0},{1,9},{9... | collective-permute-start | bytes 393224 | tf_op jit(solution)/shard_map/ppermute | solution.py:283
  9.4 3.3 %collective-permute-start.1 = (bf16[512,128]{1,0:T(8,128)(2,1)S(1)}, bf16[512,128]{1,0:T(8,128)(2,1)S(1)}, u32[]{:S(2)}, u32[]{:S(2)}) collective-permute-start(bf16[512,128]{1,0:T(8,128)(2,1)S(1)} %fusion.3), channel_id=1, source_target_pairs={{0,8},{4,12},{8,16},{12,20},{16,24},{20,28},{1,9},{5,13},{9,17},{1... | collective-permute-start | bytes 393224 | tf_op jit(solution)/shard_map/ppermute | solution.py:274
  14.3 1.5 %collective-permute-start.21 = (bf16[512,128]{1,0:T(8,128)(2,1)S(1)}, bf16[512,128]{1,0:T(8,128)(2,1)S(1)}, u32[]{:S(2)}, u32[]{:S(2)}) collective-permute-start(bf16[512,128]{1,0:T(8,128)(2,1)S(1)} %collective-permute-done.20.refs_16_), channel_id=1, source_target_pairs={{0,2},{1,3},{2,0},{3,1},{4,6},{5,7},{6,4},{7,5},{8,10},{9,11},{10,... | collective-permute-start | bytes 393224 | tf_op jit(solution)/shard_map/ppermute | solution.py:259
  17.1 3.7 %collective-permute-done.8.refs_4_ = bf16[512,128]{1,0:T(8,128)(2,1)S(1)} collective-permute-done((bf16[512,128]{1,0:T(8,128)(2,1)S(1)}, bf16[512,128]{1,0:T(8,128)(2,1)S(1)}, u32[]{:S(2)}, u32[]{:S(2)}) %collective-permute-start.8) | collective-permute-done | bytes 131104 | tf_op jit(solution)/shard_map/ppermute | solution.py:283
  20.8 3.6 %collective-permute-start.2 = (bf16[512,128]{1,0:T(8,128)(2,1)S(1)}, bf16[512,128]{1,0:T(8,128)(2,1)S(1)}, u32[]{:S(2)}, u32[]{:S(2)}) collective-permute-start(bf16[512,128]{1,0:T(8,128)(2,1)S(1)} %fusion.2), channel_id=1, source_target_pairs={{0,16},{4,20},{8,24},{12,28},{1,17},{5,21},{9,25},{13,29},{2,18},{... | collective-permute-start | bytes 393224 | tf_op jit(solution)/shard_map/ppermute | solution.py:274
  24.4 1.8 %collective-permute-start.12 = (bf16[512,128]{1,0:T(8,128)(2,1)S(1)}, bf16[512,128]{1,0:T(8,128)(2,1)S(1)}, u32[]{:S(2)}, u32[]{:S(2)}) collective-permute-start(bf16[512,128]{1,0:T(8,128)(2,1)S(1)} %collective-permute-done.8.refs_4_), channel_id=1, source_target_pairs={{0,8},{8,16},{16,24},{24,28},{28,20},{20,12},{12,4},{4,0},{1,9},{9... | collective-permute-start | bytes 393224 | tf_op jit(solution)/shard_map/ppermute | solution.py:283
  27.2 1.5 %collective-permute-start.25 = (bf16[512,128]{1,0:T(8,128)(2,1)S(1)}, bf16[512,128]{1,0:T(8,128)(2,1)S(1)}, u32[]{:S(2)}, u32[]{:S(2)}) collective-permute-start(bf16[512,128]{1,0:T(8,128)(2,1)S(1)} %collective-permute-done.24.refs_20_), channel_id=1, source_target_pairs={{0,2},{1,3},{2,0},{3,1},{4,6},{5,7},{6,4},{7,5},{8,10},{9,11},{10,... | collective-permute-start | bytes 393224 | tf_op jit(solution)/shard_map/ppermute | solution.py:259
  28.7 2.0 %collective-permute-done.12.refs_8_ = bf16[512,128]{1,0:T(8,128)(2,1)S(1)} collective-permute-done((bf16[512,128]{1,0:T(8,128)(2,1)S(1)}, bf16[512,128]{1,0:T(8,128)(2,1)S(1)}, u32[]{:S(2)}, u32[]{:S(2)}) %collective-permute-start.12) | collective-permute-done | bytes 131104 | tf_op jit(solution)/shard_map/ppermute | solution.py:283
  32.6 1.8 %collective-permute-done.25.refs_21_ = bf16[512,128]{1,0:T(8,128)(2,1)S(1)} collective-permute-done((bf16[512,128]{1,0:T(8,128)(2,1)S(1)}, bf16[512,128]{1,0:T(8,128)(2,1)S(1)}, u32[]{:S(2)}, u32[]{:S(2)}) %collective-permute-start.25) | collective-permute-done | bytes 131104 | tf_op jit(solution)/shard_map/ppermute | solution.py:259
  35.1 1.7 %collective-permute-start.16 = (bf16[512,128]{1,0:T(8,128)(2,1)S(1)}, bf16[512,128]{1,0:T(8,128)(2,1)S(1)}, u32[]{:S(2)}, u32[]{:S(2)}) collective-permute-start(bf16[512,128]{1,0:T(8,128)(2,1)S(1)} %collective-permute-done.12.refs_8_), channel_id=1, source_target_pairs={{0,8},{8,16},{16,24},{24,28},{28,20},{20,12},{12,4},{4,0},{1,9},{9... | collective-permute-start | bytes 393224 | tf_op jit(solution)/shard_map/ppermute | solution.py:283
  37.3 1.5 %collective-permute-start.29 = (bf16[512,128]{1,0:T(8,128)(2,1)S(1)}, bf16[512,128]{1,0:T(8,128)(2,1)S(1)}, u32[]{:S(2)}, u32[]{:S(2)}) collective-permute-start(bf16[512,128]{1,0:T(8,128)(2,1)S(1)} %collective-permute-done.28.refs_24_), channel_id=1, source_target_pairs={{0,2},{1,3},{2,0},{3,1},{4,6},{5,7},{6,4},{7,5},{8,10},{9,11},{10,... | collective-permute-start | bytes 393224 | tf_op jit(solution)/shard_map/ppermute | solution.py:259
  38.8 1.5 %collective-permute-done.3.po_ref = bf16[512,128]{1,0:T(8,128)(2,1)S(1)} collective-permute-done((bf16[512,128]{1,0:T(8,128)(2,1)S(1)}, bf16[512,128]{1,0:T(8,128)(2,1)S(1)}, u32[]{:S(2)}, u32[]{:S(2)}) %collective-permute-start.3) | collective-permute-done | bytes 131104 | tf_op jit(solution)/shard_map/ppermute | solution.py:237
  40.3 1.4 %collective-permute-done.16.refs_12_ = bf16[512,128]{1,0:T(8,128)(2,1)S(1)} collective-permute-done((bf16[512,128]{1,0:T(8,128)(2,1)S(1)}, bf16[512,128]{1,0:T(8,128)(2,1)S(1)}, u32[]{:S(2)}, u32[]{:S(2)}) %collective-permute-start.16) | collective-permute-done | bytes 131104 | tf_op jit(solution)/shard_map/ppermute | solution.py:283
  45.2 2.5 %collective-permute-done.17.refs_13_ = bf16[512,128]{1,0:T(8,128)(2,1)S(1)} collective-permute-done((bf16[512,128]{1,0:T(8,128)(2,1)S(1)}, bf16[512,128]{1,0:T(8,128)(2,1)S(1)}, u32[]{:S(2)}, u32[]{:S(2)}) %collective-permute-start.17) | collective-permute-done | bytes 131104 | tf_op jit(solution)/shard_map/ppermute | solution.py:259
  50.6 1.5 %shard_map.94 = (bf16[128,1024]{1,0:T(8,128)(2,1)S(1)}, bf16[128,1024]{1,0:T(8,128)(2,1)S(1)}, bf16[64,1024]{1,0:T(8,128)(2,1)S(1)}, bf16[64,1024]{1,0:T(8,128)(...) custom-call(bf16[128,1024]{1,0:T(8,128)(2,1)S(1)} %copy-done.6, f32[128,1024]{1,0:T(8,128)S(1)} %shard_map.91.ia_ref, ...), custom_call_target="tpu_custom_call" | custom-call | tf_op jit(solution)/shard_map/pallas_call | solution.py:33
  52.2 1.9 %collective-permute-start.33 = (bf16[128,1024]{1,0:T(8,128)(2,1)S(1)}, bf16[128,1024]{1,0:T(8,128)(2,1)S(1)}, u32[]{:S(2)}, u32[]{:S(2)}) collective-permute-start(bf16[128,1024]{1,0:T(8,128)(2,1)S(1)} %get-tuple-element.28), channel_id=1, source_target_pairs={{0,16},{4,20},{8,24},{12,28},{16,0},{20,4},{24,8},{28,12},{1,17},{... | collective-permute-start | bytes 786440 | tf_op jit(solution)/shard_map/ppermute | solution.py:237
  55.1 12.4 %collective-permute-done.32.meta_ref = f32[4,128]{1,0:T(4,128)S(1)} collective-permute-done((f32[4,128]{1,0:T(4,128)S(1)}, f32[4,128]{1,0:T(4,128)S(1)}, u32[]{:S(2)}, u32[]{:S(2)}) %collective-permute-start.32) | collective-permute-done | bytes 2080 | tf_op jit(solution)/shard_map/ppermute | solution.py:237
  69.5 2.0 %collective-permute-start.36 = (bf16[64,1024]{1,0:T(8,128)(2,1)S(1)}, bf16[64,1024]{1,0:T(8,128)(2,1)S(1)}, u32[]{:S(2)}, u32[]{:S(2)}) collective-permute-start(bf16[64,1024]{1,0:T(8,128)(2,1)S(1)} %get-tuple-element.32), channel_id=1, source_target_pairs={{0,12},{4,8},{8,4},{12,0},{16,28},{20,24},{24,20},{28,16},{1,13},{... | collective-permute-start | bytes 393224 | tf_op jit(solution)/shard_map/ppermute | solution.py:237
  71.5 2.0 %collective-permute-done.34.refs_1_ = bf16[64,1024]{1,0:T(8,128)(2,1)S(1)} collective-permute-done((bf16[64,1024]{1,0:T(8,128)(2,1)S(1)}, bf16[64,1024]{1,0:T(8,128)(2,1)S(1)}, u32[]{:S(2)}, u32[]{:S(2)}) %collective-permute-start.34) | collective-permute-done | bytes 131104 | tf_op jit(solution)/shard_map/ppermute | solution.py:237
  73.5 1.6 %collective-permute-done.35.refs_2_ = bf16[64,1024]{1,0:T(8,128)(2,1)S(1)} collective-permute-done((bf16[64,1024]{1,0:T(8,128)(2,1)S(1)}, bf16[64,1024]{1,0:T(8,128)(2,1)S(1)}, u32[]{:S(2)}, u32[]{:S(2)}) %collective-permute-start.35) | collective-permute-done | bytes 131104 | tf_op jit(solution)/shard_map/ppermute | solution.py:237
  75.1 1.9 %collective-permute-done.36.refs_3_ = bf16[64,1024]{1,0:T(8,128)(2,1)S(1)} collective-permute-done((bf16[64,1024]{1,0:T(8,128)(2,1)S(1)}, bf16[64,1024]{1,0:T(8,128)(2,1)S(1)}, u32[]{:S(2)}, u32[]{:S(2)}) %collective-permute-start.36) | collective-permute-done | bytes 131104 | tf_op jit(solution)/shard_map/ppermute | solution.py:237
  80.2 1.6 %collective-permute-start.39 = (bf16[64,1024]{1,0:T(8,128)(2,1)S(1)}, bf16[64,1024]{1,0:T(8,128)(2,1)S(1)}, u32[]{:S(2)}, u32[]{:S(2)}) collective-permute-start(bf16[64,1024]{1,0:T(8,128)(2,1)S(1)} %get-tuple-element.36), channel_id=1, source_target_pairs={{0,12},{4,8},{8,4},{12,0},{16,28},{20,24},{24,20},{28,16},{1,13},{... | collective-permute-start | bytes 393224 | tf_op jit(solution)/shard_map/ppermute | solution.py:237
  83.7 2.3 %collective-permute-done.37.refs_1_ = bf16[64,1024]{1,0:T(8,128)(2,1)S(1)} collective-permute-done((bf16[64,1024]{1,0:T(8,128)(2,1)S(1)}, bf16[64,1024]{1,0:T(8,128)(2,1)S(1)}, u32[]{:S(2)}, u32[]{:S(2)}) %collective-permute-start.37) | collective-permute-done | bytes 131104 | tf_op jit(solution)/shard_map/ppermute | solution.py:237
  86.9 2.2 %collective-permute-done.39.refs_3_ = bf16[64,1024]{1,0:T(8,128)(2,1)S(1)} collective-permute-done((bf16[64,1024]{1,0:T(8,128)(2,1)S(1)}, bf16[64,1024]{1,0:T(8,128)(2,1)S(1)}, u32[]{:S(2)}, u32[]{:S(2)}) %collective-permute-start.39) | collective-permute-done | bytes 131104 | tf_op jit(solution)/shard_map/ppermute | solution.py:237
  89.6 1.9 %collective-permute-start.40 = (bf16[128,1024]{1,0:T(8,128)(2,1)S(1)}, bf16[128,1024]{1,0:T(8,128)(2,1)S(1)}, u32[]{:S(2)}, u32[]{:S(2)}) collective-permute-start(bf16[128,1024]{1,0:T(8,128)(2,1)S(1)} %shard_map.97), channel_id=1, source_target_pairs={{0,16},{4,20},{8,24},{12,28},{16,0},{20,4},{24,8},{28,12},{1,17},{... | collective-permute-start | bytes 786440 | tf_op jit(solution)/shard_map/ppermute | solution.py:237
  91.4 1.7 %collective-permute-done.42.refs_2_ = bf16[64,1024]{1,0:T(8,128)(2,1)S(1)} collective-permute-done((bf16[64,1024]{1,0:T(8,128)(2,1)S(1)}, bf16[64,1024]{1,0:T(8,128)(2,1)S(1)}, u32[]{:S(2)}, u32[]{:S(2)}) %collective-permute-start.42) | collective-permute-done | bytes 131104 | tf_op jit(solution)/shard_map/ppermute | solution.py:237
  93.2 1.9 %collective-permute-done.43.refs_3_ = bf16[64,1024]{1,0:T(8,128)(2,1)S(1)} collective-permute-done((bf16[64,1024]{1,0:T(8,128)(2,1)S(1)}, bf16[64,1024]{1,0:T(8,128)(2,1)S(1)}, u32[]{:S(2)}, u32[]{:S(2)}) %collective-permute-start.43) | collective-permute-done | bytes 131104 | tf_op jit(solution)/shard_map/ppermute | solution.py:237
  96.3 1.5 %collective-permute-start.44 = (bf16[64,1024]{1,0:T(8,128)(2,1)S(1)}, bf16[64,1024]{1,0:T(8,128)(2,1)S(1)}, u32[]{:S(2)}, u32[]{:S(2)}) collective-permute-start(bf16[64,1024]{1,0:T(8,128)(2,1)S(1)} %get-tuple-element.42), channel_id=1, source_target_pairs={{0,4},{4,0},{8,12},{12,8},{16,20},{20,16},{24,28},{28,24},{1,5},{5... | collective-permute-start | bytes 393224 | tf_op jit(solution)/shard_map/ppermute | solution.py:237
  97.8 2.0 %collective-permute-start.46 = (bf16[64,1024]{1,0:T(8,128)(2,1)S(1)}, bf16[64,1024]{1,0:T(8,128)(2,1)S(1)}, u32[]{:S(2)}, u32[]{:S(2)}) collective-permute-start(bf16[64,1024]{1,0:T(8,128)(2,1)S(1)} %get-tuple-element.44), channel_id=1, source_target_pairs={{0,12},{4,8},{8,4},{12,0},{16,28},{20,24},{24,20},{28,16},{1,13},{... | collective-permute-start | bytes 393224 | tf_op jit(solution)/shard_map/ppermute | solution.py:237
  99.8 2.0 %collective-permute-done.44.refs_1_ = bf16[64,1024]{1,0:T(8,128)(2,1)S(1)} collective-permute-done((bf16[64,1024]{1,0:T(8,128)(2,1)S(1)}, bf16[64,1024]{1,0:T(8,128)(2,1)S(1)}, u32[]{:S(2)}, u32[]{:S(2)}) %collective-permute-start.44) | collective-permute-done | bytes 131104 | tf_op jit(solution)/shard_map/ppermute | solution.py:237
  102.9 1.9 %collective-permute-done.46.refs_3_ = bf16[64,1024]{1,0:T(8,128)(2,1)S(1)} collective-permute-done((bf16[64,1024]{1,0:T(8,128)(2,1)S(1)}, bf16[64,1024]{1,0:T(8,128)(2,1)S(1)}, u32[]{:S(2)}, u32[]{:S(2)}) %collective-permute-start.46) | collective-permute-done | bytes 131104 | tf_op jit(solution)/shard_map/ppermute | solution.py:237
  (99 shorter events, 30.9 us)
Async XLA Ops:
  2.4 6.9 %collective-permute-start = (bf16[512,128]{1,0:T(8,128)(2,1)S(1)}, bf16[512,128]{1,0:T(8,128)(2,1)S(1)}, u32[]{:S(2)}, u32[]{:S(2)}) collective-permute-start(bf16[512,128]{1,0:T(8,128)(2,1)S(1)} %get-tuple-element.26), channel_id=1, source_target_pairs={{0,4},{4,0},{8,12},{12,8},{16,20},{20,16},{24,28},{28,24},{1,5},{5... | collective-permute-start | bytes 393224 | tf_op jit(solution)/shard_map/ppermute | solution.py:237
  6.4 9.4 %collective-permute-start.4 = (bf16[512,128]{1,0:T(8,128)(2,1)S(1)}, bf16[512,128]{1,0:T(8,128)(2,1)S(1)}, u32[]{:S(2)}, u32[]{:S(2)}) collective-permute-start(bf16[512,128]{1,0:T(8,128)(2,1)S(1)} %constant_dynamic-slice_fusion), channel_id=1, source_target_pairs={{0,8},{8,16},{16,24},{24,28},{28,20},{20,12},{12,4},{4,0},{1,9},{9... | collective-permute-start | bytes 393224 | tf_op jit(solution)/shard_map/ppermute | solution.py:283
  9.4 7.7 %collective-permute-start.1 = (bf16[512,128]{1,0:T(8,128)(2,1)S(1)}, bf16[512,128]{1,0:T(8,128)(2,1)S(1)}, u32[]{:S(2)}, u32[]{:S(2)}) collective-permute-start(bf16[512,128]{1,0:T(8,128)(2,1)S(1)} %fusion.3), channel_id=1, source_target_pairs={{0,8},{4,12},{8,16},{12,20},{16,24},{20,28},{1,9},{5,13},{9,17},{1... | collective-permute-start | bytes 393224 | tf_op jit(solution)/shard_map/ppermute | solution.py:274
  13.0 7.8 %collective-permute-start.24 = (bf16[512,128]{1,0:T(8,128)(2,1)S(1)}, bf16[512,128]{1,0:T(8,128)(2,1)S(1)}, u32[]{:S(2)}, u32[]{:S(2)}) collective-permute-start(bf16[512,128]{1,0:T(8,128)(2,1)S(1)} %collective-permute-done.20.refs_16_), channel_id=1, source_target_pairs={{8,0},{16,8},{24,16},{28,24},{20,28},{12,20},{4,12},{0,4},{9,1},{1... | collective-permute-start | bytes 393224 | tf_op jit(solution)/shard_map/ppermute | solution.py:286
  14.3 10.1 %collective-permute-start.21 = (bf16[512,128]{1,0:T(8,128)(2,1)S(1)}, bf16[512,128]{1,0:T(8,128)(2,1)S(1)}, u32[]{:S(2)}, u32[]{:S(2)}) collective-permute-start(bf16[512,128]{1,0:T(8,128)(2,1)S(1)} %collective-permute-done.20.refs_16_), channel_id=1, source_target_pairs={{0,2},{1,3},{2,0},{3,1},{4,6},{5,7},{6,4},{7,5},{8,10},{9,11},{10,... | collective-permute-start | bytes 393224 | tf_op jit(solution)/shard_map/ppermute | solution.py:259
  16.5 9.7 %collective-permute-start.5 = (bf16[512,128]{1,0:T(8,128)(2,1)S(1)}, bf16[512,128]{1,0:T(8,128)(2,1)S(1)}, u32[]{:S(2)}, u32[]{:S(2)}) collective-permute-start(bf16[512,128]{1,0:T(8,128)(2,1)S(1)} %collective-permute-done.4.refs_0_), channel_id=1, source_target_pairs={{0,2},{1,3},{2,0},{3,1},{4,6},{5,7},{6,4},{7,5},{8,10},{9,11},{10,... | collective-permute-start | bytes 393224 | tf_op jit(solution)/shard_map/ppermute | solution.py:259
  17.0 9.7 %collective-permute-start.22 = (bf16[512,128]{1,0:T(8,128)(2,1)S(1)}, bf16[512,128]{1,0:T(8,128)(2,1)S(1)}, u32[]{:S(2)}, u32[]{:S(2)}) collective-permute-start(bf16[512,128]{1,0:T(8,128)(2,1)S(1)} %collective-permute-done.20.refs_16_), channel_id=1, source_target_pairs={{0,1},{1,0},{2,3},{3,2},{4,5},{5,4},{6,7},{7,6},{8,9},{9,8},{10,11... | collective-permute-start | bytes 393224 | tf_op jit(solution)/shard_map/ppermute | solution.py:259
  20.8 6.4 %collective-permute-start.6 = (bf16[512,128]{1,0:T(8,128)(2,1)S(1)}, bf16[512,128]{1,0:T(8,128)(2,1)S(1)}, u32[]{:S(2)}, u32[]{:S(2)}) collective-permute-start(bf16[512,128]{1,0:T(8,128)(2,1)S(1)} %collective-permute-done.4.refs_0_), channel_id=1, source_target_pairs={{0,1},{1,0},{2,3},{3,2},{4,5},{5,4},{6,7},{7,6},{8,9},{9,8},{10,11... | collective-permute-start | bytes 393224 | tf_op jit(solution)/shard_map/ppermute | solution.py:259
  20.8 7.9 %collective-permute-start.2 = (bf16[512,128]{1,0:T(8,128)(2,1)S(1)}, bf16[512,128]{1,0:T(8,128)(2,1)S(1)}, u32[]{:S(2)}, u32[]{:S(2)}) collective-permute-start(bf16[512,128]{1,0:T(8,128)(2,1)S(1)} %fusion.2), channel_id=1, source_target_pairs={{0,16},{4,20},{8,24},{12,28},{1,17},{5,21},{9,25},{13,29},{2,18},{... | collective-permute-start | bytes 393224 | tf_op jit(solution)/shard_map/ppermute | solution.py:274
  24.4 6.2 %collective-permute-start.12 = (bf16[512,128]{1,0:T(8,128)(2,1)S(1)}, bf16[512,128]{1,0:T(8,128)(2,1)S(1)}, u32[]{:S(2)}, u32[]{:S(2)}) collective-permute-start(bf16[512,128]{1,0:T(8,128)(2,1)S(1)} %collective-permute-done.8.refs_4_), channel_id=1, source_target_pairs={{0,8},{8,16},{16,24},{24,28},{28,20},{20,12},{12,4},{4,0},{1,9},{9... | collective-permute-start | bytes 393224 | tf_op jit(solution)/shard_map/ppermute | solution.py:283
  26.2 6.4 %collective-permute-start.9 = (bf16[512,128]{1,0:T(8,128)(2,1)S(1)}, bf16[512,128]{1,0:T(8,128)(2,1)S(1)}, u32[]{:S(2)}, u32[]{:S(2)}) collective-permute-start(bf16[512,128]{1,0:T(8,128)(2,1)S(1)} %collective-permute-done.8.refs_4_), channel_id=1, source_target_pairs={{0,2},{1,3},{2,0},{3,1},{4,6},{5,7},{6,4},{7,5},{8,10},{9,11},{10,... | collective-permute-start | bytes 393224 | tf_op jit(solution)/shard_map/ppermute | solution.py:259
  27.2 7.2 %collective-permute-start.25 = (bf16[512,128]{1,0:T(8,128)(2,1)S(1)}, bf16[512,128]{1,0:T(8,128)(2,1)S(1)}, u32[]{:S(2)}, u32[]{:S(2)}) collective-permute-start(bf16[512,128]{1,0:T(8,128)(2,1)S(1)} %collective-permute-done.24.refs_20_), channel_id=1, source_target_pairs={{0,2},{1,3},{2,0},{3,1},{4,6},{5,7},{6,4},{7,5},{8,10},{9,11},{10,... | collective-permute-start | bytes 393224 | tf_op jit(solution)/shard_map/ppermute | solution.py:259
  28.7 6.5 %collective-permute-start.10 = (bf16[512,128]{1,0:T(8,128)(2,1)S(1)}, bf16[512,128]{1,0:T(8,128)(2,1)S(1)}, u32[]{:S(2)}, u32[]{:S(2)}) collective-permute-start(bf16[512,128]{1,0:T(8,128)(2,1)S(1)} %collective-permute-done.8.refs_4_), channel_id=1, source_target_pairs={{0,1},{1,0},{2,3},{3,2},{4,5},{5,4},{6,7},{7,6},{8,9},{9,8},{10,11... | collective-permute-start | bytes 393224 | tf_op jit(solution)/shard_map/ppermute | solution.py:259
  30.7 6.1 %collective-permute-start.26 = (bf16[512,128]{1,0:T(8,128)(2,1)S(1)}, bf16[512,128]{1,0:T(8,128)(2,1)S(1)}, u32[]{:S(2)}, u32[]{:S(2)}) collective-permute-start(bf16[512,128]{1,0:T(8,128)(2,1)S(1)} %collective-permute-done.24.refs_20_), channel_id=1, source_target_pairs={{0,1},{1,0},{2,3},{3,2},{4,5},{5,4},{6,7},{7,6},{8,9},{9,8},{10,11... | collective-permute-start | bytes 393224 | tf_op jit(solution)/shard_map/ppermute | solution.py:259
  32.6 6.3 %collective-permute-start.7 = (bf16[512,128]{1,0:T(8,128)(2,1)S(1)}, bf16[512,128]{1,0:T(8,128)(2,1)S(1)}, u32[]{:S(2)}, u32[]{:S(2)}) collective-permute-start(bf16[512,128]{1,0:T(8,128)(2,1)S(1)} %collective-permute-done.5.refs_1_), channel_id=1, source_target_pairs={{0,1},{1,0},{2,3},{3,2},{4,5},{5,4},{6,7},{7,6},{8,9},{9,8},{10,11... | collective-permute-start | bytes 393224 | tf_op jit(solution)/shard_map/ppermute | solution.py:259
  35.1 6.6 %collective-permute-start.16 = (bf16[512,128]{1,0:T(8,128)(2,1)S(1)}, bf16[512,128]{1,0:T(8,128)(2,1)S(1)}, u32[]{:S(2)}, u32[]{:S(2)}) collective-permute-start(bf16[512,128]{1,0:T(8,128)(2,1)S(1)} %collective-permute-done.12.refs_8_), channel_id=1, source_target_pairs={{0,8},{8,16},{16,24},{24,28},{28,20},{20,12},{12,4},{4,0},{1,9},{9... | collective-permute-start | bytes 393224 | tf_op jit(solution)/shard_map/ppermute | solution.py:283
  36.8 6.0 %collective-permute-start.13 = (bf16[512,128]{1,0:T(8,128)(2,1)S(1)}, bf16[512,128]{1,0:T(8,128)(2,1)S(1)}, u32[]{:S(2)}, u32[]{:S(2)}) collective-permute-start(bf16[512,128]{1,0:T(8,128)(2,1)S(1)} %collective-permute-done.12.refs_8_), channel_id=1, source_target_pairs={{0,2},{1,3},{2,0},{3,1},{4,6},{5,7},{6,4},{7,5},{8,10},{9,11},{10,... | collective-permute-start | bytes 393224 | tf_op jit(solution)/shard_map/ppermute | solution.py:259
  37.3 6.9 %collective-permute-start.29 = (bf16[512,128]{1,0:T(8,128)(2,1)S(1)}, bf16[512,128]{1,0:T(8,128)(2,1)S(1)}, u32[]{:S(2)}, u32[]{:S(2)}) collective-permute-start(bf16[512,128]{1,0:T(8,128)(2,1)S(1)} %collective-permute-done.28.refs_24_), channel_id=1, source_target_pairs={{0,2},{1,3},{2,0},{3,1},{4,6},{5,7},{6,4},{7,5},{8,10},{9,11},{10,... | collective-permute-start | bytes 393224 | tf_op jit(solution)/shard_map/ppermute | solution.py:259
  44.2 6.3 %collective-permute-start.27 = (bf16[512,128]{1,0:T(8,128)(2,1)S(1)}, bf16[512,128]{1,0:T(8,128)(2,1)S(1)}, u32[]{:S(2)}, u32[]{:S(2)}) collective-permute-start(bf16[512,128]{1,0:T(8,128)(2,1)S(1)} %collective-permute-done.25.refs_21_), channel_id=1, source_target_pairs={{0,1},{1,0},{2,3},{3,2},{4,5},{5,4},{6,7},{7,6},{8,9},{9,8},{10,11... | collective-permute-start | bytes 393224 | tf_op jit(solution)/shard_map/ppermute | solution.py:259
  44.2 6.3 %collective-permute-start.18 = (bf16[512,128]{1,0:T(8,128)(2,1)S(1)}, bf16[512,128]{1,0:T(8,128)(2,1)S(1)}, u32[]{:S(2)}, u32[]{:S(2)}) collective-permute-start(bf16[512,128]{1,0:T(8,128)(2,1)S(1)} %collective-permute-done.16.refs_12_), channel_id=1, source_target_pairs={{0,1},{1,0},{2,3},{3,2},{4,5},{5,4},{6,7},{7,6},{8,9},{9,8},{10,11... | collective-permute-start | bytes 393224 | tf_op jit(solution)/shard_map/ppermute | solution.py:259
  52.2 15.4 %collective-permute-start.33 = (bf16[128,1024]{1,0:T(8,128)(2,1)S(1)}, bf16[128,1024]{1,0:T(8,128)(2,1)S(1)}, u32[]{:S(2)}, u32[]{:S(2)}) collective-permute-start(bf16[128,1024]{1,0:T(8,128)(2,1)S(1)} %get-tuple-element.28), channel_id=1, source_target_pairs={{0,16},{4,20},{8,24},{12,28},{16,0},{20,4},{24,8},{28,12},{1,17},{... | collective-permute-start | bytes 786440 | tf_op jit(solution)/shard_map/ppermute | solution.py:237
  54.0 13.5 %collective-permute-start.32 = (f32[4,128]{1,0:T(4,128)S(1)}, f32[4,128]{1,0:T(4,128)S(1)}, u32[]{:S(2)}, u32[]{:S(2)}) collective-permute-start(f32[4,128]{1,0:T(4,128)S(1)} %maximum_bitcast_fusion.meta_ref), channel_id=1, source_target_pairs={{0,16},{4,20},{8,24},{12,28},{16,0},{20,4},{24,8},{28,12},{1,17},{... | collective-permute-start | bytes 6152 | tf_op jit(solution)/shard_map/ppermute | solution.py:237
  68.8 6.4 %collective-permute-start.35 = (bf16[64,1024]{1,0:T(8,128)(2,1)S(1)}, bf16[64,1024]{1,0:T(8,128)(2,1)S(1)}, u32[]{:S(2)}, u32[]{:S(2)}) collective-permute-start(bf16[64,1024]{1,0:T(8,128)(2,1)S(1)} %get-tuple-element.31), channel_id=1, source_target_pairs={{0,8},{4,12},{8,0},{12,4},{16,24},{20,28},{24,16},{28,20},{1,9},{5... | collective-permute-start | bytes 393224 | tf_op jit(solution)/shard_map/ppermute | solution.py:237
  69.5 7.6 %collective-permute-start.36 = (bf16[64,1024]{1,0:T(8,128)(2,1)S(1)}, bf16[64,1024]{1,0:T(8,128)(2,1)S(1)}, u32[]{:S(2)}, u32[]{:S(2)}) collective-permute-start(bf16[64,1024]{1,0:T(8,128)(2,1)S(1)} %get-tuple-element.32), channel_id=1, source_target_pairs={{0,12},{4,8},{8,4},{12,0},{16,28},{20,24},{24,20},{28,16},{1,13},{... | collective-permute-start | bytes 393224 | tf_op jit(solution)/shard_map/ppermute | solution.py:237
  78.3 7.7 %collective-permute-start.37 = (bf16[64,1024]{1,0:T(8,128)(2,1)S(1)}, bf16[64,1024]{1,0:T(8,128)(2,1)S(1)}, u32[]{:S(2)}, u32[]{:S(2)}) collective-permute-start(bf16[64,1024]{1,0:T(8,128)(2,1)S(1)} %get-tuple-element.34), channel_id=1, source_target_pairs={{0,4},{4,0},{8,12},{12,8},{16,20},{20,16},{24,28},{28,24},{1,5},{5... | collective-permute-start | bytes 393224 | tf_op jit(solution)/shard_map/ppermute | solution.py:237
  79.4 7.5 %collective-permute-start.38 = (bf16[64,1024]{1,0:T(8,128)(2,1)S(1)}, bf16[64,1024]{1,0:T(8,128)(2,1)S(1)}, u32[]{:S(2)}, u32[]{:S(2)}) collective-permute-start(bf16[64,1024]{1,0:T(8,128)(2,1)S(1)} %get-tuple-element.35), channel_id=1, source_target_pairs={{0,8},{4,12},{8,0},{12,4},{16,24},{20,28},{24,16},{28,20},{1,9},{5... | collective-permute-start | bytes 393224 | tf_op jit(solution)/shard_map/ppermute | solution.py:237
  80.2 8.8 %collective-permute-start.39 = (bf16[64,1024]{1,0:T(8,128)(2,1)S(1)}, bf16[64,1024]{1,0:T(8,128)(2,1)S(1)}, u32[]{:S(2)}, u32[]{:S(2)}) collective-permute-start(bf16[64,1024]{1,0:T(8,128)(2,1)S(1)} %get-tuple-element.36), channel_id=1, source_target_pairs={{0,12},{4,8},{8,4},{12,0},{16,28},{20,24},{24,20},{28,16},{1,13},{... | collective-permute-start | bytes 393224 | tf_op jit(solution)/shard_map/ppermute | solution.py:237
  81.8 9.6 %collective-permute-start.41 = (bf16[64,1024]{1,0:T(8,128)(2,1)S(1)}, bf16[64,1024]{1,0:T(8,128)(2,1)S(1)}, u32[]{:S(2)}, u32[]{:S(2)}) collective-permute-start(bf16[64,1024]{1,0:T(8,128)(2,1)S(1)} %get-tuple-element.38), channel_id=1, source_target_pairs={{0,4},{4,0},{8,12},{12,8},{16,20},{20,16},{24,28},{28,24},{1,5},{5... | collective-permute-start | bytes 393224 | tf_op jit(solution)/shard_map/ppermute | solution.py:237
  82.8 10.3 %collective-permute-start.42 = (bf16[64,1024]{1,0:T(8,128)(2,1)S(1)}, bf16[64,1024]{1,0:T(8,128)(2,1)S(1)}, u32[]{:S(2)}, u32[]{:S(2)}) collective-permute-start(bf16[64,1024]{1,0:T(8,128)(2,1)S(1)} %get-tuple-element.39), channel_id=1, source_target_pairs={{0,8},{4,12},{8,0},{12,4},{16,24},{20,28},{24,16},{28,20},{1,9},{5... | collective-permute-start | bytes 393224 | tf_op jit(solution)/shard_map/ppermute | solution.py:237
  86.0 9.1 %collective-permute-start.43 = (bf16[64,1024]{1,0:T(8,128)(2,1)S(1)}, bf16[64,1024]{1,0:T(8,128)(2,1)S(1)}, u32[]{:S(2)}, u32[]{:S(2)}) collective-permute-start(bf16[64,1024]{1,0:T(8,128)(2,1)S(1)} %get-tuple-element.40), channel_id=1, source_target_pairs={{0,12},{4,8},{8,4},{12,0},{16,28},{20,24},{24,20},{28,16},{1,13},{... | collective-permute-start | bytes 393224 | tf_op jit(solution)/shard_map/ppermute | solution.py:237
  89.6 15.3 %collective-permute-start.40 = (bf16[128,1024]{1,0:T(8,128)(2,1)S(1)}, bf16[128,1024]{1,0:T(8,128)(2,1)S(1)}, u32[]{:S(2)}, u32[]{:S(2)}) collective-permute-start(bf16[128,1024]{1,0:T(8,128)(2,1)S(1)} %shard_map.97), channel_id=1, source_target_pairs={{0,16},{4,20},{8,24},{12,28},{16,0},{20,4},{24,8},{28,12},{1,17},{... | collective-permute-start | bytes 786440 | tf_op jit(solution)/shard_map/ppermute | solution.py:237
  97.8 7.1 %collective-permute-start.46 = (bf16[64,1024]{1,0:T(8,128)(2,1)S(1)}, bf16[64,1024]{1,0:T(8,128)(2,1)S(1)}, u32[]{:S(2)}, u32[]{:S(2)}) collective-permute-start(bf16[64,1024]{1,0:T(8,128)(2,1)S(1)} %get-tuple-element.44), channel_id=1, source_target_pairs={{0,12},{4,8},{8,4},{12,0},{16,28},{20,24},{24,20},{28,16},{1,13},{... | collective-permute-start | bytes 393224 | tf_op jit(solution)/shard_map/ppermute | solution.py:237
  (26 other events, 331.9 us)

commit v3 on v2

--- a/solution.py
+++ b/solution.py
@@ -21,16 +21,17 @@
 VMEM = pl.BlockSpec(memory_space=pltpu.VMEM)
 
 
-def call(body, outs, n_in, scratch=()):
+def call(body, outs, xs, scratch=(), in_hbm=()):
     run = pl.pallas_call(
         body,
         out_shape=outs,
-        in_specs=[VMEM] * n_in,
+        in_specs=[pl.BlockSpec(memory_space=pl.ANY) if i in in_hbm else VMEM for i in range(len(xs))],
         out_specs=jax.tree.map(lambda _: VMEM, outs),
         scratch_shapes=scratch,
         compiler_params=pltpu.CompilerParams(vmem_limit_bytes=KERNEL_VMEM),
     )
-    return lambda *xs: run(*[pltpu.with_memory_space_constraint(x, pltpu.VMEM) for x in xs])
+    spaces = [pltpu.HBM if i in in_hbm else pltpu.VMEM for i in range(len(xs))]
+    return run(*[pltpu.with_memory_space_constraint(x, m) for x, m in zip(xs, spaces)])
 
 
 def sds(shape, dtype):
@@ -41,7 +42,13 @@
     return lax.dot_general(a, b, (dims, ((), ())), preferred_element_type=F32)
 
 
-def states_body(k_ref, v_ref, mine_ref, send_ref, full):
+def states_body(k_ref, v_ref, ids_ref, gates_ref, w_ref, mine_ref, send_ref, meta_ref, piece_ref, full, sem):
+    rows = piece_ref.shape[0]
+    start = pl.multiple_of(lax.axis_index("win") * rows, rows)
+    copy = pltpu.make_async_copy(w_ref.at[pl.ds(start, rows), :], piece_ref, sem)
+    copy.start()
+    meta_ref[0:TOP, :] = ids_ref[...].astype(F32)
+    meta_ref[TOP : 2 * TOP, :] = gates_ref[...]
     half = full.shape[0] // 2
     for p in range(H // 2):
         r = dot(k_ref[:, 2 * DK * p : 2 * DK * (p + 1)], v_ref[:, 2 * DV * p : 2 * DV * (p + 1)], ((0,), (0,)))
@@ -50,6 +57,33 @@
     y = lax.rem(lax.axis_index("seq"), 2)
     mine_ref[...] = full[pl.ds(pl.multiple_of(y * half, half), half), :]
     send_ref[...] = full[pl.ds(pl.multiple_of((1 - y) * half, half), half), :].astype(BF)
+    copy.wait()
+
+
+def running_body(mine_ref, *refs):
+    total = mine_ref[...]
+    for r in refs[:-1]:
+        total = total + r[...].astype(F32)
+    refs[-1][...] = total.astype(BF)
+
+
+def prefix_body(mine_ref, got_ref, *refs):
+    came, own_ref, back_ref = refs[:-2], refs[-2], refs[-1]
+    before = came[0][...].astype(F32)
+    for r in came[1:]:
+        before = before + r[...].astype(F32)
+    even = lax.rem(lax.axis_index("seq"), 2) == 0
+    got = got_ref[...].astype(F32)
+    own_ref[...] = (before + jnp.where(even, jnp.zeros_like(got), got)).astype(BF)
+    mine = mine_ref[...]
+    back_ref[...] = (before + jnp.where(even, mine, jnp.zeros_like(mine))).astype(BF)
+
+
+def pack_body(*refs):
+    at = 0
+    for r in refs[:-1]:
+        refs[-1][at : at + r.shape[0], :] = r[...]
+        at += r.shape[0]
 
 
 def intra_body(first, q_ref, k_ref, v_ref, out_ref):
@@ -97,13 +131,10 @@
         out[...] = rows[k * cap : (k + 1) * cap, :]
 
 
-def project_body(n, offsets, q_ref, ia_ref, ib_ref, pm_ref, po_ref, wown_ref, res_ref, meta_ref, *refs):
-    fwd, bwd = n // 2, n // 2 - 1
+def project_body(n, offsets, groups, q_ref, ia_ref, ib_ref, pm_ref, po_ref, wown_ref, res_ref, meta_ref, *refs):
     copies = len(offsets)
-    fs = [refs[j * copies : (j + 1) * copies] for j in range(fwd)]
-    refs = refs[fwd * copies :]
-    bs = [refs[j * copies : (j + 1) * copies] for j in range(bwd)]
-    refs = refs[bwd * copies :]
+    packs = [refs[g * copies : (g + 1) * copies] for g in range(len(groups))]
+    refs = refs[len(groups) * copies :]
     hidden_ref, normed_ref = refs[:2]
     outs = refs[2 : 2 + n // 2]
     prefix, att, hid, key_ref = refs[2 + n // 2 :]
@@ -140,18 +171,16 @@
         hid[:, pl.ds(pl.multiple_of(source(shift) * width, width), width)] = value
 
     put(0, dot(att[...], wown_ref[...]))
-    for j in range(fwd):
-        both = j < bwd
-        total = None
-        for i, part in enumerate(parts):
-            m = fs[j][i][...]
-            if both:
-                m = jnp.concatenate([m, bs[j][i][...]], axis=1)
-            r = dot(part, m)
-            total = r if total is None else total + r
-        put(-(j + 1), total[:, :width])
-        if both:
-            put(j + 1, total[:, width:])
+    for shifts, held in zip(groups, packs):
+        for i in range(0, len(shifts), 2):
+            some = shifts[i : i + 2]
+            total = None
+            for part, pack in zip(parts, held):
+                m = [pack[(i + o) * rows : (i + o + 1) * rows, :] for o in range(len(some))]
+                r = dot(part, jnp.concatenate(m, axis=1) if len(m) > 1 else m[0])
+                total = r if total is None else total + r
+            for o, shift in enumerate(some):
+                put(shift, total[:, o * width : (o + 1) * width])
     hidden = (res_ref[...].astype(F32) + hid[...]).astype(BF)
     hidden_ref[...] = hidden
     h = hidden.astype(F32)
@@ -236,15 +265,14 @@
     def flip(x, k):
         return lax.ppermute(x, "seq", [(i, i ^ k) for i in range(n)])
 
-    def kernel(body, outs, xs, scratch=()):
-        return call(body, outs, len(xs), scratch)(*xs)
+    def kernel(body, outs, xs, scratch=(), in_hbm=()):
+        return call(body, outs, xs, scratch, in_hbm)
 
     def flips(xs):
         return [xs[0]] + [flip(xs[k], k) for k in range(1, near)]
 
     offsets = [0]
     rows = H * DV // copies
-    piece = lax.dynamic_slice_in_dim(out_weight, lax.axis_index("win") * rows, rows, 0)
     spread = []
     bit = copies // 2
     while bit:
@@ -259,35 +287,48 @@
             held = held + [lax.ppermute(h, "win", pairs) for h in held]
         return held
 
-    mine, sent = kernel(
+    width = out_weight.shape[1]
+    mine, sent, meta, piece = kernel(
         states_body,
-        (sds((half, DV), F32), sds((half, DV), BF)),
-        (key_rows, value_rows),
-        [pltpu.VMEM((2 * half, DV), F32)],
-    )
-    got = flip(sent, 1).astype(F32)
-    run = mine + got
-    before = jnp.zeros_like(mine)
+        (sds((half, DV), F32), sds((half, DV), BF), sds((2 * TOP, length), F32), sds((rows, width), BF)),
+        (key_rows, value_rows, expert_ids.T, gate_values.T, out_weight),
+        [pltpu.VMEM((2 * half, DV), F32), pltpu.SemaphoreType.DMA],
+        in_hbm=(4,),
+    )
+    meta_far = flip(meta, near)
+    state = sds((half, DV), BF)
+    got = flip(sent, 1)
+    came = []
     step = 1
     while step < n // 2:
         hop = [(i, i + 2 * step) for i in range(n - 2 * step)]
-        came = lax.ppermute(run.astype(BF), "seq", hop).astype(F32)
-        before, run = before + came, run + came
+        run = kernel(running_body, state, (mine, got, *came))
+        came.append(lax.ppermute(run, "seq", hop))
         step *= 2
-    prefix_mine = (before + jnp.where(y == 0, 0.0, got)).astype(BF)
-    prefix_other = flip((before + jnp.where(y == 0, mine, 0.0)).astype(BF), 1)
+    prefix_mine, prefix_back = kernel(prefix_body, (state, state), (mine, got, *came))
+    prefix_other = flip(prefix_back, 1)
 
     fs, bs = [], []
     f = b = piece
     for j in range(near):
         f = lax.ppermute(f, "seq", ahead)
-        fs += share(f)
+        fs.append(f)
         if j < near - 1:
             b = lax.ppermute(b, "seq", back)
-            bs += share(b)
-
-    meta = jnp.concatenate([expert_ids.astype(F32), gate_values], axis=1).T
-    meta_far = flip(meta, near)
+            bs.append(b)
+    steps = [[j] for j in range(near - 2)] + [[near - 2, near - 1]]
+    groups, packs = [], []
+    for js in steps:
+        shifts, xs = [], []
+        for j in js:
+            shifts.append(-(j + 1))
+            xs.append(fs[j])
+            if j < near - 1:
+                shifts.append(j + 1)
+                xs.append(bs[j])
+        groups.append(shifts)
+        pack = kernel(pack_body, sds((rows * len(xs), width), BF), xs)
+        packs += share(pack)
 
     tokens = (queries, key_rows, value_rows)
     intra = [
@@ -298,9 +339,9 @@
     full = sds((length, D), BF)
     keys = pltpu.VMEM((n, length), F32)
     hidden, normed, *deal_own = kernel(
-        functools.partial(project_body, n, offsets),
+        functools.partial(project_body, n, offsets, groups),
         (full, full, *[row_buf] * near),
-        (queries, *intra, prefix_mine, prefix_other, out_weight, residual, meta, *fs, *bs),
+        (queries, *intra, prefix_mine, prefix_other, out_weight, residual, meta, *packs),
         [
             pltpu.VMEM((2 * half, DV), BF),
             pltpu.VMEM((length, H * DV), BF),

time: 106 us -> 110 us (1.038)
  starting transfers between devices: 44.7 us -> 46.2 us
    ppermute x21 -> x9, waiting for transfers between devices: 7.04 us -> 1.19 us  [share(): held = held + [lax.ppermute(h, 'win', pairs) for h in held]]
    ppermute x4, waiting for transfers between devices: 7.05 us -> 12.7 us  [small_group(): f = lax.ppermute(f, 'seq', ahead)]
    ppermute x2, starting transfers between devices: 6.95 us -> 10.3 us  [small_group(): came.append(lax.ppermute(run, 'seq', hop))]
    ppermute x4, starting transfers between devices: 5.78 us -> 8.73 us  [small_group(): f = lax.ppermute(f, 'seq', ahead)]
    ppermute x3, starting transfers between devices: 2.19 us -> 0.47 us  [small_group(): b = lax.ppermute(b, 'seq', back)]
    ppermute x17, starting transfers between devices: 22.1 us -> 20.6 us  [flip(): return lax.ppermute(x, 'seq', [(i, i ^ k) for i in range(n)])]
    ppermute x21 -> x9, starting transfers between devices: 7.66 us -> 6.16 us  [share(): held = held + [lax.ppermute(h, 'win', pairs) for h in held]]
    ppermute x2, waiting for transfers between devices: 0.01 us -> 1.37 us  [small_group(): came.append(lax.ppermute(run, 'seq', hop))]
  transfers between devices with their start and end apart: 47 -> 35, of which waited for: 23 -> 19; matrix products, arithmetic and copies ran while one was open for 1% -> 0% of each run, Pallas kernels for 4% -> 4%
where the time goes in v3:
time: 110 us
  waiting for transfers between devices  49.8 us (45%)
  starting transfers between devices  46.2 us (42%)
  Pallas kernels  9.98 us (9%)
  local copies, waits for them, and re-layouts  3.39 us (3%)
    ppermute x17, waiting for transfers between devices, flip(): return lax.ppermute(x, 'seq', [(i, i ^ k) for i in range(n)])  34.5 us
    ppermute x17, starting transfers between devices, flip(): return lax.ppermute(x, 'seq', [(i, i ^ k) for i in range(n)])  20.6 us
    ppermute x4, waiting for transfers between devices, small_group(): f = lax.ppermute(f, 'seq', ahead)  12.7 us
    ppermute x2, starting transfers between devices, small_group(): came.append(lax.ppermute(run, 'seq', hop))  10.3 us
    pallas_call x15, Pallas kernels, call(): run(*[pltpu.with_memory_space_constraint(x, m) for x, m in zip(xs, spaces)])  9.98 us
    ppermute x4, starting transfers between devices, small_group(): f = lax.ppermute(f, 'seq', ahead)  8.73 us
    ppermute x9, starting transfers between devices, share(): held = held + [lax.ppermute(h, 'win', pairs) for h in held]  6.16 us
    unnamed x22, local copies, waits for them, and re-layouts  3.39 us
  transfers between devices with their start and end apart: 35, of which 19 were waited for; matrix products, arithmetic and copies ran while one was open for 0% of the time, Pallas kernels for 4%

profile of v3, /device:TPU:0, one launch (start us, length us, event | category | flops | bytes accessed | tf_op | source)
XLA Modules:
  0.0 109.7 jit_solution(657332723663430223)
XLA Ops:
  4.4 3.1 %collective-permute-start.4 = (bf16[512,128]{1,0:T(8,128)(2,1)S(1)}, bf16[512,128]{1,0:T(8,128)(2,1)S(1)}, u32[]{:S(2)}, u32[]{:S(2)}) collective-permute-start(bf16[512,128]{1,0:T(8,128)(2,1)S(1)} %get-tuple-element.34), channel_id=1, source_target_pairs={{0,8},{8,16},{16,24},{24,28},{28,20},{20,12},{12,4},{4,0},{1,9},{9... | collective-permute-start | bytes 393224 | tf_op jit(solution)/shard_map/ppermute | solution.py:314
  7.5 3.4 %collective-permute-done.4.refs_0_ = bf16[512,128]{1,0:T(8,128)(2,1)S(1)} collective-permute-done((bf16[512,128]{1,0:T(8,128)(2,1)S(1)}, bf16[512,128]{1,0:T(8,128)(2,1)S(1)}, u32[]{:S(2)}, u32[]{:S(2)}) %collective-permute-start.4) | collective-permute-done | bytes 131104 | tf_op jit(solution)/shard_map/ppermute | solution.py:314
  11.0 1.8 %collective-permute-start.9 = (bf16[512,128]{1,0:T(8,128)(2,1)S(1)}, bf16[512,128]{1,0:T(8,128)(2,1)S(1)}, u32[]{:S(2)}, u32[]{:S(2)}) collective-permute-start(bf16[512,128]{1,0:T(8,128)(2,1)S(1)} %collective-permute-done.4.refs_0_), channel_id=1, source_target_pairs={{0,8},{8,16},{16,24},{24,28},{28,20},{20,12},{12,4},{4,0},{1,9},{9... | collective-permute-start | bytes 393224 | tf_op jit(solution)/shard_map/ppermute | solution.py:314
  13.0 2.9 %collective-permute-done.9.refs_0_ = bf16[512,128]{1,0:T(8,128)(2,1)S(1)} collective-permute-done((bf16[512,128]{1,0:T(8,128)(2,1)S(1)}, bf16[512,128]{1,0:T(8,128)(2,1)S(1)}, u32[]{:S(2)}, u32[]{:S(2)}) %collective-permute-start.9) | collective-permute-done | bytes 131104 | tf_op jit(solution)/shard_map/ppermute | solution.py:314
  15.9 1.8 %collective-permute-start.14 = (bf16[512,128]{1,0:T(8,128)(2,1)S(1)}, bf16[512,128]{1,0:T(8,128)(2,1)S(1)}, u32[]{:S(2)}, u32[]{:S(2)}) collective-permute-start(bf16[512,128]{1,0:T(8,128)(2,1)S(1)} %collective-permute-done.9.refs_0_), channel_id=1, source_target_pairs={{0,8},{8,16},{16,24},{24,28},{28,20},{20,12},{12,4},{4,0},{1,9},{9... | collective-permute-start | bytes 393224 | tf_op jit(solution)/shard_map/ppermute | solution.py:314
  18.0 3.4 %collective-permute-done.14.refs_0_ = bf16[512,128]{1,0:T(8,128)(2,1)S(1)} collective-permute-done((bf16[512,128]{1,0:T(8,128)(2,1)S(1)}, bf16[512,128]{1,0:T(8,128)(2,1)S(1)}, u32[]{:S(2)}, u32[]{:S(2)}) %collective-permute-start.14) | collective-permute-done | bytes 131104 | tf_op jit(solution)/shard_map/ppermute | solution.py:314
  21.3 2.0 %collective-permute-start.16 = (bf16[512,128]{1,0:T(8,128)(2,1)S(1)}, bf16[512,128]{1,0:T(8,128)(2,1)S(1)}, u32[]{:S(2)}, u32[]{:S(2)}) collective-permute-start(bf16[512,128]{1,0:T(8,128)(2,1)S(1)} %collective-permute-done.14.refs_0_), channel_id=1, source_target_pairs={{0,8},{8,16},{16,24},{24,28},{28,20},{20,12},{12,4},{4,0},{1,9},{9... | collective-permute-start | bytes 393224 | tf_op jit(solution)/shard_map/ppermute | solution.py:314
  23.4 2.9 %collective-permute-done.16.refs_2_ = bf16[512,128]{1,0:T(8,128)(2,1)S(1)} collective-permute-done((bf16[512,128]{1,0:T(8,128)(2,1)S(1)}, bf16[512,128]{1,0:T(8,128)(2,1)S(1)}, u32[]{:S(2)}, u32[]{:S(2)}) %collective-permute-start.16) | collective-permute-done | bytes 131104 | tf_op jit(solution)/shard_map/ppermute | solution.py:314
  26.4 2.0 %collective-permute-start.17 = (bf16[1536,128]{1,0:T(8,128)(2,1)S(1)}, bf16[1536,128]{1,0:T(8,128)(2,1)S(1)}, u32[]{:S(2)}, u32[]{:S(2)}) collective-permute-start(bf16[1536,128]{1,0:T(8,128)(2,1)S(1)} %shard_map.99.refs_8_), channel_id=1, source_target_pairs={{0,2},{1,3},{2,0},{3,1},{4,6},{5,7},{6,4},{7,5},{8,10},{9,11},{10,... | collective-permute-start | bytes 1179656 | tf_op jit(solution)/shard_map/ppermute | solution.py:287
  28.4 3.5 %collective-permute-start.1 = (bf16[512,128]{1,0:T(8,128)(2,1)S(1)}, bf16[512,128]{1,0:T(8,128)(2,1)S(1)}, u32[]{:S(2)}, u32[]{:S(2)}) collective-permute-start(bf16[512,128]{1,0:T(8,128)(2,1)S(1)} %shard_map.94), channel_id=1, source_target_pairs={{0,8},{4,12},{8,16},{12,20},{16,24},{20,28},{1,9},{5,13},{9,17},{1... | collective-permute-start | bytes 393224 | tf_op jit(solution)/shard_map/ppermute | solution.py:306
  31.9 1.5 %collective-permute-start.6 = (bf16[1024,128]{1,0:T(8,128)(2,1)S(1)}, bf16[1024,128]{1,0:T(8,128)(2,1)S(1)}, u32[]{:S(2)}, u32[]{:S(2)}) collective-permute-start(bf16[1024,128]{1,0:T(8,128)(2,1)S(1)} %shard_map.97.refs_0_), channel_id=1, source_target_pairs={{0,2},{1,3},{2,0},{3,1},{4,6},{5,7},{6,4},{7,5},{8,10},{9,11},{10,... | collective-permute-start | bytes 786440 | tf_op jit(solution)/shard_map/ppermute | solution.py:287
  34.5 6.8 %collective-permute-start.2 = (bf16[512,128]{1,0:T(8,128)(2,1)S(1)}, bf16[512,128]{1,0:T(8,128)(2,1)S(1)}, u32[]{:S(2)}, u32[]{:S(2)}) collective-permute-start(bf16[512,128]{1,0:T(8,128)(2,1)S(1)} %shard_map.95), channel_id=1, source_target_pairs={{0,16},{4,20},{8,24},{12,28},{1,17},{5,21},{9,25},{13,29},{2,18},{... | collective-permute-start | bytes 393224 | tf_op jit(solution)/shard_map/ppermute | solution.py:306
  41.4 2.0 %collective-permute-start.11 = (bf16[1024,128]{1,0:T(8,128)(2,1)S(1)}, bf16[1024,128]{1,0:T(8,128)(2,1)S(1)}, u32[]{:S(2)}, u32[]{:S(2)}) collective-permute-start(bf16[1024,128]{1,0:T(8,128)(2,1)S(1)} %shard_map.98.refs_4_), channel_id=1, source_target_pairs={{0,2},{1,3},{2,0},{3,1},{4,6},{5,7},{6,4},{7,5},{8,10},{9,11},{10,... | collective-permute-start | bytes 786440 | tf_op jit(solution)/shard_map/ppermute | solution.py:287
  43.9 2.0 %collective-permute-start.3 = (bf16[512,128]{1,0:T(8,128)(2,1)S(1)}, bf16[512,128]{1,0:T(8,128)(2,1)S(1)}, u32[]{:S(2)}, u32[]{:S(2)}) collective-permute-start(bf16[512,128]{1,0:T(8,128)(2,1)S(1)} %get-tuple-element.33), channel_id=1, source_target_pairs={{0,4},{4,0},{8,12},{12,8},{16,20},{20,16},{24,28},{28,24},{1,5},{5... | collective-permute-start | bytes 393224 | tf_op jit(solution)/shard_map/ppermute | solution.py:266
  46.4 2.7 %collective-permute-done.3.po_ref = bf16[512,128]{1,0:T(8,128)(2,1)S(1)} collective-permute-done((bf16[512,128]{1,0:T(8,128)(2,1)S(1)}, bf16[512,128]{1,0:T(8,128)(2,1)S(1)}, u32[]{:S(2)}, u32[]{:S(2)}) %collective-permute-start.3) | collective-permute-done | bytes 131104 | tf_op jit(solution)/shard_map/ppermute | solution.py:266
  53.1 1.5 %shard_map.100 = (bf16[128,1024]{1,0:T(8,128)(2,1)S(1)}, bf16[128,1024]{1,0:T(8,128)(2,1)S(1)}, bf16[64,1024]{1,0:T(8,128)(2,1)S(1)}, bf16[64,1024]{1,0:T(8,128)...) custom-call(bf16[128,1024]{1,0:T(8,128)(2,1)S(1)} %copy-done.6, f32[128,1024]{1,0:T(8,128)S(1)} %shard_map.92.ia_ref, ...), custom_call_target="tpu_custom_call" | custom-call | tf_op jit(solution)/shard_map/pallas_call | solution.py:34
  54.7 2.6 %collective-permute-start.21 = (bf16[128,1024]{1,0:T(8,128)(2,1)S(1)}, bf16[128,1024]{1,0:T(8,128)(2,1)S(1)}, u32[]{:S(2)}, u32[]{:S(2)}) collective-permute-start(bf16[128,1024]{1,0:T(8,128)(2,1)S(1)} %get-tuple-element.36), channel_id=1, source_target_pairs={{0,16},{4,20},{8,24},{12,28},{16,0},{20,4},{24,8},{28,12},{1,17},{... | collective-permute-start | bytes 786440 | tf_op jit(solution)/shard_map/ppermute | solution.py:266
  57.7 12.4 %collective-permute-done.20.meta_ref = f32[4,128]{1,0:T(4,128)S(1)} collective-permute-done((f32[4,128]{1,0:T(4,128)S(1)}, f32[4,128]{1,0:T(4,128)S(1)}, u32[]{:S(2)}, u32[]{:S(2)}) %collective-permute-start.20) | collective-permute-done | bytes 2080 | tf_op jit(solution)/shard_map/ppermute | solution.py:266
  71.6 2.4 %collective-permute-start.24 = (bf16[64,1024]{1,0:T(8,128)(2,1)S(1)}, bf16[64,1024]{1,0:T(8,128)(2,1)S(1)}, u32[]{:S(2)}, u32[]{:S(2)}) collective-permute-start(bf16[64,1024]{1,0:T(8,128)(2,1)S(1)} %get-tuple-element.40), channel_id=1, source_target_pairs={{0,12},{4,8},{8,4},{12,0},{16,28},{20,24},{24,20},{28,16},{1,13},{... | collective-permute-start | bytes 393224 | tf_op jit(solution)/shard_map/ppermute | solution.py:266
  74.0 2.0 %collective-permute-done.22.refs_1_ = bf16[64,1024]{1,0:T(8,128)(2,1)S(1)} collective-permute-done((bf16[64,1024]{1,0:T(8,128)(2,1)S(1)}, bf16[64,1024]{1,0:T(8,128)(2,1)S(1)}, u32[]{:S(2)}, u32[]{:S(2)}) %collective-permute-start.22) | collective-permute-done | bytes 131104 | tf_op jit(solution)/shard_map/ppermute | solution.py:266
  76.0 2.0 %collective-permute-done.23.refs_2_ = bf16[64,1024]{1,0:T(8,128)(2,1)S(1)} collective-permute-done((bf16[64,1024]{1,0:T(8,128)(2,1)S(1)}, bf16[64,1024]{1,0:T(8,128)(2,1)S(1)}, u32[]{:S(2)}, u32[]{:S(2)}) %collective-permute-start.23) | collective-permute-done | bytes 131104 | tf_op jit(solution)/shard_map/ppermute | solution.py:266
  78.0 1.6 %collective-permute-done.24.refs_3_ = bf16[64,1024]{1,0:T(8,128)(2,1)S(1)} collective-permute-done((bf16[64,1024]{1,0:T(8,128)(2,1)S(1)}, bf16[64,1024]{1,0:T(8,128)(2,1)S(1)}, u32[]{:S(2)}, u32[]{:S(2)}) %collective-permute-start.24) | collective-permute-done | bytes 131104 | tf_op jit(solution)/shard_map/ppermute | solution.py:266
  80.8 1.6 %collective-permute-start.25 = (bf16[64,1024]{1,0:T(8,128)(2,1)S(1)}, bf16[64,1024]{1,0:T(8,128)(2,1)S(1)}, u32[]{:S(2)}, u32[]{:S(2)}) collective-permute-start(bf16[64,1024]{1,0:T(8,128)(2,1)S(1)} %get-tuple-element.42), channel_id=1, source_target_pairs={{0,4},{4,0},{8,12},{12,8},{16,20},{20,16},{24,28},{28,24},{1,5},{5... | collective-permute-start | bytes 393224 | tf_op jit(solution)/shard_map/ppermute | solution.py:266
  82.7 1.7 %collective-permute-start.27 = (bf16[64,1024]{1,0:T(8,128)(2,1)S(1)}, bf16[64,1024]{1,0:T(8,128)(2,1)S(1)}, u32[]{:S(2)}, u32[]{:S(2)}) collective-permute-start(bf16[64,1024]{1,0:T(8,128)(2,1)S(1)} %get-tuple-element.44), channel_id=1, source_target_pairs={{0,12},{4,8},{8,4},{12,0},{16,28},{20,24},{24,20},{28,16},{1,13},{... | collective-permute-start | bytes 393224 | tf_op jit(solution)/shard_map/ppermute | solution.py:266
  86.2 2.1 %collective-permute-done.25.refs_1_ = bf16[64,1024]{1,0:T(8,128)(2,1)S(1)} collective-permute-done((bf16[64,1024]{1,0:T(8,128)(2,1)S(1)}, bf16[64,1024]{1,0:T(8,128)(2,1)S(1)}, u32[]{:S(2)}, u32[]{:S(2)}) %collective-permute-start.25) | collective-permute-done | bytes 131104 | tf_op jit(solution)/shard_map/ppermute | solution.py:266
  89.0 2.6 %collective-permute-done.27.refs_3_ = bf16[64,1024]{1,0:T(8,128)(2,1)S(1)} collective-permute-done((bf16[64,1024]{1,0:T(8,128)(2,1)S(1)}, bf16[64,1024]{1,0:T(8,128)(2,1)S(1)}, u32[]{:S(2)}, u32[]{:S(2)}) %collective-permute-start.27) | collective-permute-done | bytes 131104 | tf_op jit(solution)/shard_map/ppermute | solution.py:266
  92.1 2.2 %collective-permute-start.28 = (bf16[128,1024]{1,0:T(8,128)(2,1)S(1)}, bf16[128,1024]{1,0:T(8,128)(2,1)S(1)}, u32[]{:S(2)}, u32[]{:S(2)}) collective-permute-start(bf16[128,1024]{1,0:T(8,128)(2,1)S(1)} %shard_map.103), channel_id=1, source_target_pairs={{0,16},{4,20},{8,24},{12,28},{16,0},{20,4},{24,8},{28,12},{1,17},{... | collective-permute-start | bytes 786440 | tf_op jit(solution)/shard_map/ppermute | solution.py:266
  94.3 2.0 %collective-permute-done.30.refs_2_ = bf16[64,1024]{1,0:T(8,128)(2,1)S(1)} collective-permute-done((bf16[64,1024]{1,0:T(8,128)(2,1)S(1)}, bf16[64,1024]{1,0:T(8,128)(2,1)S(1)}, u32[]{:S(2)}, u32[]{:S(2)}) %collective-permute-start.30) | collective-permute-done | bytes 131104 | tf_op jit(solution)/shard_map/ppermute | solution.py:266
  98.8 2.3 %collective-permute-start.32 = (bf16[64,1024]{1,0:T(8,128)(2,1)S(1)}, bf16[64,1024]{1,0:T(8,128)(2,1)S(1)}, u32[]{:S(2)}, u32[]{:S(2)}) collective-permute-start(bf16[64,1024]{1,0:T(8,128)(2,1)S(1)} %get-tuple-element.50), channel_id=1, source_target_pairs={{0,4},{4,0},{8,12},{12,8},{16,20},{20,16},{24,28},{28,24},{1,5},{5... | collective-permute-start | bytes 393224 | tf_op jit(solution)/shard_map/ppermute | solution.py:266
  101.0 1.5 %collective-permute-start.34 = (bf16[64,1024]{1,0:T(8,128)(2,1)S(1)}, bf16[64,1024]{1,0:T(8,128)(2,1)S(1)}, u32[]{:S(2)}, u32[]{:S(2)}) collective-permute-start(bf16[64,1024]{1,0:T(8,128)(2,1)S(1)} %get-tuple-element.52), channel_id=1, source_target_pairs={{0,12},{4,8},{8,4},{12,0},{16,28},{20,24},{24,20},{28,16},{1,13},{... | collective-permute-start | bytes 393224 | tf_op jit(solution)/shard_map/ppermute | solution.py:266
  102.6 2.0 %collective-permute-done.32.refs_1_ = bf16[64,1024]{1,0:T(8,128)(2,1)S(1)} collective-permute-done((bf16[64,1024]{1,0:T(8,128)(2,1)S(1)}, bf16[64,1024]{1,0:T(8,128)(2,1)S(1)}, u32[]{:S(2)}, u32[]{:S(2)}) %collective-permute-start.32) | collective-permute-done | bytes 131104 | tf_op jit(solution)/shard_map/ppermute | solution.py:266
  106.0 2.5 %collective-permute-done.34.refs_3_ = bf16[64,1024]{1,0:T(8,128)(2,1)S(1)} collective-permute-done((bf16[64,1024]{1,0:T(8,128)(2,1)S(1)}, bf16[64,1024]{1,0:T(8,128)(2,1)S(1)}, u32[]{:S(2)}, u32[]{:S(2)}) %collective-permute-start.34) | collective-permute-done | bytes 131104 | tf_op jit(solution)/shard_map/ppermute | solution.py:266
  (75 shorter events, 22.6 us)
Async XLA Ops:
  4.4 6.5 %collective-permute-start.4 = (bf16[512,128]{1,0:T(8,128)(2,1)S(1)}, bf16[512,128]{1,0:T(8,128)(2,1)S(1)}, u32[]{:S(2)}, u32[]{:S(2)}) collective-permute-start(bf16[512,128]{1,0:T(8,128)(2,1)S(1)} %get-tuple-element.34), channel_id=1, source_target_pairs={{0,8},{8,16},{16,24},{24,28},{28,20},{20,12},{12,4},{4,0},{1,9},{9... | collective-permute-start | bytes 393224 | tf_op jit(solution)/shard_map/ppermute | solution.py:314
  7.5 5.2 %collective-permute-start.5 = (bf16[512,128]{1,0:T(8,128)(2,1)S(1)}, bf16[512,128]{1,0:T(8,128)(2,1)S(1)}, u32[]{:S(2)}, u32[]{:S(2)}) collective-permute-start(bf16[512,128]{1,0:T(8,128)(2,1)S(1)} %get-tuple-element.34), channel_id=1, source_target_pairs={{8,0},{16,8},{24,16},{28,24},{20,28},{12,20},{4,12},{0,4},{9,1},{1... | collective-permute-start | bytes 393224 | tf_op jit(solution)/shard_map/ppermute | solution.py:317
  11.0 5.0 %collective-permute-start.9 = (bf16[512,128]{1,0:T(8,128)(2,1)S(1)}, bf16[512,128]{1,0:T(8,128)(2,1)S(1)}, u32[]{:S(2)}, u32[]{:S(2)}) collective-permute-start(bf16[512,128]{1,0:T(8,128)(2,1)S(1)} %collective-permute-done.4.refs_0_), channel_id=1, source_target_pairs={{0,8},{8,16},{16,24},{24,28},{28,20},{20,12},{12,4},{4,0},{1,9},{9... | collective-permute-start | bytes 393224 | tf_op jit(solution)/shard_map/ppermute | solution.py:314
  12.8 5.0 %collective-permute-start.10 = (bf16[512,128]{1,0:T(8,128)(2,1)S(1)}, bf16[512,128]{1,0:T(8,128)(2,1)S(1)}, u32[]{:S(2)}, u32[]{:S(2)}) collective-permute-start(bf16[512,128]{1,0:T(8,128)(2,1)S(1)} %collective-permute-done.5.refs_1_), channel_id=1, source_target_pairs={{8,0},{16,8},{24,16},{28,24},{20,28},{12,20},{4,12},{0,4},{9,1},{1... | collective-permute-start | bytes 393224 | tf_op jit(solution)/shard_map/ppermute | solution.py:317
  15.9 5.4 %collective-permute-start.14 = (bf16[512,128]{1,0:T(8,128)(2,1)S(1)}, bf16[512,128]{1,0:T(8,128)(2,1)S(1)}, u32[]{:S(2)}, u32[]{:S(2)}) collective-permute-start(bf16[512,128]{1,0:T(8,128)(2,1)S(1)} %collective-permute-done.9.refs_0_), channel_id=1, source_target_pairs={{0,8},{8,16},{16,24},{24,28},{28,20},{20,12},{12,4},{4,0},{1,9},{9... | collective-permute-start | bytes 393224 | tf_op jit(solution)/shard_map/ppermute | solution.py:314
  17.7 5.6 %collective-permute-start.15 = (bf16[512,128]{1,0:T(8,128)(2,1)S(1)}, bf16[512,128]{1,0:T(8,128)(2,1)S(1)}, u32[]{:S(2)}, u32[]{:S(2)}) collective-permute-start(bf16[512,128]{1,0:T(8,128)(2,1)S(1)} %collective-permute-done.10.refs_1_), channel_id=1, source_target_pairs={{8,0},{16,8},{24,16},{28,24},{20,28},{12,20},{4,12},{0,4},{9,1},{1... | collective-permute-start | bytes 393224 | tf_op jit(solution)/shard_map/ppermute | solution.py:317
  21.3 5.0 %collective-permute-start.16 = (bf16[512,128]{1,0:T(8,128)(2,1)S(1)}, bf16[512,128]{1,0:T(8,128)(2,1)S(1)}, u32[]{:S(2)}, u32[]{:S(2)}) collective-permute-start(bf16[512,128]{1,0:T(8,128)(2,1)S(1)} %collective-permute-done.14.refs_0_), channel_id=1, source_target_pairs={{0,8},{8,16},{16,24},{24,28},{28,20},{20,12},{12,4},{4,0},{1,9},{9... | collective-permute-start | bytes 393224 | tf_op jit(solution)/shard_map/ppermute | solution.py:314
  23.4 5.0 %collective-permute-start = (bf16[512,128]{1,0:T(8,128)(2,1)S(1)}, bf16[512,128]{1,0:T(8,128)(2,1)S(1)}, u32[]{:S(2)}, u32[]{:S(2)}) collective-permute-start(bf16[512,128]{1,0:T(8,128)(2,1)S(1)} %get-tuple-element.31), channel_id=1, source_target_pairs={{0,4},{4,0},{8,12},{12,8},{16,20},{20,16},{24,28},{28,24},{1,5},{5... | collective-permute-start | bytes 393224 | tf_op jit(solution)/shard_map/ppermute | solution.py:266
  26.4 19.5 %collective-permute-start.17 = (bf16[1536,128]{1,0:T(8,128)(2,1)S(1)}, bf16[1536,128]{1,0:T(8,128)(2,1)S(1)}, u32[]{:S(2)}, u32[]{:S(2)}) collective-permute-start(bf16[1536,128]{1,0:T(8,128)(2,1)S(1)} %shard_map.99.refs_8_), channel_id=1, source_target_pairs={{0,2},{1,3},{2,0},{3,1},{4,6},{5,7},{6,4},{7,5},{8,10},{9,11},{10,... | collective-permute-start | bytes 1179656 | tf_op jit(solution)/shard_map/ppermute | solution.py:287
  28.4 6.0 %collective-permute-start.1 = (bf16[512,128]{1,0:T(8,128)(2,1)S(1)}, bf16[512,128]{1,0:T(8,128)(2,1)S(1)}, u32[]{:S(2)}, u32[]{:S(2)}) collective-permute-start(bf16[512,128]{1,0:T(8,128)(2,1)S(1)} %shard_map.94), channel_id=1, source_target_pairs={{0,8},{4,12},{8,16},{12,20},{16,24},{20,28},{1,9},{5,13},{9,17},{1... | collective-permute-start | bytes 393224 | tf_op jit(solution)/shard_map/ppermute | solution.py:306
  31.9 13.9 %collective-permute-start.6 = (bf16[1024,128]{1,0:T(8,128)(2,1)S(1)}, bf16[1024,128]{1,0:T(8,128)(2,1)S(1)}, u32[]{:S(2)}, u32[]{:S(2)}) collective-permute-start(bf16[1024,128]{1,0:T(8,128)(2,1)S(1)} %shard_map.97.refs_0_), channel_id=1, source_target_pairs={{0,2},{1,3},{2,0},{3,1},{4,6},{5,7},{6,4},{7,5},{8,10},{9,11},{10,... | collective-permute-start | bytes 786440 | tf_op jit(solution)/shard_map/ppermute | solution.py:287
  34.5 9.3 %collective-permute-start.2 = (bf16[512,128]{1,0:T(8,128)(2,1)S(1)}, bf16[512,128]{1,0:T(8,128)(2,1)S(1)}, u32[]{:S(2)}, u32[]{:S(2)}) collective-permute-start(bf16[512,128]{1,0:T(8,128)(2,1)S(1)} %shard_map.95), channel_id=1, source_target_pairs={{0,16},{4,20},{8,24},{12,28},{1,17},{5,21},{9,25},{13,29},{2,18},{... | collective-permute-start | bytes 393224 | tf_op jit(solution)/shard_map/ppermute | solution.py:306
  41.3 5.1 %collective-permute-start.7 = (bf16[1024,128]{1,0:T(8,128)(2,1)S(1)}, bf16[1024,128]{1,0:T(8,128)(2,1)S(1)}, u32[]{:S(2)}, u32[]{:S(2)}) collective-permute-start(bf16[1024,128]{1,0:T(8,128)(2,1)S(1)} %shard_map.97.refs_0_), channel_id=1, source_target_pairs={{0,1},{1,0},{2,3},{3,2},{4,5},{5,4},{6,7},{7,6},{8,9},{9,8},{10,11... | collective-permute-start | bytes 786440 | tf_op jit(solution)/shard_map/ppermute | solution.py:287
  41.4 9.0 %collective-permute-start.11 = (bf16[1024,128]{1,0:T(8,128)(2,1)S(1)}, bf16[1024,128]{1,0:T(8,128)(2,1)S(1)}, u32[]{:S(2)}, u32[]{:S(2)}) collective-permute-start(bf16[1024,128]{1,0:T(8,128)(2,1)S(1)} %shard_map.98.refs_4_), channel_id=1, source_target_pairs={{0,2},{1,3},{2,0},{3,1},{4,6},{5,7},{6,4},{7,5},{8,10},{9,11},{10,... | collective-permute-start | bytes 786440 | tf_op jit(solution)/shard_map/ppermute | solution.py:287
  43.9 5.3 %collective-permute-start.3 = (bf16[512,128]{1,0:T(8,128)(2,1)S(1)}, bf16[512,128]{1,0:T(8,128)(2,1)S(1)}, u32[]{:S(2)}, u32[]{:S(2)}) collective-permute-start(bf16[512,128]{1,0:T(8,128)(2,1)S(1)} %get-tuple-element.33), channel_id=1, source_target_pairs={{0,4},{4,0},{8,12},{12,8},{16,20},{20,16},{24,28},{28,24},{1,5},{5... | collective-permute-start | bytes 393224 | tf_op jit(solution)/shard_map/ppermute | solution.py:266
  45.9 7.2 %collective-permute-start.18 = (bf16[1536,128]{1,0:T(8,128)(2,1)S(1)}, bf16[1536,128]{1,0:T(8,128)(2,1)S(1)}, u32[]{:S(2)}, u32[]{:S(2)}) collective-permute-start(bf16[1536,128]{1,0:T(8,128)(2,1)S(1)} %shard_map.99.refs_8_), channel_id=1, source_target_pairs={{0,1},{1,0},{2,3},{3,2},{4,5},{5,4},{6,7},{7,6},{8,9},{9,8},{10,11... | collective-permute-start | bytes 1179656 | tf_op jit(solution)/shard_map/ppermute | solution.py:287
  45.9 7.2 %collective-permute-start.19 = (bf16[1536,128]{1,0:T(8,128)(2,1)S(1)}, bf16[1536,128]{1,0:T(8,128)(2,1)S(1)}, u32[]{:S(2)}, u32[]{:S(2)}) collective-permute-start(bf16[1536,128]{1,0:T(8,128)(2,1)S(1)} %collective-permute-done.17.refs_9_), channel_id=1, source_target_pairs={{0,1},{1,0},{2,3},{3,2},{4,5},{5,4},{6,7},{7,6},{8,9},{9,8},{10,11... | collective-permute-start | bytes 1179656 | tf_op jit(solution)/shard_map/ppermute | solution.py:287
  46.4 6.7 %collective-permute-start.12 = (bf16[1024,128]{1,0:T(8,128)(2,1)S(1)}, bf16[1024,128]{1,0:T(8,128)(2,1)S(1)}, u32[]{:S(2)}, u32[]{:S(2)}) collective-permute-start(bf16[1024,128]{1,0:T(8,128)(2,1)S(1)} %shard_map.98.refs_4_), channel_id=1, source_target_pairs={{0,1},{1,0},{2,3},{3,2},{4,5},{5,4},{6,7},{7,6},{8,9},{9,8},{10,11... | collective-permute-start | bytes 786440 | tf_op jit(solution)/shard_map/ppermute | solution.py:287
  54.7 15.4 %collective-permute-start.21 = (bf16[128,1024]{1,0:T(8,128)(2,1)S(1)}, bf16[128,1024]{1,0:T(8,128)(2,1)S(1)}, u32[]{:S(2)}, u32[]{:S(2)}) collective-permute-start(bf16[128,1024]{1,0:T(8,128)(2,1)S(1)} %get-tuple-element.36), channel_id=1, source_target_pairs={{0,16},{4,20},{8,24},{12,28},{16,0},{20,4},{24,8},{28,12},{1,17},{... | collective-permute-start | bytes 786440 | tf_op jit(solution)/shard_map/ppermute | solution.py:266
  57.3 12.8 %collective-permute-start.20 = (f32[4,128]{1,0:T(4,128)S(1)}, f32[4,128]{1,0:T(4,128)S(1)}, u32[]{:S(2)}, u32[]{:S(2)}) collective-permute-start(f32[4,128]{1,0:T(4,128)S(1)} %get-tuple-element.29.meta_ref), channel_id=1, source_target_pairs={{0,16},{4,20},{8,24},{12,28},{16,0},{20,4},{24,8},{28,12},{1,17},{... | collective-permute-start | bytes 6152 | tf_op jit(solution)/shard_map/ppermute | solution.py:266
  70.5 5.5 %collective-permute-start.22 = (bf16[64,1024]{1,0:T(8,128)(2,1)S(1)}, bf16[64,1024]{1,0:T(8,128)(2,1)S(1)}, u32[]{:S(2)}, u32[]{:S(2)}) collective-permute-start(bf16[64,1024]{1,0:T(8,128)(2,1)S(1)} %get-tuple-element.38), channel_id=1, source_target_pairs={{0,4},{4,0},{8,12},{12,8},{16,20},{20,16},{24,28},{28,24},{1,5},{5... | collective-permute-start | bytes 393224 | tf_op jit(solution)/shard_map/ppermute | solution.py:266
  71.6 6.4 %collective-permute-start.23 = (bf16[64,1024]{1,0:T(8,128)(2,1)S(1)}, bf16[64,1024]{1,0:T(8,128)(2,1)S(1)}, u32[]{:S(2)}, u32[]{:S(2)}) collective-permute-start(bf16[64,1024]{1,0:T(8,128)(2,1)S(1)} %get-tuple-element.39), channel_id=1, source_target_pairs={{0,8},{4,12},{8,0},{12,4},{16,24},{20,28},{24,16},{28,20},{1,9},{5... | collective-permute-start | bytes 393224 | tf_op jit(solution)/shard_map/ppermute | solution.py:266
  71.6 8.0 %collective-permute-start.24 = (bf16[64,1024]{1,0:T(8,128)(2,1)S(1)}, bf16[64,1024]{1,0:T(8,128)(2,1)S(1)}, u32[]{:S(2)}, u32[]{:S(2)}) collective-permute-start(bf16[64,1024]{1,0:T(8,128)(2,1)S(1)} %get-tuple-element.40), channel_id=1, source_target_pairs={{0,12},{4,8},{8,4},{12,0},{16,28},{20,24},{24,20},{28,16},{1,13},{... | collective-permute-start | bytes 393224 | tf_op jit(solution)/shard_map/ppermute | solution.py:266
  80.8 7.4 %collective-permute-start.25 = (bf16[64,1024]{1,0:T(8,128)(2,1)S(1)}, bf16[64,1024]{1,0:T(8,128)(2,1)S(1)}, u32[]{:S(2)}, u32[]{:S(2)}) collective-permute-start(bf16[64,1024]{1,0:T(8,128)(2,1)S(1)} %get-tuple-element.42), channel_id=1, source_target_pairs={{0,4},{4,0},{8,12},{12,8},{16,20},{20,16},{24,28},{28,24},{1,5},{5... | collective-permute-start | bytes 393224 | tf_op jit(solution)/shard_map/ppermute | solution.py:266
  82.4 6.6 %collective-permute-start.26 = (bf16[64,1024]{1,0:T(8,128)(2,1)S(1)}, bf16[64,1024]{1,0:T(8,128)(2,1)S(1)}, u32[]{:S(2)}, u32[]{:S(2)}) collective-permute-start(bf16[64,1024]{1,0:T(8,128)(2,1)S(1)} %get-tuple-element.43), channel_id=1, source_target_pairs={{0,8},{4,12},{8,0},{12,4},{16,24},{20,28},{24,16},{28,20},{1,9},{5... | collective-permute-start | bytes 393224 | tf_op jit(solution)/shard_map/ppermute | solution.py:266
  82.7 9.0 %collective-permute-start.27 = (bf16[64,1024]{1,0:T(8,128)(2,1)S(1)}, bf16[64,1024]{1,0:T(8,128)(2,1)S(1)}, u32[]{:S(2)}, u32[]{:S(2)}) collective-permute-start(bf16[64,1024]{1,0:T(8,128)(2,1)S(1)} %get-tuple-element.44), channel_id=1, source_target_pairs={{0,12},{4,8},{8,4},{12,0},{16,28},{20,24},{24,20},{28,16},{1,13},{... | collective-permute-start | bytes 393224 | tf_op jit(solution)/shard_map/ppermute | solution.py:266
  84.4 9.9 %collective-permute-start.29 = (bf16[64,1024]{1,0:T(8,128)(2,1)S(1)}, bf16[64,1024]{1,0:T(8,128)(2,1)S(1)}, u32[]{:S(2)}, u32[]{:S(2)}) collective-permute-start(bf16[64,1024]{1,0:T(8,128)(2,1)S(1)} %get-tuple-element.46), channel_id=1, source_target_pairs={{0,4},{4,0},{8,12},{12,8},{16,20},{20,16},{24,28},{28,24},{1,5},{5... | collective-permute-start | bytes 393224 | tf_op jit(solution)/shard_map/ppermute | solution.py:266
  85.9 10.4 %collective-permute-start.30 = (bf16[64,1024]{1,0:T(8,128)(2,1)S(1)}, bf16[64,1024]{1,0:T(8,128)(2,1)S(1)}, u32[]{:S(2)}, u32[]{:S(2)}) collective-permute-start(bf16[64,1024]{1,0:T(8,128)(2,1)S(1)} %get-tuple-element.47), channel_id=1, source_target_pairs={{0,8},{4,12},{8,0},{12,4},{16,24},{20,28},{24,16},{28,20},{1,9},{5... | collective-permute-start | bytes 393224 | tf_op jit(solution)/shard_map/ppermute | solution.py:266
  88.2 9.3 %collective-permute-start.31 = (bf16[64,1024]{1,0:T(8,128)(2,1)S(1)}, bf16[64,1024]{1,0:T(8,128)(2,1)S(1)}, u32[]{:S(2)}, u32[]{:S(2)}) collective-permute-start(bf16[64,1024]{1,0:T(8,128)(2,1)S(1)} %get-tuple-element.48), channel_id=1, source_target_pairs={{0,12},{4,8},{8,4},{12,0},{16,28},{20,24},{24,20},{28,16},{1,13},{... | collective-permute-start | bytes 393224 | tf_op jit(solution)/shard_map/ppermute | solution.py:266
  92.1 16.3 %collective-permute-start.28 = (bf16[128,1024]{1,0:T(8,128)(2,1)S(1)}, bf16[128,1024]{1,0:T(8,128)(2,1)S(1)}, u32[]{:S(2)}, u32[]{:S(2)}) collective-permute-start(bf16[128,1024]{1,0:T(8,128)(2,1)S(1)} %shard_map.103), channel_id=1, source_target_pairs={{0,16},{4,20},{8,24},{12,28},{16,0},{20,4},{24,8},{28,12},{1,17},{... | collective-permute-start | bytes 786440 | tf_op jit(solution)/shard_map/ppermute | solution.py:266
  98.8 5.8 %collective-permute-start.32 = (bf16[64,1024]{1,0:T(8,128)(2,1)S(1)}, bf16[64,1024]{1,0:T(8,128)(2,1)S(1)}, u32[]{:S(2)}, u32[]{:S(2)}) collective-permute-start(bf16[64,1024]{1,0:T(8,128)(2,1)S(1)} %get-tuple-element.50), channel_id=1, source_target_pairs={{0,4},{4,0},{8,12},{12,8},{16,20},{20,16},{24,28},{28,24},{1,5},{5... | collective-permute-start | bytes 393224 | tf_op jit(solution)/shard_map/ppermute | solution.py:266
  101.0 7.4 %collective-permute-start.34 = (bf16[64,1024]{1,0:T(8,128)(2,1)S(1)}, bf16[64,1024]{1,0:T(8,128)(2,1)S(1)}, u32[]{:S(2)}, u32[]{:S(2)}) collective-permute-start(bf16[64,1024]{1,0:T(8,128)(2,1)S(1)} %get-tuple-element.52), channel_id=1, source_target_pairs={{0,12},{4,8},{8,4},{12,0},{16,28},{20,24},{24,20},{28,16},{1,13},{... | collective-permute-start | bytes 393224 | tf_op jit(solution)/shard_map/ppermute | solution.py:266
  (14 other events, 158.4 us)

commit v4 on v3

--- a/solution.py
+++ b/solution.py
@@ -21,7 +21,7 @@
 VMEM = pl.BlockSpec(memory_space=pltpu.VMEM)
 
 
-def call(body, outs, xs, scratch=(), in_hbm=()):
+def call(body, outs, xs, scratch=(), in_hbm=(), loads=False):
     run = pl.pallas_call(
         body,
         out_shape=outs,
@@ -30,7 +30,7 @@
         scratch_shapes=scratch,
         compiler_params=pltpu.CompilerParams(vmem_limit_bytes=KERNEL_VMEM),
     )
-    spaces = [pltpu.HBM if i in in_hbm else pltpu.VMEM for i in range(len(xs))]
+    spaces = [pltpu.HBM if i in in_hbm or loads else pltpu.VMEM for i in range(len(xs))]
     return run(*[pltpu.with_memory_space_constraint(x, m) for x, m in zip(xs, spaces)])
 
 
@@ -67,16 +67,15 @@
     refs[-1][...] = total.astype(BF)
 
 
-def prefix_body(mine_ref, got_ref, *refs):
+def prefix_body(bits, mine_ref, got_ref, *refs):
     came, own_ref, back_ref = refs[:-2], refs[-2], refs[-1]
-    before = came[0][...].astype(F32)
-    for r in came[1:]:
-        before = before + r[...].astype(F32)
-    even = lax.rem(lax.axis_index("seq"), 2) == 0
-    got = got_ref[...].astype(F32)
-    own_ref[...] = (before + jnp.where(even, jnp.zeros_like(got), got)).astype(BF)
-    mine = mine_ref[...]
-    back_ref[...] = (before + jnp.where(even, mine, jnp.zeros_like(mine))).astype(BF)
+    s = lax.axis_index("seq")
+    before = jnp.zeros(mine_ref.shape, F32)
+    for bit, r in zip(bits, came):
+        before = before + jnp.where(jnp.bitwise_and(s, bit) != 0, r[...].astype(F32), 0.0)
+    even = jnp.bitwise_and(s, 1) == 0
+    own_ref[...] = (before + jnp.where(even, 0.0, got_ref[...].astype(F32))).astype(BF)
+    back_ref[...] = (before + jnp.where(even, mine_ref[...], 0.0)).astype(BF)
 
 
 def pack_body(*refs):
@@ -265,8 +264,8 @@
     def flip(x, k):
         return lax.ppermute(x, "seq", [(i, i ^ k) for i in range(n)])
 
-    def kernel(body, outs, xs, scratch=(), in_hbm=()):
-        return call(body, outs, xs, scratch, in_hbm)
+    def kernel(body, outs, xs, scratch=(), in_hbm=(), loads=False):
+        return call(body, outs, xs, scratch, in_hbm, loads)
 
     def flips(xs):
         return [xs[0]] + [flip(xs[k], k) for k in range(1, near)]
@@ -294,18 +293,21 @@
         (key_rows, value_rows, expert_ids.T, gate_values.T, out_weight),
         [pltpu.VMEM((2 * half, DV), F32), pltpu.SemaphoreType.DMA],
         in_hbm=(4,),
+        loads=True,
     )
     meta_far = flip(meta, near)
     state = sds((half, DV), BF)
     got = flip(sent, 1)
-    came = []
-    step = 1
-    while step < n // 2:
-        hop = [(i, i + 2 * step) for i in range(n - 2 * step)]
+    came, bits = [], []
+    bit = 2
+    while bit < n:
         run = kernel(running_body, state, (mine, got, *came))
-        came.append(lax.ppermute(run, "seq", hop))
-        step *= 2
-    prefix_mine, prefix_back = kernel(prefix_body, (state, state), (mine, got, *came))
+        came.append(flip(run, bit))
+        bits.append(bit)
+        bit *= 2
+    prefix_mine, prefix_back = kernel(
+        functools.partial(prefix_body, bits), (state, state), (mine, got, *came)
+    )
     prefix_other = flip(prefix_back, 1)
 
     fs, bs = [], []

time: 110 us -> 105 us (0.955)
  starting transfers between devices: 46.2 us -> 40.8 us
  local copies, waits for them, and re-layouts: 3.39 us -> 0.04 us
  waiting for transfers between devices: 49.8 us -> 52.8 us
    ppermute x2 -> x0, starting transfers between devices: 10.3 us -> none  [small_group(): came.append(lax.ppermute(run, 'seq', hop))]
    ppermute x17 -> x19, starting transfers between devices: 20.6 us -> 26.7 us  [flip(): return lax.ppermute(x, 'seq', [(i, i ^ k) for i in range(n)])]
    ppermute x17 -> x19, waiting for transfers between devices: 34.5 us -> 40 us  [flip(): return lax.ppermute(x, 'seq', [(i, i ^ k) for i in range(n)])]
    unnamed x22 -> x14, local copies, waits for them, and re-layouts: 3.39 us -> 0.04 us
    ppermute x2 -> x0, waiting for transfers between devices: 1.37 us -> none  [small_group(): came.append(lax.ppermute(run, 'seq', hop))]
    ppermute x9, starting transfers between devices: 6.16 us -> 4.91 us  [share(): held = held + [lax.ppermute(h, 'win', pairs) for h in held]]
    ppermute x9, waiting for transfers between devices: 1.19 us -> 0.02 us  [share(): held = held + [lax.ppermute(h, 'win', pairs) for h in held]]
  transfers between devices with their start and end apart: 35 -> 35, of which waited for: 19 -> 18; matrix products, arithmetic and copies ran while one was open for 0% -> 0% of each run, Pallas kernels for 4% -> 4%
where the time goes in v4:
time: 105 us
  waiting for transfers between devices  52.8 us (50%)
  starting transfers between devices  40.8 us (39%)
  Pallas kernels  11 us (10%)
    ppermute x19, waiting for transfers between devices, flip(): return lax.ppermute(x, 'seq', [(i, i ^ k) for i in range(n)])  40 us
    ppermute x19, starting transfers between devices, flip(): return lax.ppermute(x, 'seq', [(i, i ^ k) for i in range(n)])  26.7 us
    ppermute x4, waiting for transfers between devices, small_group(): f = lax.ppermute(f, 'seq', ahead)  12.7 us
    pallas_call x15, Pallas kernels, call(): run(*[pltpu.with_memory_space_constraint(x, m) for x, m in zip(xs, spaces)])  11 us
    ppermute x4, starting transfers between devices, small_group(): f = lax.ppermute(f, 'seq', ahead)  8.73 us
    ppermute x9, starting transfers between devices, share(): held = held + [lax.ppermute(h, 'win', pairs) for h in held]  4.91 us
  transfers between devices with their start and end apart: 35, of which 18 were waited for; matrix products, arithmetic and copies ran while one was open for 0% of the time, Pallas kernels for 4%

profile of v4, /device:TPU:0, one launch (start us, length us, event | category | flops | bytes accessed | tf_op | source)
XLA Modules:
  0.0 104.8 jit_solution(12333411093713941135)
XLA Ops:
  0.0 2.0 %shard_map.91 = (f32[512,128]{1,0:T(8,128)S(1)}, bf16[512,128]{1,0:T(8,128)(2,1)S(1)}, f32[4,128]{1,0:T(4,128)S(1)}, bf16[512,128]{1,0:T(8,128)(2,1)S(1)}) custom-call(bf16[128,1024]{1,0:T(8,128)(2,1)} %k_ref.5, bf16[128,2048]{1,0:T(8,128)(2,1)} %v_ref.5, s32[2,128]{1,0:T(2,128)} %bitcast.2, f32[2,128]{1,0:T(2,128)} %bitcast.3, bf16[2048,128]{1,0:T(8,128)(2,1)} %wown_ref.1), custom_call_target="tpu_custom_call" | custom-call | tf_op jit(solution)/shard_map/pallas_call | solution.py:34
  2.1 3.1 %collective-permute-start.4 = (bf16[512,128]{1,0:T(8,128)(2,1)S(1)}, bf16[512,128]{1,0:T(8,128)(2,1)S(1)}, u32[]{:S(2)}, u32[]{:S(2)}) collective-permute-start(bf16[512,128]{1,0:T(8,128)(2,1)S(1)} %get-tuple-element.34), channel_id=1, source_target_pairs={{0,8},{8,16},{16,24},{24,28},{28,20},{20,12},{12,4},{4,0},{1,9},{9... | collective-permute-start | bytes 393224 | tf_op jit(solution)/shard_map/ppermute | solution.py:316
  5.2 3.4 %collective-permute-done.4.refs_0_ = bf16[512,128]{1,0:T(8,128)(2,1)S(1)} collective-permute-done((bf16[512,128]{1,0:T(8,128)(2,1)S(1)}, bf16[512,128]{1,0:T(8,128)(2,1)S(1)}, u32[]{:S(2)}, u32[]{:S(2)}) %collective-permute-start.4) | collective-permute-done | bytes 131104 | tf_op jit(solution)/shard_map/ppermute | solution.py:316
  8.6 1.8 %collective-permute-start.9 = (bf16[512,128]{1,0:T(8,128)(2,1)S(1)}, bf16[512,128]{1,0:T(8,128)(2,1)S(1)}, u32[]{:S(2)}, u32[]{:S(2)}) collective-permute-start(bf16[512,128]{1,0:T(8,128)(2,1)S(1)} %collective-permute-done.4.refs_0_), channel_id=1, source_target_pairs={{0,8},{8,16},{16,24},{24,28},{28,20},{20,12},{12,4},{4,0},{1,9},{9... | collective-permute-start | bytes 393224 | tf_op jit(solution)/shard_map/ppermute | solution.py:316
  10.6 2.9 %collective-permute-done.9.refs_0_ = bf16[512,128]{1,0:T(8,128)(2,1)S(1)} collective-permute-done((bf16[512,128]{1,0:T(8,128)(2,1)S(1)}, bf16[512,128]{1,0:T(8,128)(2,1)S(1)}, u32[]{:S(2)}, u32[]{:S(2)}) %collective-permute-start.9) | collective-permute-done | bytes 131104 | tf_op jit(solution)/shard_map/ppermute | solution.py:316
  13.6 1.8 %collective-permute-start.14 = (bf16[512,128]{1,0:T(8,128)(2,1)S(1)}, bf16[512,128]{1,0:T(8,128)(2,1)S(1)}, u32[]{:S(2)}, u32[]{:S(2)}) collective-permute-start(bf16[512,128]{1,0:T(8,128)(2,1)S(1)} %collective-permute-done.9.refs_0_), channel_id=1, source_target_pairs={{0,8},{8,16},{16,24},{24,28},{28,20},{20,12},{12,4},{4,0},{1,9},{9... | collective-permute-start | bytes 393224 | tf_op jit(solution)/shard_map/ppermute | solution.py:316
  15.6 3.4 %collective-permute-done.14.refs_0_ = bf16[512,128]{1,0:T(8,128)(2,1)S(1)} collective-permute-done((bf16[512,128]{1,0:T(8,128)(2,1)S(1)}, bf16[512,128]{1,0:T(8,128)(2,1)S(1)}, u32[]{:S(2)}, u32[]{:S(2)}) %collective-permute-start.14) | collective-permute-done | bytes 131104 | tf_op jit(solution)/shard_map/ppermute | solution.py:316
  19.0 2.0 %collective-permute-start.16 = (bf16[512,128]{1,0:T(8,128)(2,1)S(1)}, bf16[512,128]{1,0:T(8,128)(2,1)S(1)}, u32[]{:S(2)}, u32[]{:S(2)}) collective-permute-start(bf16[512,128]{1,0:T(8,128)(2,1)S(1)} %collective-permute-done.14.refs_0_), channel_id=1, source_target_pairs={{0,8},{8,16},{16,24},{24,28},{28,20},{20,12},{12,4},{4,0},{1,9},{9... | collective-permute-start | bytes 393224 | tf_op jit(solution)/shard_map/ppermute | solution.py:316
  21.0 2.9 %collective-permute-done.16.refs_2_ = bf16[512,128]{1,0:T(8,128)(2,1)S(1)} collective-permute-done((bf16[512,128]{1,0:T(8,128)(2,1)S(1)}, bf16[512,128]{1,0:T(8,128)(2,1)S(1)}, u32[]{:S(2)}, u32[]{:S(2)}) %collective-permute-start.16) | collective-permute-done | bytes 131104 | tf_op jit(solution)/shard_map/ppermute | solution.py:316
  24.0 2.1 %collective-permute-start.17 = (bf16[1536,128]{1,0:T(8,128)(2,1)S(1)}, bf16[1536,128]{1,0:T(8,128)(2,1)S(1)}, u32[]{:S(2)}, u32[]{:S(2)}) collective-permute-start(bf16[1536,128]{1,0:T(8,128)(2,1)S(1)} %shard_map.99.refs_8_), channel_id=1, source_target_pairs={{0,2},{1,3},{2,0},{3,1},{4,6},{5,7},{6,4},{7,5},{8,10},{9,11},{10,... | collective-permute-start | bytes 1179656 | tf_op jit(solution)/shard_map/ppermute | solution.py:286
  26.2 2.5 %collective-permute-start.1 = (bf16[512,128]{1,0:T(8,128)(2,1)S(1)}, bf16[512,128]{1,0:T(8,128)(2,1)S(1)}, u32[]{:S(2)}, u32[]{:S(2)}) collective-permute-start(bf16[512,128]{1,0:T(8,128)(2,1)S(1)} %shard_map.94), channel_id=1, source_target_pairs={{0,8},{4,12},{8,0},{12,4},{16,24},{20,28},{24,16},{28,20},{1,9},{5... | collective-permute-start | bytes 393224 | tf_op jit(solution)/shard_map/ppermute | solution.py:265
  29.2 3.0 %collective-permute-done.1.refs_1_.refs_0_ = bf16[512,128]{1,0:T(8,128)(2,1)S(1)} collective-permute-done((bf16[512,128]{1,0:T(8,128)(2,1)S(1)}, bf16[512,128]{1,0:T(8,128)(2,1)S(1)}, u32[]{:S(2)}, u32[]{:S(2)}) %collective-permute-start.1) | collective-permute-done | bytes 131104 | tf_op jit(solution)/shard_map/ppermute | solution.py:265
  32.3 2.3 %collective-permute-start.2 = (bf16[512,128]{1,0:T(8,128)(2,1)S(1)}, bf16[512,128]{1,0:T(8,128)(2,1)S(1)}, u32[]{:S(2)}, u32[]{:S(2)}) collective-permute-start(bf16[512,128]{1,0:T(8,128)(2,1)S(1)} %shard_map.95), channel_id=1, source_target_pairs={{0,16},{4,20},{8,24},{12,28},{16,0},{20,4},{24,8},{28,12},{1,17},{... | collective-permute-start | bytes 393224 | tf_op jit(solution)/shard_map/ppermute | solution.py:265
  35.8 3.8 %collective-permute-done.2.refs_1_ = bf16[512,128]{1,0:T(8,128)(2,1)S(1)} collective-permute-done((bf16[512,128]{1,0:T(8,128)(2,1)S(1)}, bf16[512,128]{1,0:T(8,128)(2,1)S(1)}, u32[]{:S(2)}, u32[]{:S(2)}) %collective-permute-start.2) | collective-permute-done | bytes 131104 | tf_op jit(solution)/shard_map/ppermute | solution.py:265
  39.8 2.2 %collective-permute-start.3 = (bf16[512,128]{1,0:T(8,128)(2,1)S(1)}, bf16[512,128]{1,0:T(8,128)(2,1)S(1)}, u32[]{:S(2)}, u32[]{:S(2)}) collective-permute-start(bf16[512,128]{1,0:T(8,128)(2,1)S(1)} %get-tuple-element.33), channel_id=1, source_target_pairs={{0,4},{4,0},{8,12},{12,8},{16,20},{20,16},{24,28},{28,24},{1,5},{5... | collective-permute-start | bytes 393224 | tf_op jit(solution)/shard_map/ppermute | solution.py:265
  42.5 2.4 %collective-permute-done.3.po_ref = bf16[512,128]{1,0:T(8,128)(2,1)S(1)} collective-permute-done((bf16[512,128]{1,0:T(8,128)(2,1)S(1)}, bf16[512,128]{1,0:T(8,128)(2,1)S(1)}, u32[]{:S(2)}, u32[]{:S(2)}) %collective-permute-start.3) | collective-permute-done | bytes 131104 | tf_op jit(solution)/shard_map/ppermute | solution.py:265
  50.6 2.1 %collective-permute-start.20 = (f32[4,128]{1,0:T(4,128)S(1)}, f32[4,128]{1,0:T(4,128)S(1)}, u32[]{:S(2)}, u32[]{:S(2)}) collective-permute-start(f32[4,128]{1,0:T(4,128)S(1)} %get-tuple-element.29.meta_ref), channel_id=1, source_target_pairs={{0,16},{4,20},{8,24},{12,28},{16,0},{20,4},{24,8},{28,12},{1,17},{... | collective-permute-start | bytes 6152 | tf_op jit(solution)/shard_map/ppermute | solution.py:265
  52.7 11.9 %collective-permute-done.20.meta_ref = f32[4,128]{1,0:T(4,128)S(1)} collective-permute-done((f32[4,128]{1,0:T(4,128)S(1)}, f32[4,128]{1,0:T(4,128)S(1)}, u32[]{:S(2)}, u32[]{:S(2)}) %collective-permute-start.20) | collective-permute-done | bytes 2080 | tf_op jit(solution)/shard_map/ppermute | solution.py:265
  65.1 1.8 %collective-permute-start.22 = (bf16[64,1024]{1,0:T(8,128)(2,1)S(1)}, bf16[64,1024]{1,0:T(8,128)(2,1)S(1)}, u32[]{:S(2)}, u32[]{:S(2)}) collective-permute-start(bf16[64,1024]{1,0:T(8,128)(2,1)S(1)} %get-tuple-element.38), channel_id=1, source_target_pairs={{0,4},{4,0},{8,12},{12,8},{16,20},{20,16},{24,28},{28,24},{1,5},{5... | collective-permute-start | bytes 393224 | tf_op jit(solution)/shard_map/ppermute | solution.py:265
  66.8 1.8 %collective-permute-start.24 = (bf16[64,1024]{1,0:T(8,128)(2,1)S(1)}, bf16[64,1024]{1,0:T(8,128)(2,1)S(1)}, u32[]{:S(2)}, u32[]{:S(2)}) collective-permute-start(bf16[64,1024]{1,0:T(8,128)(2,1)S(1)} %get-tuple-element.40), channel_id=1, source_target_pairs={{0,12},{4,8},{8,4},{12,0},{16,28},{20,24},{24,20},{28,16},{1,13},{... | collective-permute-start | bytes 393224 | tf_op jit(solution)/shard_map/ppermute | solution.py:265
  68.6 1.9 %collective-permute-done.22.refs_1_ = bf16[64,1024]{1,0:T(8,128)(2,1)S(1)} collective-permute-done((bf16[64,1024]{1,0:T(8,128)(2,1)S(1)}, bf16[64,1024]{1,0:T(8,128)(2,1)S(1)}, u32[]{:S(2)}, u32[]{:S(2)}) %collective-permute-start.22) | collective-permute-done | bytes 131104 | tf_op jit(solution)/shard_map/ppermute | solution.py:265
  70.5 2.7 %collective-permute-done.23.refs_2_ = bf16[64,1024]{1,0:T(8,128)(2,1)S(1)} collective-permute-done((bf16[64,1024]{1,0:T(8,128)(2,1)S(1)}, bf16[64,1024]{1,0:T(8,128)(2,1)S(1)}, u32[]{:S(2)}, u32[]{:S(2)}) %collective-permute-start.23) | collective-permute-done | bytes 131104 | tf_op jit(solution)/shard_map/ppermute | solution.py:265
  75.8 1.7 %collective-permute-start.25 = (bf16[64,1024]{1,0:T(8,128)(2,1)S(1)}, bf16[64,1024]{1,0:T(8,128)(2,1)S(1)}, u32[]{:S(2)}, u32[]{:S(2)}) collective-permute-start(bf16[64,1024]{1,0:T(8,128)(2,1)S(1)} %get-tuple-element.42), channel_id=1, source_target_pairs={{0,4},{4,0},{8,12},{12,8},{16,20},{20,16},{24,28},{28,24},{1,5},{5... | collective-permute-start | bytes 393224 | tf_op jit(solution)/shard_map/ppermute | solution.py:265
  79.3 1.7 %collective-permute-start.29 = (bf16[64,1024]{1,0:T(8,128)(2,1)S(1)}, bf16[64,1024]{1,0:T(8,128)(2,1)S(1)}, u32[]{:S(2)}, u32[]{:S(2)}) collective-permute-start(bf16[64,1024]{1,0:T(8,128)(2,1)S(1)} %get-tuple-element.46), channel_id=1, source_target_pairs={{0,4},{4,0},{8,12},{12,8},{16,20},{20,16},{24,28},{28,24},{1,5},{5... | collective-permute-start | bytes 393224 | tf_op jit(solution)/shard_map/ppermute | solution.py:265
  81.3 1.7 %collective-permute-done.25.refs_1_ = bf16[64,1024]{1,0:T(8,128)(2,1)S(1)} collective-permute-done((bf16[64,1024]{1,0:T(8,128)(2,1)S(1)}, bf16[64,1024]{1,0:T(8,128)(2,1)S(1)}, u32[]{:S(2)}, u32[]{:S(2)}) %collective-permute-start.25) | collective-permute-done | bytes 131104 | tf_op jit(solution)/shard_map/ppermute | solution.py:265
  84.2 2.4 %collective-permute-done.27.refs_3_ = bf16[64,1024]{1,0:T(8,128)(2,1)S(1)} collective-permute-done((bf16[64,1024]{1,0:T(8,128)(2,1)S(1)}, bf16[64,1024]{1,0:T(8,128)(2,1)S(1)}, u32[]{:S(2)}, u32[]{:S(2)}) %collective-permute-start.27) | collective-permute-done | bytes 131104 | tf_op jit(solution)/shard_map/ppermute | solution.py:265
  87.1 2.5 %collective-permute-start.28 = (bf16[128,1024]{1,0:T(8,128)(2,1)S(1)}, bf16[128,1024]{1,0:T(8,128)(2,1)S(1)}, u32[]{:S(2)}, u32[]{:S(2)}) collective-permute-start(bf16[128,1024]{1,0:T(8,128)(2,1)S(1)} %shard_map.103), channel_id=1, source_target_pairs={{0,16},{4,20},{8,24},{12,28},{16,0},{20,4},{24,8},{28,12},{1,17},{... | collective-permute-start | bytes 786440 | tf_op jit(solution)/shard_map/ppermute | solution.py:265
  89.5 1.8 %collective-permute-done.30.refs_2_ = bf16[64,1024]{1,0:T(8,128)(2,1)S(1)} collective-permute-done((bf16[64,1024]{1,0:T(8,128)(2,1)S(1)}, bf16[64,1024]{1,0:T(8,128)(2,1)S(1)}, u32[]{:S(2)}, u32[]{:S(2)}) %collective-permute-start.30) | collective-permute-done | bytes 131104 | tf_op jit(solution)/shard_map/ppermute | solution.py:265
  93.8 2.5 %collective-permute-start.32 = (bf16[64,1024]{1,0:T(8,128)(2,1)S(1)}, bf16[64,1024]{1,0:T(8,128)(2,1)S(1)}, u32[]{:S(2)}, u32[]{:S(2)}) collective-permute-start(bf16[64,1024]{1,0:T(8,128)(2,1)S(1)} %get-tuple-element.50), channel_id=1, source_target_pairs={{0,4},{4,0},{8,12},{12,8},{16,20},{20,16},{24,28},{28,24},{1,5},{5... | collective-permute-start | bytes 393224 | tf_op jit(solution)/shard_map/ppermute | solution.py:265
  96.3 1.5 %collective-permute-start.34 = (bf16[64,1024]{1,0:T(8,128)(2,1)S(1)}, bf16[64,1024]{1,0:T(8,128)(2,1)S(1)}, u32[]{:S(2)}, u32[]{:S(2)}) collective-permute-start(bf16[64,1024]{1,0:T(8,128)(2,1)S(1)} %get-tuple-element.52), channel_id=1, source_target_pairs={{0,12},{4,8},{8,4},{12,0},{16,28},{20,24},{24,20},{28,16},{1,13},{... | collective-permute-start | bytes 393224 | tf_op jit(solution)/shard_map/ppermute | solution.py:265
  97.9 2.3 %collective-permute-done.32.refs_1_ = bf16[64,1024]{1,0:T(8,128)(2,1)S(1)} collective-permute-done((bf16[64,1024]{1,0:T(8,128)(2,1)S(1)}, bf16[64,1024]{1,0:T(8,128)(2,1)S(1)}, u32[]{:S(2)}, u32[]{:S(2)}) %collective-permute-start.32) | collective-permute-done | bytes 131104 | tf_op jit(solution)/shard_map/ppermute | solution.py:265
  101.5 2.1 %collective-permute-done.34.refs_3_ = bf16[64,1024]{1,0:T(8,128)(2,1)S(1)} collective-permute-done((bf16[64,1024]{1,0:T(8,128)(2,1)S(1)}, bf16[64,1024]{1,0:T(8,128)(2,1)S(1)}, u32[]{:S(2)}, u32[]{:S(2)}) %collective-permute-start.34) | collective-permute-done | bytes 131104 | tf_op jit(solution)/shard_map/ppermute | solution.py:265
  (67 shorter events, 20.2 us)
Async XLA Ops:
  2.1 6.5 %collective-permute-start.4 = (bf16[512,128]{1,0:T(8,128)(2,1)S(1)}, bf16[512,128]{1,0:T(8,128)(2,1)S(1)}, u32[]{:S(2)}, u32[]{:S(2)}) collective-permute-start(bf16[512,128]{1,0:T(8,128)(2,1)S(1)} %get-tuple-element.34), channel_id=1, source_target_pairs={{0,8},{8,16},{16,24},{24,28},{28,20},{20,12},{12,4},{4,0},{1,9},{9... | collective-permute-start | bytes 393224 | tf_op jit(solution)/shard_map/ppermute | solution.py:316
  5.2 5.2 %collective-permute-start.5 = (bf16[512,128]{1,0:T(8,128)(2,1)S(1)}, bf16[512,128]{1,0:T(8,128)(2,1)S(1)}, u32[]{:S(2)}, u32[]{:S(2)}) collective-permute-start(bf16[512,128]{1,0:T(8,128)(2,1)S(1)} %get-tuple-element.34), channel_id=1, source_target_pairs={{8,0},{16,8},{24,16},{28,24},{20,28},{12,20},{4,12},{0,4},{9,1},{1... | collective-permute-start | bytes 393224 | tf_op jit(solution)/shard_map/ppermute | solution.py:319
  8.6 5.0 %collective-permute-start.9 = (bf16[512,128]{1,0:T(8,128)(2,1)S(1)}, bf16[512,128]{1,0:T(8,128)(2,1)S(1)}, u32[]{:S(2)}, u32[]{:S(2)}) collective-permute-start(bf16[512,128]{1,0:T(8,128)(2,1)S(1)} %collective-permute-done.4.refs_0_), channel_id=1, source_target_pairs={{0,8},{8,16},{16,24},{24,28},{28,20},{20,12},{12,4},{4,0},{1,9},{9... | collective-permute-start | bytes 393224 | tf_op jit(solution)/shard_map/ppermute | solution.py:316
  10.4 5.0 %collective-permute-start.10 = (bf16[512,128]{1,0:T(8,128)(2,1)S(1)}, bf16[512,128]{1,0:T(8,128)(2,1)S(1)}, u32[]{:S(2)}, u32[]{:S(2)}) collective-permute-start(bf16[512,128]{1,0:T(8,128)(2,1)S(1)} %collective-permute-done.5.refs_1_), channel_id=1, source_target_pairs={{8,0},{16,8},{24,16},{28,24},{20,28},{12,20},{4,12},{0,4},{9,1},{1... | collective-permute-start | bytes 393224 | tf_op jit(solution)/shard_map/ppermute | solution.py:319
  13.6 5.4 %collective-permute-start.14 = (bf16[512,128]{1,0:T(8,128)(2,1)S(1)}, bf16[512,128]{1,0:T(8,128)(2,1)S(1)}, u32[]{:S(2)}, u32[]{:S(2)}) collective-permute-start(bf16[512,128]{1,0:T(8,128)(2,1)S(1)} %collective-permute-done.9.refs_0_), channel_id=1, source_target_pairs={{0,8},{8,16},{16,24},{24,28},{28,20},{20,12},{12,4},{4,0},{1,9},{9... | collective-permute-start | bytes 393224 | tf_op jit(solution)/shard_map/ppermute | solution.py:316
  15.4 5.6 %collective-permute-start.15 = (bf16[512,128]{1,0:T(8,128)(2,1)S(1)}, bf16[512,128]{1,0:T(8,128)(2,1)S(1)}, u32[]{:S(2)}, u32[]{:S(2)}) collective-permute-start(bf16[512,128]{1,0:T(8,128)(2,1)S(1)} %collective-permute-done.10.refs_1_), channel_id=1, source_target_pairs={{8,0},{16,8},{24,16},{28,24},{20,28},{12,20},{4,12},{0,4},{9,1},{1... | collective-permute-start | bytes 393224 | tf_op jit(solution)/shard_map/ppermute | solution.py:319
  21.0 5.2 %collective-permute-start = (bf16[512,128]{1,0:T(8,128)(2,1)S(1)}, bf16[512,128]{1,0:T(8,128)(2,1)S(1)}, u32[]{:S(2)}, u32[]{:S(2)}) collective-permute-start(bf16[512,128]{1,0:T(8,128)(2,1)S(1)} %get-tuple-element.31), channel_id=1, source_target_pairs={{0,4},{4,0},{8,12},{12,8},{16,20},{20,16},{24,28},{28,24},{1,5},{5... | collective-permute-start | bytes 393224 | tf_op jit(solution)/shard_map/ppermute | solution.py:265
  24.0 17.9 %collective-permute-start.17 = (bf16[1536,128]{1,0:T(8,128)(2,1)S(1)}, bf16[1536,128]{1,0:T(8,128)(2,1)S(1)}, u32[]{:S(2)}, u32[]{:S(2)}) collective-permute-start(bf16[1536,128]{1,0:T(8,128)(2,1)S(1)} %shard_map.99.refs_8_), channel_id=1, source_target_pairs={{0,2},{1,3},{2,0},{3,1},{4,6},{5,7},{6,4},{7,5},{8,10},{9,11},{10,... | collective-permute-start | bytes 1179656 | tf_op jit(solution)/shard_map/ppermute | solution.py:286
  26.2 6.1 %collective-permute-start.1 = (bf16[512,128]{1,0:T(8,128)(2,1)S(1)}, bf16[512,128]{1,0:T(8,128)(2,1)S(1)}, u32[]{:S(2)}, u32[]{:S(2)}) collective-permute-start(bf16[512,128]{1,0:T(8,128)(2,1)S(1)} %shard_map.94), channel_id=1, source_target_pairs={{0,8},{4,12},{8,0},{12,4},{16,24},{20,28},{24,16},{28,20},{1,9},{5... | collective-permute-start | bytes 393224 | tf_op jit(solution)/shard_map/ppermute | solution.py:265
  28.8 13.2 %collective-permute-start.6 = (bf16[1024,128]{1,0:T(8,128)(2,1)S(1)}, bf16[1024,128]{1,0:T(8,128)(2,1)S(1)}, u32[]{:S(2)}, u32[]{:S(2)}) collective-permute-start(bf16[1024,128]{1,0:T(8,128)(2,1)S(1)} %shard_map.97.refs_0_), channel_id=1, source_target_pairs={{0,2},{1,3},{2,0},{3,1},{4,6},{5,7},{6,4},{7,5},{8,10},{9,11},{10,... | collective-permute-start | bytes 786440 | tf_op jit(solution)/shard_map/ppermute | solution.py:286
  32.3 7.3 %collective-permute-start.2 = (bf16[512,128]{1,0:T(8,128)(2,1)S(1)}, bf16[512,128]{1,0:T(8,128)(2,1)S(1)}, u32[]{:S(2)}, u32[]{:S(2)}) collective-permute-start(bf16[512,128]{1,0:T(8,128)(2,1)S(1)} %shard_map.95), channel_id=1, source_target_pairs={{0,16},{4,20},{8,24},{12,28},{16,0},{20,4},{24,8},{28,12},{1,17},{... | collective-permute-start | bytes 393224 | tf_op jit(solution)/shard_map/ppermute | solution.py:265
  34.6 7.9 %collective-permute-start.7 = (bf16[1024,128]{1,0:T(8,128)(2,1)S(1)}, bf16[1024,128]{1,0:T(8,128)(2,1)S(1)}, u32[]{:S(2)}, u32[]{:S(2)}) collective-permute-start(bf16[1024,128]{1,0:T(8,128)(2,1)S(1)} %shard_map.97.refs_0_), channel_id=1, source_target_pairs={{0,1},{1,0},{2,3},{3,2},{4,5},{5,4},{6,7},{7,6},{8,9},{9,8},{10,11... | collective-permute-start | bytes 786440 | tf_op jit(solution)/shard_map/ppermute | solution.py:286
  34.6 10.3 %collective-permute-start.11 = (bf16[1024,128]{1,0:T(8,128)(2,1)S(1)}, bf16[1024,128]{1,0:T(8,128)(2,1)S(1)}, u32[]{:S(2)}, u32[]{:S(2)}) collective-permute-start(bf16[1024,128]{1,0:T(8,128)(2,1)S(1)} %shard_map.98.refs_4_), channel_id=1, source_target_pairs={{0,2},{1,3},{2,0},{3,1},{4,6},{5,7},{6,4},{7,5},{8,10},{9,11},{10,... | collective-permute-start | bytes 786440 | tf_op jit(solution)/shard_map/ppermute | solution.py:286
  39.8 5.1 %collective-permute-start.3 = (bf16[512,128]{1,0:T(8,128)(2,1)S(1)}, bf16[512,128]{1,0:T(8,128)(2,1)S(1)}, u32[]{:S(2)}, u32[]{:S(2)}) collective-permute-start(bf16[512,128]{1,0:T(8,128)(2,1)S(1)} %get-tuple-element.33), channel_id=1, source_target_pairs={{0,4},{4,0},{8,12},{12,8},{16,20},{20,16},{24,28},{28,24},{1,5},{5... | collective-permute-start | bytes 393224 | tf_op jit(solution)/shard_map/ppermute | solution.py:265
  41.9 6.2 %collective-permute-start.18 = (bf16[1536,128]{1,0:T(8,128)(2,1)S(1)}, bf16[1536,128]{1,0:T(8,128)(2,1)S(1)}, u32[]{:S(2)}, u32[]{:S(2)}) collective-permute-start(bf16[1536,128]{1,0:T(8,128)(2,1)S(1)} %shard_map.99.refs_8_), channel_id=1, source_target_pairs={{0,1},{1,0},{2,3},{3,2},{4,5},{5,4},{6,7},{7,6},{8,9},{9,8},{10,11... | collective-permute-start | bytes 1179656 | tf_op jit(solution)/shard_map/ppermute | solution.py:286
  41.9 6.2 %collective-permute-start.19 = (bf16[1536,128]{1,0:T(8,128)(2,1)S(1)}, bf16[1536,128]{1,0:T(8,128)(2,1)S(1)}, u32[]{:S(2)}, u32[]{:S(2)}) collective-permute-start(bf16[1536,128]{1,0:T(8,128)(2,1)S(1)} %collective-permute-done.17.refs_9_), channel_id=1, source_target_pairs={{0,1},{1,0},{2,3},{3,2},{4,5},{5,4},{6,7},{7,6},{8,9},{9,8},{10,11... | collective-permute-start | bytes 1179656 | tf_op jit(solution)/shard_map/ppermute | solution.py:286
  42.5 5.6 %collective-permute-start.12 = (bf16[1024,128]{1,0:T(8,128)(2,1)S(1)}, bf16[1024,128]{1,0:T(8,128)(2,1)S(1)}, u32[]{:S(2)}, u32[]{:S(2)}) collective-permute-start(bf16[1024,128]{1,0:T(8,128)(2,1)S(1)} %shard_map.98.refs_4_), channel_id=1, source_target_pairs={{0,1},{1,0},{2,3},{3,2},{4,5},{5,4},{6,7},{7,6},{8,9},{9,8},{10,11... | collective-permute-start | bytes 786440 | tf_op jit(solution)/shard_map/ppermute | solution.py:286
  49.7 14.9 %collective-permute-start.21 = (bf16[128,1024]{1,0:T(8,128)(2,1)S(1)}, bf16[128,1024]{1,0:T(8,128)(2,1)S(1)}, u32[]{:S(2)}, u32[]{:S(2)}) collective-permute-start(bf16[128,1024]{1,0:T(8,128)(2,1)S(1)} %get-tuple-element.36), channel_id=1, source_target_pairs={{0,16},{4,20},{8,24},{12,28},{16,0},{20,4},{24,8},{28,12},{1,17},{... | collective-permute-start | bytes 786440 | tf_op jit(solution)/shard_map/ppermute | solution.py:265
  50.6 14.0 %collective-permute-start.20 = (f32[4,128]{1,0:T(4,128)S(1)}, f32[4,128]{1,0:T(4,128)S(1)}, u32[]{:S(2)}, u32[]{:S(2)}) collective-permute-start(f32[4,128]{1,0:T(4,128)S(1)} %get-tuple-element.29.meta_ref), channel_id=1, source_target_pairs={{0,16},{4,20},{8,24},{12,28},{16,0},{20,4},{24,8},{28,12},{1,17},{... | collective-permute-start | bytes 6152 | tf_op jit(solution)/shard_map/ppermute | solution.py:265
  65.1 5.5 %collective-permute-start.22 = (bf16[64,1024]{1,0:T(8,128)(2,1)S(1)}, bf16[64,1024]{1,0:T(8,128)(2,1)S(1)}, u32[]{:S(2)}, u32[]{:S(2)}) collective-permute-start(bf16[64,1024]{1,0:T(8,128)(2,1)S(1)} %get-tuple-element.38), channel_id=1, source_target_pairs={{0,4},{4,0},{8,12},{12,8},{16,20},{20,16},{24,28},{28,24},{1,5},{5... | collective-permute-start | bytes 393224 | tf_op jit(solution)/shard_map/ppermute | solution.py:265
  66.8 6.4 %collective-permute-start.23 = (bf16[64,1024]{1,0:T(8,128)(2,1)S(1)}, bf16[64,1024]{1,0:T(8,128)(2,1)S(1)}, u32[]{:S(2)}, u32[]{:S(2)}) collective-permute-start(bf16[64,1024]{1,0:T(8,128)(2,1)S(1)} %get-tuple-element.39), channel_id=1, source_target_pairs={{0,8},{4,12},{8,0},{12,4},{16,24},{20,28},{24,16},{28,20},{1,9},{5... | collective-permute-start | bytes 393224 | tf_op jit(solution)/shard_map/ppermute | solution.py:265
  66.8 7.7 %collective-permute-start.24 = (bf16[64,1024]{1,0:T(8,128)(2,1)S(1)}, bf16[64,1024]{1,0:T(8,128)(2,1)S(1)}, u32[]{:S(2)}, u32[]{:S(2)}) collective-permute-start(bf16[64,1024]{1,0:T(8,128)(2,1)S(1)} %get-tuple-element.40), channel_id=1, source_target_pairs={{0,12},{4,8},{8,4},{12,0},{16,28},{20,24},{24,20},{28,16},{1,13},{... | collective-permute-start | bytes 393224 | tf_op jit(solution)/shard_map/ppermute | solution.py:265
  75.8 7.2 %collective-permute-start.25 = (bf16[64,1024]{1,0:T(8,128)(2,1)S(1)}, bf16[64,1024]{1,0:T(8,128)(2,1)S(1)}, u32[]{:S(2)}, u32[]{:S(2)}) collective-permute-start(bf16[64,1024]{1,0:T(8,128)(2,1)S(1)} %get-tuple-element.42), channel_id=1, source_target_pairs={{0,4},{4,0},{8,12},{12,8},{16,20},{20,16},{24,28},{28,24},{1,5},{5... | collective-permute-start | bytes 393224 | tf_op jit(solution)/shard_map/ppermute | solution.py:265
  77.5 6.7 %collective-permute-start.26 = (bf16[64,1024]{1,0:T(8,128)(2,1)S(1)}, bf16[64,1024]{1,0:T(8,128)(2,1)S(1)}, u32[]{:S(2)}, u32[]{:S(2)}) collective-permute-start(bf16[64,1024]{1,0:T(8,128)(2,1)S(1)} %get-tuple-element.43), channel_id=1, source_target_pairs={{0,8},{4,12},{8,0},{12,4},{16,24},{20,28},{24,16},{28,20},{1,9},{5... | collective-permute-start | bytes 393224 | tf_op jit(solution)/shard_map/ppermute | solution.py:265
  77.8 8.8 %collective-permute-start.27 = (bf16[64,1024]{1,0:T(8,128)(2,1)S(1)}, bf16[64,1024]{1,0:T(8,128)(2,1)S(1)}, u32[]{:S(2)}, u32[]{:S(2)}) collective-permute-start(bf16[64,1024]{1,0:T(8,128)(2,1)S(1)} %get-tuple-element.44), channel_id=1, source_target_pairs={{0,12},{4,8},{8,4},{12,0},{16,28},{20,24},{24,20},{28,16},{1,13},{... | collective-permute-start | bytes 393224 | tf_op jit(solution)/shard_map/ppermute | solution.py:265
  79.3 10.2 %collective-permute-start.29 = (bf16[64,1024]{1,0:T(8,128)(2,1)S(1)}, bf16[64,1024]{1,0:T(8,128)(2,1)S(1)}, u32[]{:S(2)}, u32[]{:S(2)}) collective-permute-start(bf16[64,1024]{1,0:T(8,128)(2,1)S(1)} %get-tuple-element.46), channel_id=1, source_target_pairs={{0,4},{4,0},{8,12},{12,8},{16,20},{20,16},{24,28},{28,24},{1,5},{5... | collective-permute-start | bytes 393224 | tf_op jit(solution)/shard_map/ppermute | solution.py:265
  81.0 10.4 %collective-permute-start.30 = (bf16[64,1024]{1,0:T(8,128)(2,1)S(1)}, bf16[64,1024]{1,0:T(8,128)(2,1)S(1)}, u32[]{:S(2)}, u32[]{:S(2)}) collective-permute-start(bf16[64,1024]{1,0:T(8,128)(2,1)S(1)} %get-tuple-element.47), channel_id=1, source_target_pairs={{0,8},{4,12},{8,0},{12,4},{16,24},{20,28},{24,16},{28,20},{1,9},{5... | collective-permute-start | bytes 393224 | tf_op jit(solution)/shard_map/ppermute | solution.py:265
  83.0 9.6 %collective-permute-start.31 = (bf16[64,1024]{1,0:T(8,128)(2,1)S(1)}, bf16[64,1024]{1,0:T(8,128)(2,1)S(1)}, u32[]{:S(2)}, u32[]{:S(2)}) collective-permute-start(bf16[64,1024]{1,0:T(8,128)(2,1)S(1)} %get-tuple-element.48), channel_id=1, source_target_pairs={{0,12},{4,8},{8,4},{12,0},{16,28},{20,24},{24,20},{28,16},{1,13},{... | collective-permute-start | bytes 393224 | tf_op jit(solution)/shard_map/ppermute | solution.py:265
  87.1 16.5 %collective-permute-start.28 = (bf16[128,1024]{1,0:T(8,128)(2,1)S(1)}, bf16[128,1024]{1,0:T(8,128)(2,1)S(1)}, u32[]{:S(2)}, u32[]{:S(2)}) collective-permute-start(bf16[128,1024]{1,0:T(8,128)(2,1)S(1)} %shard_map.103), channel_id=1, source_target_pairs={{0,16},{4,20},{8,24},{12,28},{16,0},{20,4},{24,8},{28,12},{1,17},{... | collective-permute-start | bytes 786440 | tf_op jit(solution)/shard_map/ppermute | solution.py:265
  93.8 6.4 %collective-permute-start.32 = (bf16[64,1024]{1,0:T(8,128)(2,1)S(1)}, bf16[64,1024]{1,0:T(8,128)(2,1)S(1)}, u32[]{:S(2)}, u32[]{:S(2)}) collective-permute-start(bf16[64,1024]{1,0:T(8,128)(2,1)S(1)} %get-tuple-element.50), channel_id=1, source_target_pairs={{0,4},{4,0},{8,12},{12,8},{16,20},{20,16},{24,28},{28,24},{1,5},{5... | collective-permute-start | bytes 393224 | tf_op jit(solution)/shard_map/ppermute | solution.py:265
  96.3 5.2 %collective-permute-start.33 = (bf16[64,1024]{1,0:T(8,128)(2,1)S(1)}, bf16[64,1024]{1,0:T(8,128)(2,1)S(1)}, u32[]{:S(2)}, u32[]{:S(2)}) collective-permute-start(bf16[64,1024]{1,0:T(8,128)(2,1)S(1)} %get-tuple-element.51), channel_id=1, source_target_pairs={{0,8},{4,12},{8,0},{12,4},{16,24},{20,28},{24,16},{28,20},{1,9},{5... | collective-permute-start | bytes 393224 | tf_op jit(solution)/shard_map/ppermute | solution.py:265
  96.3 7.3 %collective-permute-start.34 = (bf16[64,1024]{1,0:T(8,128)(2,1)S(1)}, bf16[64,1024]{1,0:T(8,128)(2,1)S(1)}, u32[]{:S(2)}, u32[]{:S(2)}) collective-permute-start(bf16[64,1024]{1,0:T(8,128)(2,1)S(1)} %get-tuple-element.52), channel_id=1, source_target_pairs={{0,12},{4,8},{8,4},{12,0},{16,28},{20,24},{24,20},{28,16},{1,13},{... | collective-permute-start | bytes 393224 | tf_op jit(solution)/shard_map/ppermute | solution.py:265
  (10 other events, 145.3 us)

commit v5 on v4

--- a/solution.py
+++ b/solution.py
@@ -130,15 +130,43 @@
         out[...] = rows[k * cap : (k + 1) * cap, :]
 
 
-def project_body(n, offsets, groups, q_ref, ia_ref, ib_ref, pm_ref, po_ref, wown_ref, res_ref, meta_ref, *refs):
-    copies = len(offsets)
-    packs = [refs[g * copies : (g + 1) * copies] for g in range(len(groups))]
-    refs = refs[len(groups) * copies :]
-    hidden_ref, normed_ref = refs[:2]
-    outs = refs[2 : 2 + n // 2]
-    prefix, att, hid, key_ref = refs[2 + n // 2 :]
+def column_of(n, s, shift):
+    pos = jnp.where(jnp.bitwise_and(s, 1) == 0, s // 2, n - 1 - s // 2)
+    at = lax.rem(pos + shift + n, n)
+    return jnp.where(at < n // 2, 2 * at, 2 * (n - 1 - at) + 1)
+
+
+def columns(n, s, shift, width):
+    return pl.ds(pl.multiple_of(column_of(n, s, shift) * width, width), width)
+
+
+def project_some(n, offsets, groups, packs, att, res_ref, out_ref, at):
     s = lax.axis_index("seq")
     w = lax.axis_index("win")
+    rows = att.shape[1] // len(offsets)
+    width = packs[0].shape[1]
+    parts = [
+        att[:, pl.ds(pl.multiple_of(jnp.bitwise_xor(w, o) * rows, rows), rows)] for o in offsets
+    ]
+    for g, shifts in enumerate(groups):
+        held = packs[g * len(offsets) : (g + 1) * len(offsets)]
+        for i in range(0, len(shifts), 2):
+            some = shifts[i : i + 2]
+            total = None
+            for part, pack in zip(parts, held):
+                m = [pack[(i + o) * rows : (i + o + 1) * rows, :] for o in range(len(some))]
+                r = dot(part, jnp.concatenate(m, axis=1) if len(m) > 1 else m[0])
+                total = r if total is None else total + r
+            for o, shift in enumerate(some):
+                value = total[:, o * width : (o + 1) * width]
+                value = value + res_ref[:, columns(n, s, shift, width)].astype(F32)
+                out_ref[:, at : at + width] = value.astype(BF)
+                at += width
+
+
+def early_body(n, offsets, groups, q_ref, ia_ref, ib_ref, pm_ref, po_ref, wown_ref, res_ref, *refs):
+    packs, att, out_ref, prefix = refs[:-3], refs[-3], refs[-2], refs[-1]
+    s = lax.axis_index("seq")
     y = lax.rem(s, 2)
     length = q_ref.shape[0]
     half = prefix.shape[0] // 2
@@ -155,44 +183,41 @@
         src, at = (ia_ref, p) if p < H // 4 else (ib_ref, p - H // 4)
         intra = src[:, 2 * DV * at : 2 * DV * (at + 1)]
         att[:, cols] = ((intra + inter) * scaling).astype(BF)
-    rows = att.shape[1] // copies
     width = wown_ref.shape[1]
-    parts = [
-        att[:, pl.ds(pl.multiple_of(jnp.bitwise_xor(w, o) * rows, rows), rows)] for o in offsets
-    ]
-    pos = jnp.where(y == 0, s // 2, n - 1 - s // 2)
-
-    def source(shift):
-        at = lax.rem(pos + shift + n, n)
-        return jnp.where(at < n // 2, 2 * at, 2 * (n - 1 - at) + 1)
-
-    def put(shift, value):
-        hid[:, pl.ds(pl.multiple_of(source(shift) * width, width), width)] = value
-
-    put(0, dot(att[...], wown_ref[...]))
-    for shifts, held in zip(groups, packs):
-        for i in range(0, len(shifts), 2):
-            some = shifts[i : i + 2]
-            total = None
-            for part, pack in zip(parts, held):
-                m = [pack[(i + o) * rows : (i + o + 1) * rows, :] for o in range(len(some))]
-                r = dot(part, jnp.concatenate(m, axis=1) if len(m) > 1 else m[0])
-                total = r if total is None else total + r
-            for o, shift in enumerate(some):
-                put(shift, total[:, o * width : (o + 1) * width])
-    hidden = (res_ref[...].astype(F32) + hid[...]).astype(BF)
-    hidden_ref[...] = hidden
-    h = hidden.astype(F32)
-    normed = (h * lax.rsqrt(jnp.mean(h * h, axis=-1, keepdims=True) + 1e-06)).astype(BF)
-    normed_ref[...] = normed
+    own = dot(att[...], wown_ref[...]) + res_ref[:, columns(n, s, 0, width)].astype(F32)
+    out_ref[:, :width] = own.astype(BF)
+    project_some(n, offsets, groups, packs, att, res_ref, out_ref, width)
+
+
+def assemble(n, s, shifts, first, second, hid):
+    width = hid.shape[1] // n
+    cut = first.shape[1] // width
+    for i, shift in enumerate(shifts):
+        src, at = (first, i) if i < cut else (second, i - cut)
+        hid[:, columns(n, s, shift, width)] = src[:, at * width : (at + 1) * width].astype(F32)
+    h = hid[...]
+    return h, (h * lax.rsqrt(jnp.mean(h * h, axis=-1, keepdims=True) + 1e-06)).astype(BF)
+
+
+def late_body(n, offsets, groups, shifts, att_ref, first_ref, res_ref, meta_ref, *refs):
+    near = n // 2
+    packs, refs = refs[: len(groups) * len(offsets)], refs[len(groups) * len(offsets) :]
+    second_ref, hidden_ref = refs[:2]
+    outs = refs[2 : 2 + near]
+    hid, key_ref = refs[2 + near :]
+    project_some(n, offsets, groups, packs, att_ref, res_ref, second_ref, 0)
+    h, normed = assemble(n, lax.axis_index("seq"), shifts, first_ref, second_ref, hid)
+    hidden_ref[...] = h.astype(BF)
     key_ref[...] = keys_of(meta_ref[...], n)[0]
     deal(key_ref, normed, outs, outs[0].shape[0])
 
 
-def deal_body(n, normed_ref, meta_ref, *refs):
-    outs, key_ref = refs[:-1], refs[-1]
+def deal_body(n, shifts, first_ref, second_ref, meta_ref, *refs):
+    outs, hid, key_ref = refs[:-2], refs[-2], refs[-1]
     key_ref[...] = keys_of(meta_ref[...], n)[0]
-    deal(key_ref, normed_ref[...], outs, outs[0].shape[0])
+    sender = jnp.bitwise_xor(lax.axis_index("seq"), n // 2)
+    normed = assemble(n, sender, shifts, first_ref, second_ref, hid)[1]
+    deal(key_ref, normed, outs, outs[0].shape[0])
 
 
 def expert_body(parts, win_ref, wout_ref, *refs):
@@ -340,21 +365,33 @@
     row_buf = sds((cap, D), BF)
     full = sds((length, D), BF)
     keys = pltpu.VMEM((n, length), F32)
-    hidden, normed, *deal_own = kernel(
-        functools.partial(project_body, n, offsets, groups),
-        (full, full, *[row_buf] * near),
-        (queries, *intra, prefix_mine, prefix_other, out_weight, residual, meta, *packs),
-        [
-            pltpu.VMEM((2 * half, DV), BF),
-            pltpu.VMEM((length, H * DV), BF),
-            pltpu.VMEM((length, D), F32),
-            keys,
-        ],
-    )
-    normed_far = flip(normed, near)
+    early, late = groups[:-1], groups[-1:]
+    ahead_packs, last_packs = packs[:-copies], packs[-copies:]
+    shifts = [0] + [x for g in groups for x in g]
+    left = len(groups[-1])
+    some = sds((length, (n - left) * width), BF)
+    rest = sds((length, left * width), BF)
+    whole = pltpu.VMEM((length, D), F32)
+    att, first = kernel(
+        functools.partial(early_body, n, offsets, early),
+        (sds((length, H * DV), BF), some),
+        (queries, *intra, prefix_mine, prefix_other, out_weight, residual, *ahead_packs),
+        [pltpu.VMEM((2 * half, DV), BF)],
+    )
+    first_far = flip(first, near)
+    second, hidden, *deal_own = kernel(
+        functools.partial(late_body, n, offsets, late, shifts),
+        (rest, full, *[row_buf] * near),
+        (att, first, residual, meta, *last_packs),
+        [whole, keys],
+    )
+    second_far = flip(second, near)
     own_in = flips(deal_own)
     deal_far = kernel(
-        functools.partial(deal_body, n), tuple([row_buf] * near), (normed_far, meta_far), [keys]
+        functools.partial(deal_body, n, shifts),
+        tuple([row_buf] * near),
+        (first_far, second_far, meta_far),
+        [whole, keys],
     )
     far_in = flips(deal_far)
 

time: 105 us -> 104 us (level)
  waiting for transfers between devices: 52.8 us -> 51 us
    ppermute x19 -> x20, waiting for transfers between devices: 40 us -> 38.3 us  [flip(): return lax.ppermute(x, 'seq', [(i, i ^ k) for i in range(n)])]
    ppermute x19 -> x20, starting transfers between devices: 26.7 us -> 27.5 us  [flip(): return lax.ppermute(x, 'seq', [(i, i ^ k) for i in range(n)])]
    pallas_call x15 -> x16, Pallas kernels: 11 us -> 11.1 us  [call(): run(*[pltpu.with_memory_space_constraint(x, m) for x, m in zip(xs, spaces)])]
  transfers between devices with their start and end apart: 35 -> 36, of which waited for: 18 -> 18; matrix products, arithmetic and copies ran while one was open for 0% -> 0% of each run, Pallas kernels for 4% -> 6%
where the time goes in v5:
time: 104 us
  waiting for transfers between devices  51 us (49%)
  starting transfers between devices  41.7 us (40%)
  Pallas kernels  11.1 us (11%)
    ppermute x20, waiting for transfers between devices, flip(): return lax.ppermute(x, 'seq', [(i, i ^ k) for i in range(n)])  38.3 us
    ppermute x20, starting transfers between devices, flip(): return lax.ppermute(x, 'seq', [(i, i ^ k) for i in range(n)])  27.5 us
    ppermute x4, waiting for transfers between devices, small_group(): f = lax.ppermute(f, 'seq', ahead)  12.7 us
    pallas_call x16, Pallas kernels, call(): run(*[pltpu.with_memory_space_constraint(x, m) for x, m in zip(xs, spaces)])  11.1 us
    ppermute x4, starting transfers between devices, small_group(): f = lax.ppermute(f, 'seq', ahead)  8.73 us
    ppermute x9, starting transfers between devices, share(): held = held + [lax.ppermute(h, 'win', pairs) for h in held]  4.91 us
  transfers between devices with their start and end apart: 36, of which 18 were waited for; matrix products, arithmetic and copies ran while one was open for 0% of the time, Pallas kernels for 6%

profile of v5, /device:TPU:0, one launch (start us, length us, event | category | flops | bytes accessed | tf_op | source)
XLA Modules:
  0.0 104.1 jit_solution(13724934353999934305)
XLA Ops:
  0.0 2.0 %shard_map.91 = (f32[512,128]{1,0:T(8,128)S(1)}, bf16[512,128]{1,0:T(8,128)(2,1)S(1)}, f32[4,128]{1,0:T(4,128)S(1)}, bf16[512,128]{1,0:T(8,128)(2,1)S(1)}) custom-call(bf16[128,1024]{1,0:T(8,128)(2,1)} %k_ref.5, bf16[128,2048]{1,0:T(8,128)(2,1)} %v_ref.5, s32[2,128]{1,0:T(2,128)} %bitcast.2, f32[2,128]{1,0:T(2,128)} %bitcast.3, bf16[2048,128]{1,0:T(8,128)(2,1)} %wown_ref.1), custom_call_target="tpu_custom_call" | custom-call | tf_op jit(solution)/shard_map/pallas_call | solution.py:34
  2.1 3.1 %collective-permute-start.4 = (bf16[512,128]{1,0:T(8,128)(2,1)S(1)}, bf16[512,128]{1,0:T(8,128)(2,1)S(1)}, u32[]{:S(2)}, u32[]{:S(2)}) collective-permute-start(bf16[512,128]{1,0:T(8,128)(2,1)S(1)} %get-tuple-element.36), channel_id=1, source_target_pairs={{0,8},{8,16},{16,24},{24,28},{28,20},{20,12},{12,4},{4,0},{1,9},{9... | collective-permute-start | bytes 393224 | tf_op jit(solution)/shard_map/ppermute | solution.py:341
  5.2 3.4 %collective-permute-done.4.refs_0_ = bf16[512,128]{1,0:T(8,128)(2,1)S(1)} collective-permute-done((bf16[512,128]{1,0:T(8,128)(2,1)S(1)}, bf16[512,128]{1,0:T(8,128)(2,1)S(1)}, u32[]{:S(2)}, u32[]{:S(2)}) %collective-permute-start.4) | collective-permute-done | bytes 131104 | tf_op jit(solution)/shard_map/ppermute | solution.py:341
  8.6 1.8 %collective-permute-start.9 = (bf16[512,128]{1,0:T(8,128)(2,1)S(1)}, bf16[512,128]{1,0:T(8,128)(2,1)S(1)}, u32[]{:S(2)}, u32[]{:S(2)}) collective-permute-start(bf16[512,128]{1,0:T(8,128)(2,1)S(1)} %collective-permute-done.4.refs_0_), channel_id=1, source_target_pairs={{0,8},{8,16},{16,24},{24,28},{28,20},{20,12},{12,4},{4,0},{1,9},{9... | collective-permute-start | bytes 393224 | tf_op jit(solution)/shard_map/ppermute | solution.py:341
  10.6 2.9 %collective-permute-done.9.refs_0_ = bf16[512,128]{1,0:T(8,128)(2,1)S(1)} collective-permute-done((bf16[512,128]{1,0:T(8,128)(2,1)S(1)}, bf16[512,128]{1,0:T(8,128)(2,1)S(1)}, u32[]{:S(2)}, u32[]{:S(2)}) %collective-permute-start.9) | collective-permute-done | bytes 131104 | tf_op jit(solution)/shard_map/ppermute | solution.py:341
  13.6 1.8 %collective-permute-start.14 = (bf16[512,128]{1,0:T(8,128)(2,1)S(1)}, bf16[512,128]{1,0:T(8,128)(2,1)S(1)}, u32[]{:S(2)}, u32[]{:S(2)}) collective-permute-start(bf16[512,128]{1,0:T(8,128)(2,1)S(1)} %collective-permute-done.9.refs_0_), channel_id=1, source_target_pairs={{0,8},{8,16},{16,24},{24,28},{28,20},{20,12},{12,4},{4,0},{1,9},{9... | collective-permute-start | bytes 393224 | tf_op jit(solution)/shard_map/ppermute | solution.py:341
  15.6 3.4 %collective-permute-done.14.refs_0_ = bf16[512,128]{1,0:T(8,128)(2,1)S(1)} collective-permute-done((bf16[512,128]{1,0:T(8,128)(2,1)S(1)}, bf16[512,128]{1,0:T(8,128)(2,1)S(1)}, u32[]{:S(2)}, u32[]{:S(2)}) %collective-permute-start.14) | collective-permute-done | bytes 131104 | tf_op jit(solution)/shard_map/ppermute | solution.py:341
  19.0 2.0 %collective-permute-start.16 = (bf16[512,128]{1,0:T(8,128)(2,1)S(1)}, bf16[512,128]{1,0:T(8,128)(2,1)S(1)}, u32[]{:S(2)}, u32[]{:S(2)}) collective-permute-start(bf16[512,128]{1,0:T(8,128)(2,1)S(1)} %collective-permute-done.14.refs_0_), channel_id=1, source_target_pairs={{0,8},{8,16},{16,24},{24,28},{28,20},{20,12},{12,4},{4,0},{1,9},{9... | collective-permute-start | bytes 393224 | tf_op jit(solution)/shard_map/ppermute | solution.py:341
  21.0 2.9 %collective-permute-done.16.refs_2_ = bf16[512,128]{1,0:T(8,128)(2,1)S(1)} collective-permute-done((bf16[512,128]{1,0:T(8,128)(2,1)S(1)}, bf16[512,128]{1,0:T(8,128)(2,1)S(1)}, u32[]{:S(2)}, u32[]{:S(2)}) %collective-permute-start.16) | collective-permute-done | bytes 131104 | tf_op jit(solution)/shard_map/ppermute | solution.py:341
  24.0 2.1 %collective-permute-start.17 = (bf16[1536,128]{1,0:T(8,128)(2,1)S(1)}, bf16[1536,128]{1,0:T(8,128)(2,1)S(1)}, u32[]{:S(2)}, u32[]{:S(2)}) collective-permute-start(bf16[1536,128]{1,0:T(8,128)(2,1)S(1)} %shard_map.100.refs_0_), channel_id=1, source_target_pairs={{0,2},{1,3},{2,0},{3,1},{4,6},{5,7},{6,4},{7,5},{8,10},{9,11},{10,... | collective-permute-start | bytes 1179656 | tf_op jit(solution)/shard_map/ppermute | solution.py:311
  26.2 2.5 %collective-permute-start.1 = (bf16[512,128]{1,0:T(8,128)(2,1)S(1)}, bf16[512,128]{1,0:T(8,128)(2,1)S(1)}, u32[]{:S(2)}, u32[]{:S(2)}) collective-permute-start(bf16[512,128]{1,0:T(8,128)(2,1)S(1)} %shard_map.94), channel_id=1, source_target_pairs={{0,8},{4,12},{8,0},{12,4},{16,24},{20,28},{24,16},{28,20},{1,9},{5... | collective-permute-start | bytes 393224 | tf_op jit(solution)/shard_map/ppermute | solution.py:290
  29.2 3.0 %collective-permute-done.1.refs_1_.refs_0_ = bf16[512,128]{1,0:T(8,128)(2,1)S(1)} collective-permute-done((bf16[512,128]{1,0:T(8,128)(2,1)S(1)}, bf16[512,128]{1,0:T(8,128)(2,1)S(1)}, u32[]{:S(2)}, u32[]{:S(2)}) %collective-permute-start.1) | collective-permute-done | bytes 131104 | tf_op jit(solution)/shard_map/ppermute | solution.py:290
  32.3 2.3 %collective-permute-start.2 = (bf16[512,128]{1,0:T(8,128)(2,1)S(1)}, bf16[512,128]{1,0:T(8,128)(2,1)S(1)}, u32[]{:S(2)}, u32[]{:S(2)}) collective-permute-start(bf16[512,128]{1,0:T(8,128)(2,1)S(1)} %shard_map.95), channel_id=1, source_target_pairs={{0,16},{4,20},{8,24},{12,28},{16,0},{20,4},{24,8},{28,12},{1,17},{... | collective-permute-start | bytes 393224 | tf_op jit(solution)/shard_map/ppermute | solution.py:290
  35.8 3.8 %collective-permute-done.2.refs_1_ = bf16[512,128]{1,0:T(8,128)(2,1)S(1)} collective-permute-done((bf16[512,128]{1,0:T(8,128)(2,1)S(1)}, bf16[512,128]{1,0:T(8,128)(2,1)S(1)}, u32[]{:S(2)}, u32[]{:S(2)}) %collective-permute-start.2) | collective-permute-done | bytes 131104 | tf_op jit(solution)/shard_map/ppermute | solution.py:290
  39.8 2.2 %collective-permute-start.3 = (bf16[512,128]{1,0:T(8,128)(2,1)S(1)}, bf16[512,128]{1,0:T(8,128)(2,1)S(1)}, u32[]{:S(2)}, u32[]{:S(2)}) collective-permute-start(bf16[512,128]{1,0:T(8,128)(2,1)S(1)} %get-tuple-element.35), channel_id=1, source_target_pairs={{0,4},{4,0},{8,12},{12,8},{16,20},{20,16},{24,28},{28,24},{1,5},{5... | collective-permute-start | bytes 393224 | tf_op jit(solution)/shard_map/ppermute | solution.py:290
  42.5 2.4 %collective-permute-done.3.po_ref = bf16[512,128]{1,0:T(8,128)(2,1)S(1)} collective-permute-done((bf16[512,128]{1,0:T(8,128)(2,1)S(1)}, bf16[512,128]{1,0:T(8,128)(2,1)S(1)}, u32[]{:S(2)}, u32[]{:S(2)}) %collective-permute-start.3) | collective-permute-done | bytes 131104 | tf_op jit(solution)/shard_map/ppermute | solution.py:290
  50.6 2.2 %collective-permute-start.22 = (bf16[128,384]{1,0:T(8,128)(2,1)S(1)}, bf16[128,384]{1,0:T(8,128)(2,1)S(1)}, u32[]{:S(2)}, u32[]{:S(2)}) collective-permute-start(bf16[128,384]{1,0:T(8,128)(2,1)S(1)} %get-tuple-element.40), channel_id=1, source_target_pairs={{0,16},{4,20},{8,24},{12,28},{16,0},{20,4},{24,8},{28,12},{1,17},{... | collective-permute-start | bytes 294920 | tf_op jit(solution)/shard_map/ppermute | solution.py:290
  53.6 10.2 %collective-permute-done.20.meta_ref = f32[4,128]{1,0:T(4,128)S(1)} collective-permute-done((f32[4,128]{1,0:T(4,128)S(1)}, f32[4,128]{1,0:T(4,128)S(1)}, u32[]{:S(2)}, u32[]{:S(2)}) %collective-permute-start.20) | collective-permute-done | bytes 2080 | tf_op jit(solution)/shard_map/ppermute | solution.py:290
  64.3 1.8 %collective-permute-start.23 = (bf16[64,1024]{1,0:T(8,128)(2,1)S(1)}, bf16[64,1024]{1,0:T(8,128)(2,1)S(1)}, u32[]{:S(2)}, u32[]{:S(2)}) collective-permute-start(bf16[64,1024]{1,0:T(8,128)(2,1)S(1)} %get-tuple-element.42), channel_id=1, source_target_pairs={{0,4},{4,0},{8,12},{12,8},{16,20},{20,16},{24,28},{28,24},{1,5},{5... | collective-permute-start | bytes 393224 | tf_op jit(solution)/shard_map/ppermute | solution.py:290
  66.1 1.8 %collective-permute-start.25 = (bf16[64,1024]{1,0:T(8,128)(2,1)S(1)}, bf16[64,1024]{1,0:T(8,128)(2,1)S(1)}, u32[]{:S(2)}, u32[]{:S(2)}) collective-permute-start(bf16[64,1024]{1,0:T(8,128)(2,1)S(1)} %get-tuple-element.44), channel_id=1, source_target_pairs={{0,12},{4,8},{8,4},{12,0},{16,28},{20,24},{24,20},{28,16},{1,13},{... | collective-permute-start | bytes 393224 | tf_op jit(solution)/shard_map/ppermute | solution.py:290
  67.9 1.9 %collective-permute-done.23.refs_1_ = bf16[64,1024]{1,0:T(8,128)(2,1)S(1)} collective-permute-done((bf16[64,1024]{1,0:T(8,128)(2,1)S(1)}, bf16[64,1024]{1,0:T(8,128)(2,1)S(1)}, u32[]{:S(2)}, u32[]{:S(2)}) %collective-permute-start.23) | collective-permute-done | bytes 131104 | tf_op jit(solution)/shard_map/ppermute | solution.py:290
  69.8 2.7 %collective-permute-done.24.refs_2_ = bf16[64,1024]{1,0:T(8,128)(2,1)S(1)} collective-permute-done((bf16[64,1024]{1,0:T(8,128)(2,1)S(1)}, bf16[64,1024]{1,0:T(8,128)(2,1)S(1)}, u32[]{:S(2)}, u32[]{:S(2)}) %collective-permute-start.24) | collective-permute-done | bytes 131104 | tf_op jit(solution)/shard_map/ppermute | solution.py:290
  75.0 1.7 %collective-permute-start.26 = (bf16[64,1024]{1,0:T(8,128)(2,1)S(1)}, bf16[64,1024]{1,0:T(8,128)(2,1)S(1)}, u32[]{:S(2)}, u32[]{:S(2)}) collective-permute-start(bf16[64,1024]{1,0:T(8,128)(2,1)S(1)} %get-tuple-element.46), channel_id=1, source_target_pairs={{0,4},{4,0},{8,12},{12,8},{16,20},{20,16},{24,28},{28,24},{1,5},{5... | collective-permute-start | bytes 393224 | tf_op jit(solution)/shard_map/ppermute | solution.py:290
  78.6 1.7 %collective-permute-start.30 = (bf16[64,1024]{1,0:T(8,128)(2,1)S(1)}, bf16[64,1024]{1,0:T(8,128)(2,1)S(1)}, u32[]{:S(2)}, u32[]{:S(2)}) collective-permute-start(bf16[64,1024]{1,0:T(8,128)(2,1)S(1)} %get-tuple-element.50), channel_id=1, source_target_pairs={{0,4},{4,0},{8,12},{12,8},{16,20},{20,16},{24,28},{28,24},{1,5},{5... | collective-permute-start | bytes 393224 | tf_op jit(solution)/shard_map/ppermute | solution.py:290
  80.5 1.7 %collective-permute-done.26.refs_1_ = bf16[64,1024]{1,0:T(8,128)(2,1)S(1)} collective-permute-done((bf16[64,1024]{1,0:T(8,128)(2,1)S(1)}, bf16[64,1024]{1,0:T(8,128)(2,1)S(1)}, u32[]{:S(2)}, u32[]{:S(2)}) %collective-permute-start.26) | collective-permute-done | bytes 131104 | tf_op jit(solution)/shard_map/ppermute | solution.py:290
  83.4 2.4 %collective-permute-done.28.refs_3_ = bf16[64,1024]{1,0:T(8,128)(2,1)S(1)} collective-permute-done((bf16[64,1024]{1,0:T(8,128)(2,1)S(1)}, bf16[64,1024]{1,0:T(8,128)(2,1)S(1)}, u32[]{:S(2)}, u32[]{:S(2)}) %collective-permute-start.28) | collective-permute-done | bytes 131104 | tf_op jit(solution)/shard_map/ppermute | solution.py:290
  86.3 2.5 %collective-permute-start.29 = (bf16[128,1024]{1,0:T(8,128)(2,1)S(1)}, bf16[128,1024]{1,0:T(8,128)(2,1)S(1)}, u32[]{:S(2)}, u32[]{:S(2)}) collective-permute-start(bf16[128,1024]{1,0:T(8,128)(2,1)S(1)} %shard_map.104), channel_id=1, source_target_pairs={{0,16},{4,20},{8,24},{12,28},{16,0},{20,4},{24,8},{28,12},{1,17},{... | collective-permute-start | bytes 786440 | tf_op jit(solution)/shard_map/ppermute | solution.py:290
  88.8 1.8 %collective-permute-done.31.refs_2_ = bf16[64,1024]{1,0:T(8,128)(2,1)S(1)} collective-permute-done((bf16[64,1024]{1,0:T(8,128)(2,1)S(1)}, bf16[64,1024]{1,0:T(8,128)(2,1)S(1)}, u32[]{:S(2)}, u32[]{:S(2)}) %collective-permute-start.31) | collective-permute-done | bytes 131104 | tf_op jit(solution)/shard_map/ppermute | solution.py:290
  93.1 2.5 %collective-permute-start.33 = (bf16[64,1024]{1,0:T(8,128)(2,1)S(1)}, bf16[64,1024]{1,0:T(8,128)(2,1)S(1)}, u32[]{:S(2)}, u32[]{:S(2)}) collective-permute-start(bf16[64,1024]{1,0:T(8,128)(2,1)S(1)} %get-tuple-element.54), channel_id=1, source_target_pairs={{0,4},{4,0},{8,12},{12,8},{16,20},{20,16},{24,28},{28,24},{1,5},{5... | collective-permute-start | bytes 393224 | tf_op jit(solution)/shard_map/ppermute | solution.py:290
  95.6 1.5 %collective-permute-start.35 = (bf16[64,1024]{1,0:T(8,128)(2,1)S(1)}, bf16[64,1024]{1,0:T(8,128)(2,1)S(1)}, u32[]{:S(2)}, u32[]{:S(2)}) collective-permute-start(bf16[64,1024]{1,0:T(8,128)(2,1)S(1)} %get-tuple-element.56), channel_id=1, source_target_pairs={{0,12},{4,8},{8,4},{12,0},{16,28},{20,24},{24,20},{28,16},{1,13},{... | collective-permute-start | bytes 393224 | tf_op jit(solution)/shard_map/ppermute | solution.py:290
  97.1 2.3 %collective-permute-done.33.refs_1_ = bf16[64,1024]{1,0:T(8,128)(2,1)S(1)} collective-permute-done((bf16[64,1024]{1,0:T(8,128)(2,1)S(1)}, bf16[64,1024]{1,0:T(8,128)(2,1)S(1)}, u32[]{:S(2)}, u32[]{:S(2)}) %collective-permute-start.33) | collective-permute-done | bytes 131104 | tf_op jit(solution)/shard_map/ppermute | solution.py:290
  100.7 2.1 %collective-permute-done.35.refs_3_ = bf16[64,1024]{1,0:T(8,128)(2,1)S(1)} collective-permute-done((bf16[64,1024]{1,0:T(8,128)(2,1)S(1)}, bf16[64,1024]{1,0:T(8,128)(2,1)S(1)}, u32[]{:S(2)}, u32[]{:S(2)}) %collective-permute-start.35) | collective-permute-done | bytes 131104 | tf_op jit(solution)/shard_map/ppermute | solution.py:290
  (70 shorter events, 21.1 us)
Async XLA Ops:
  2.1 6.5 %collective-permute-start.4 = (bf16[512,128]{1,0:T(8,128)(2,1)S(1)}, bf16[512,128]{1,0:T(8,128)(2,1)S(1)}, u32[]{:S(2)}, u32[]{:S(2)}) collective-permute-start(bf16[512,128]{1,0:T(8,128)(2,1)S(1)} %get-tuple-element.36), channel_id=1, source_target_pairs={{0,8},{8,16},{16,24},{24,28},{28,20},{20,12},{12,4},{4,0},{1,9},{9... | collective-permute-start | bytes 393224 | tf_op jit(solution)/shard_map/ppermute | solution.py:341
  5.2 5.2 %collective-permute-start.5 = (bf16[512,128]{1,0:T(8,128)(2,1)S(1)}, bf16[512,128]{1,0:T(8,128)(2,1)S(1)}, u32[]{:S(2)}, u32[]{:S(2)}) collective-permute-start(bf16[512,128]{1,0:T(8,128)(2,1)S(1)} %get-tuple-element.36), channel_id=1, source_target_pairs={{8,0},{16,8},{24,16},{28,24},{20,28},{12,20},{4,12},{0,4},{9,1},{1... | collective-permute-start | bytes 393224 | tf_op jit(solution)/shard_map/ppermute | solution.py:344
  10.4 5.0 %collective-permute-start.10 = (bf16[512,128]{1,0:T(8,128)(2,1)S(1)}, bf16[512,128]{1,0:T(8,128)(2,1)S(1)}, u32[]{:S(2)}, u32[]{:S(2)}) collective-permute-start(bf16[512,128]{1,0:T(8,128)(2,1)S(1)} %collective-permute-done.5.refs_1_), channel_id=1, source_target_pairs={{8,0},{16,8},{24,16},{28,24},{20,28},{12,20},{4,12},{0,4},{9,1},{1... | collective-permute-start | bytes 393224 | tf_op jit(solution)/shard_map/ppermute | solution.py:344
  13.6 5.4 %collective-permute-start.14 = (bf16[512,128]{1,0:T(8,128)(2,1)S(1)}, bf16[512,128]{1,0:T(8,128)(2,1)S(1)}, u32[]{:S(2)}, u32[]{:S(2)}) collective-permute-start(bf16[512,128]{1,0:T(8,128)(2,1)S(1)} %collective-permute-done.9.refs_0_), channel_id=1, source_target_pairs={{0,8},{8,16},{16,24},{24,28},{28,20},{20,12},{12,4},{4,0},{1,9},{9... | collective-permute-start | bytes 393224 | tf_op jit(solution)/shard_map/ppermute | solution.py:341
  15.4 5.6 %collective-permute-start.15 = (bf16[512,128]{1,0:T(8,128)(2,1)S(1)}, bf16[512,128]{1,0:T(8,128)(2,1)S(1)}, u32[]{:S(2)}, u32[]{:S(2)}) collective-permute-start(bf16[512,128]{1,0:T(8,128)(2,1)S(1)} %collective-permute-done.10.refs_1_), channel_id=1, source_target_pairs={{8,0},{16,8},{24,16},{28,24},{20,28},{12,20},{4,12},{0,4},{9,1},{1... | collective-permute-start | bytes 393224 | tf_op jit(solution)/shard_map/ppermute | solution.py:344
  21.0 5.2 %collective-permute-start = (bf16[512,128]{1,0:T(8,128)(2,1)S(1)}, bf16[512,128]{1,0:T(8,128)(2,1)S(1)}, u32[]{:S(2)}, u32[]{:S(2)}) collective-permute-start(bf16[512,128]{1,0:T(8,128)(2,1)S(1)} %get-tuple-element.33), channel_id=1, source_target_pairs={{0,4},{4,0},{8,12},{12,8},{16,20},{20,16},{24,28},{28,24},{1,5},{5... | collective-permute-start | bytes 393224 | tf_op jit(solution)/shard_map/ppermute | solution.py:290
  24.0 17.9 %collective-permute-start.17 = (bf16[1536,128]{1,0:T(8,128)(2,1)S(1)}, bf16[1536,128]{1,0:T(8,128)(2,1)S(1)}, u32[]{:S(2)}, u32[]{:S(2)}) collective-permute-start(bf16[1536,128]{1,0:T(8,128)(2,1)S(1)} %shard_map.100.refs_0_), channel_id=1, source_target_pairs={{0,2},{1,3},{2,0},{3,1},{4,6},{5,7},{6,4},{7,5},{8,10},{9,11},{10,... | collective-permute-start | bytes 1179656 | tf_op jit(solution)/shard_map/ppermute | solution.py:311
  26.2 6.1 %collective-permute-start.1 = (bf16[512,128]{1,0:T(8,128)(2,1)S(1)}, bf16[512,128]{1,0:T(8,128)(2,1)S(1)}, u32[]{:S(2)}, u32[]{:S(2)}) collective-permute-start(bf16[512,128]{1,0:T(8,128)(2,1)S(1)} %shard_map.94), channel_id=1, source_target_pairs={{0,8},{4,12},{8,0},{12,4},{16,24},{20,28},{24,16},{28,20},{1,9},{5... | collective-permute-start | bytes 393224 | tf_op jit(solution)/shard_map/ppermute | solution.py:290
  28.8 13.2 %collective-permute-start.6 = (bf16[1024,128]{1,0:T(8,128)(2,1)S(1)}, bf16[1024,128]{1,0:T(8,128)(2,1)S(1)}, u32[]{:S(2)}, u32[]{:S(2)}) collective-permute-start(bf16[1024,128]{1,0:T(8,128)(2,1)S(1)} %shard_map.97.refs_0_), channel_id=1, source_target_pairs={{0,2},{1,3},{2,0},{3,1},{4,6},{5,7},{6,4},{7,5},{8,10},{9,11},{10,... | collective-permute-start | bytes 786440 | tf_op jit(solution)/shard_map/ppermute | solution.py:311
  32.3 7.3 %collective-permute-start.2 = (bf16[512,128]{1,0:T(8,128)(2,1)S(1)}, bf16[512,128]{1,0:T(8,128)(2,1)S(1)}, u32[]{:S(2)}, u32[]{:S(2)}) collective-permute-start(bf16[512,128]{1,0:T(8,128)(2,1)S(1)} %shard_map.95), channel_id=1, source_target_pairs={{0,16},{4,20},{8,24},{12,28},{16,0},{20,4},{24,8},{28,12},{1,17},{... | collective-permute-start | bytes 393224 | tf_op jit(solution)/shard_map/ppermute | solution.py:290
  34.6 7.9 %collective-permute-start.7 = (bf16[1024,128]{1,0:T(8,128)(2,1)S(1)}, bf16[1024,128]{1,0:T(8,128)(2,1)S(1)}, u32[]{:S(2)}, u32[]{:S(2)}) collective-permute-start(bf16[1024,128]{1,0:T(8,128)(2,1)S(1)} %shard_map.97.refs_0_), channel_id=1, source_target_pairs={{0,1},{1,0},{2,3},{3,2},{4,5},{5,4},{6,7},{7,6},{8,9},{9,8},{10,11... | collective-permute-start | bytes 786440 | tf_op jit(solution)/shard_map/ppermute | solution.py:311
  34.6 10.3 %collective-permute-start.11 = (bf16[1024,128]{1,0:T(8,128)(2,1)S(1)}, bf16[1024,128]{1,0:T(8,128)(2,1)S(1)}, u32[]{:S(2)}, u32[]{:S(2)}) collective-permute-start(bf16[1024,128]{1,0:T(8,128)(2,1)S(1)} %shard_map.98.refs_4_), channel_id=1, source_target_pairs={{0,2},{1,3},{2,0},{3,1},{4,6},{5,7},{6,4},{7,5},{8,10},{9,11},{10,... | collective-permute-start | bytes 786440 | tf_op jit(solution)/shard_map/ppermute | solution.py:311
  39.8 5.1 %collective-permute-start.3 = (bf16[512,128]{1,0:T(8,128)(2,1)S(1)}, bf16[512,128]{1,0:T(8,128)(2,1)S(1)}, u32[]{:S(2)}, u32[]{:S(2)}) collective-permute-start(bf16[512,128]{1,0:T(8,128)(2,1)S(1)} %get-tuple-element.35), channel_id=1, source_target_pairs={{0,4},{4,0},{8,12},{12,8},{16,20},{20,16},{24,28},{28,24},{1,5},{5... | collective-permute-start | bytes 393224 | tf_op jit(solution)/shard_map/ppermute | solution.py:290
  41.9 7.8 %collective-permute-start.18 = (bf16[1536,128]{1,0:T(8,128)(2,1)S(1)}, bf16[1536,128]{1,0:T(8,128)(2,1)S(1)}, u32[]{:S(2)}, u32[]{:S(2)}) collective-permute-start(bf16[1536,128]{1,0:T(8,128)(2,1)S(1)} %shard_map.100.refs_0_), channel_id=1, source_target_pairs={{0,1},{1,0},{2,3},{3,2},{4,5},{5,4},{6,7},{7,6},{8,9},{9,8},{10,11... | collective-permute-start | bytes 1179656 | tf_op jit(solution)/shard_map/ppermute | solution.py:311
  41.9 7.8 %collective-permute-start.19 = (bf16[1536,128]{1,0:T(8,128)(2,1)S(1)}, bf16[1536,128]{1,0:T(8,128)(2,1)S(1)}, u32[]{:S(2)}, u32[]{:S(2)}) collective-permute-start(bf16[1536,128]{1,0:T(8,128)(2,1)S(1)} %collective-permute-done.17.refs_1_), channel_id=1, source_target_pairs={{0,1},{1,0},{2,3},{3,2},{4,5},{5,4},{6,7},{7,6},{8,9},{9,8},{10,11... | collective-permute-start | bytes 1179656 | tf_op jit(solution)/shard_map/ppermute | solution.py:311
  42.5 5.6 %collective-permute-start.12 = (bf16[1024,128]{1,0:T(8,128)(2,1)S(1)}, bf16[1024,128]{1,0:T(8,128)(2,1)S(1)}, u32[]{:S(2)}, u32[]{:S(2)}) collective-permute-start(bf16[1024,128]{1,0:T(8,128)(2,1)S(1)} %shard_map.98.refs_4_), channel_id=1, source_target_pairs={{0,1},{1,0},{2,3},{3,2},{4,5},{5,4},{6,7},{7,6},{8,9},{9,8},{10,11... | collective-permute-start | bytes 786440 | tf_op jit(solution)/shard_map/ppermute | solution.py:311
  48.9 14.9 %collective-permute-start.21 = (bf16[128,640]{1,0:T(8,128)(2,1)S(1)}, bf16[128,640]{1,0:T(8,128)(2,1)S(1)}, u32[]{:S(2)}, u32[]{:S(2)}) collective-permute-start(bf16[128,640]{1,0:T(8,128)(2,1)S(1)} %get-tuple-element.38.first_ref), channel_id=1, source_target_pairs={{0,16},{4,20},{8,24},{12,28},{16,0},{20,4},{24,8},{28,12},{1,17},{... | collective-permute-start | bytes 491528 | tf_op jit(solution)/shard_map/ppermute | solution.py:290
  50.6 13.2 %collective-permute-start.22 = (bf16[128,384]{1,0:T(8,128)(2,1)S(1)}, bf16[128,384]{1,0:T(8,128)(2,1)S(1)}, u32[]{:S(2)}, u32[]{:S(2)}) collective-permute-start(bf16[128,384]{1,0:T(8,128)(2,1)S(1)} %get-tuple-element.40), channel_id=1, source_target_pairs={{0,16},{4,20},{8,24},{12,28},{16,0},{20,4},{24,8},{28,12},{1,17},{... | collective-permute-start | bytes 294920 | tf_op jit(solution)/shard_map/ppermute | solution.py:290
  52.9 11.0 %collective-permute-start.20 = (f32[4,128]{1,0:T(4,128)S(1)}, f32[4,128]{1,0:T(4,128)S(1)}, u32[]{:S(2)}, u32[]{:S(2)}) collective-permute-start(f32[4,128]{1,0:T(4,128)S(1)} %get-tuple-element.31.meta_ref), channel_id=1, source_target_pairs={{0,16},{4,20},{8,24},{12,28},{16,0},{20,4},{24,8},{28,12},{1,17},{... | collective-permute-start | bytes 6152 | tf_op jit(solution)/shard_map/ppermute | solution.py:290
  64.3 5.5 %collective-permute-start.23 = (bf16[64,1024]{1,0:T(8,128)(2,1)S(1)}, bf16[64,1024]{1,0:T(8,128)(2,1)S(1)}, u32[]{:S(2)}, u32[]{:S(2)}) collective-permute-start(bf16[64,1024]{1,0:T(8,128)(2,1)S(1)} %get-tuple-element.42), channel_id=1, source_target_pairs={{0,4},{4,0},{8,12},{12,8},{16,20},{20,16},{24,28},{28,24},{1,5},{5... | collective-permute-start | bytes 393224 | tf_op jit(solution)/shard_map/ppermute | solution.py:290
  66.1 6.4 %collective-permute-start.24 = (bf16[64,1024]{1,0:T(8,128)(2,1)S(1)}, bf16[64,1024]{1,0:T(8,128)(2,1)S(1)}, u32[]{:S(2)}, u32[]{:S(2)}) collective-permute-start(bf16[64,1024]{1,0:T(8,128)(2,1)S(1)} %get-tuple-element.43), channel_id=1, source_target_pairs={{0,8},{4,12},{8,0},{12,4},{16,24},{20,28},{24,16},{28,20},{1,9},{5... | collective-permute-start | bytes 393224 | tf_op jit(solution)/shard_map/ppermute | solution.py:290
  66.1 7.7 %collective-permute-start.25 = (bf16[64,1024]{1,0:T(8,128)(2,1)S(1)}, bf16[64,1024]{1,0:T(8,128)(2,1)S(1)}, u32[]{:S(2)}, u32[]{:S(2)}) collective-permute-start(bf16[64,1024]{1,0:T(8,128)(2,1)S(1)} %get-tuple-element.44), channel_id=1, source_target_pairs={{0,12},{4,8},{8,4},{12,0},{16,28},{20,24},{24,20},{28,16},{1,13},{... | collective-permute-start | bytes 393224 | tf_op jit(solution)/shard_map/ppermute | solution.py:290
  75.0 7.2 %collective-permute-start.26 = (bf16[64,1024]{1,0:T(8,128)(2,1)S(1)}, bf16[64,1024]{1,0:T(8,128)(2,1)S(1)}, u32[]{:S(2)}, u32[]{:S(2)}) collective-permute-start(bf16[64,1024]{1,0:T(8,128)(2,1)S(1)} %get-tuple-element.46), channel_id=1, source_target_pairs={{0,4},{4,0},{8,12},{12,8},{16,20},{20,16},{24,28},{28,24},{1,5},{5... | collective-permute-start | bytes 393224 | tf_op jit(solution)/shard_map/ppermute | solution.py:290
  76.8 6.7 %collective-permute-start.27 = (bf16[64,1024]{1,0:T(8,128)(2,1)S(1)}, bf16[64,1024]{1,0:T(8,128)(2,1)S(1)}, u32[]{:S(2)}, u32[]{:S(2)}) collective-permute-start(bf16[64,1024]{1,0:T(8,128)(2,1)S(1)} %get-tuple-element.47), channel_id=1, source_target_pairs={{0,8},{4,12},{8,0},{12,4},{16,24},{20,28},{24,16},{28,20},{1,9},{5... | collective-permute-start | bytes 393224 | tf_op jit(solution)/shard_map/ppermute | solution.py:290
  77.1 8.8 %collective-permute-start.28 = (bf16[64,1024]{1,0:T(8,128)(2,1)S(1)}, bf16[64,1024]{1,0:T(8,128)(2,1)S(1)}, u32[]{:S(2)}, u32[]{:S(2)}) collective-permute-start(bf16[64,1024]{1,0:T(8,128)(2,1)S(1)} %get-tuple-element.48), channel_id=1, source_target_pairs={{0,12},{4,8},{8,4},{12,0},{16,28},{20,24},{24,20},{28,16},{1,13},{... | collective-permute-start | bytes 393224 | tf_op jit(solution)/shard_map/ppermute | solution.py:290
  78.6 10.2 %collective-permute-start.30 = (bf16[64,1024]{1,0:T(8,128)(2,1)S(1)}, bf16[64,1024]{1,0:T(8,128)(2,1)S(1)}, u32[]{:S(2)}, u32[]{:S(2)}) collective-permute-start(bf16[64,1024]{1,0:T(8,128)(2,1)S(1)} %get-tuple-element.50), channel_id=1, source_target_pairs={{0,4},{4,0},{8,12},{12,8},{16,20},{20,16},{24,28},{28,24},{1,5},{5... | collective-permute-start | bytes 393224 | tf_op jit(solution)/shard_map/ppermute | solution.py:290
  80.3 10.4 %collective-permute-start.31 = (bf16[64,1024]{1,0:T(8,128)(2,1)S(1)}, bf16[64,1024]{1,0:T(8,128)(2,1)S(1)}, u32[]{:S(2)}, u32[]{:S(2)}) collective-permute-start(bf16[64,1024]{1,0:T(8,128)(2,1)S(1)} %get-tuple-element.51), channel_id=1, source_target_pairs={{0,8},{4,12},{8,0},{12,4},{16,24},{20,28},{24,16},{28,20},{1,9},{5... | collective-permute-start | bytes 393224 | tf_op jit(solution)/shard_map/ppermute | solution.py:290
  82.3 9.6 %collective-permute-start.32 = (bf16[64,1024]{1,0:T(8,128)(2,1)S(1)}, bf16[64,1024]{1,0:T(8,128)(2,1)S(1)}, u32[]{:S(2)}, u32[]{:S(2)}) collective-permute-start(bf16[64,1024]{1,0:T(8,128)(2,1)S(1)} %get-tuple-element.52), channel_id=1, source_target_pairs={{0,12},{4,8},{8,4},{12,0},{16,28},{20,24},{24,20},{28,16},{1,13},{... | collective-permute-start | bytes 393224 | tf_op jit(solution)/shard_map/ppermute | solution.py:290
  86.3 16.5 %collective-permute-start.29 = (bf16[128,1024]{1,0:T(8,128)(2,1)S(1)}, bf16[128,1024]{1,0:T(8,128)(2,1)S(1)}, u32[]{:S(2)}, u32[]{:S(2)}) collective-permute-start(bf16[128,1024]{1,0:T(8,128)(2,1)S(1)} %shard_map.104), channel_id=1, source_target_pairs={{0,16},{4,20},{8,24},{12,28},{16,0},{20,4},{24,8},{28,12},{1,17},{... | collective-permute-start | bytes 786440 | tf_op jit(solution)/shard_map/ppermute | solution.py:290
  93.1 6.4 %collective-permute-start.33 = (bf16[64,1024]{1,0:T(8,128)(2,1)S(1)}, bf16[64,1024]{1,0:T(8,128)(2,1)S(1)}, u32[]{:S(2)}, u32[]{:S(2)}) collective-permute-start(bf16[64,1024]{1,0:T(8,128)(2,1)S(1)} %get-tuple-element.54), channel_id=1, source_target_pairs={{0,4},{4,0},{8,12},{12,8},{16,20},{20,16},{24,28},{28,24},{1,5},{5... | collective-permute-start | bytes 393224 | tf_op jit(solution)/shard_map/ppermute | solution.py:290
  95.6 5.1 %collective-permute-start.34 = (bf16[64,1024]{1,0:T(8,128)(2,1)S(1)}, bf16[64,1024]{1,0:T(8,128)(2,1)S(1)}, u32[]{:S(2)}, u32[]{:S(2)}) collective-permute-start(bf16[64,1024]{1,0:T(8,128)(2,1)S(1)} %get-tuple-element.55), channel_id=1, source_target_pairs={{0,8},{4,12},{8,0},{12,4},{16,24},{20,28},{24,16},{28,20},{1,9},{5... | collective-permute-start | bytes 393224 | tf_op jit(solution)/shard_map/ppermute | solution.py:290
  95.6 7.3 %collective-permute-start.35 = (bf16[64,1024]{1,0:T(8,128)(2,1)S(1)}, bf16[64,1024]{1,0:T(8,128)(2,1)S(1)}, u32[]{:S(2)}, u32[]{:S(2)}) collective-permute-start(bf16[64,1024]{1,0:T(8,128)(2,1)S(1)} %get-tuple-element.56), channel_id=1, source_target_pairs={{0,12},{4,8},{8,4},{12,0},{16,28},{20,24},{24,20},{28,16},{1,13},{... | collective-permute-start | bytes 393224 | tf_op jit(solution)/shard_map/ppermute | solution.py:290
  (11 other events, 147.3 us)

commit v6 on v5

--- a/solution.py
+++ b/solution.py
@@ -257,11 +257,14 @@
     out_ref[...] = gather_rows(n, meta_ref[...], ins, key_ref, gate_ref).astype(BF)
 
 
-def final_body(n, meta_ref, hidden_ref, other_ref, *refs):
+def settle_body(n, meta_ref, hidden_ref, *refs):
     ins, out_ref, key_ref, gate_ref = refs[:-3], refs[-3], refs[-2], refs[-1]
     total = gather_rows(n, meta_ref[...], ins, key_ref, gate_ref)
-    total = total + other_ref[...].astype(F32) + hidden_ref[...].astype(F32)
-    out_ref[...] = total.astype(BF)
+    out_ref[...] = total + hidden_ref[...].astype(F32)
+
+
+def final_body(total_ref, other_ref, out_ref):
+    out_ref[...] = (total_ref[...] + other_ref[...].astype(F32)).astype(BF)
 
 
 def small_group(
@@ -408,12 +411,13 @@
     far_back = flips(far_out)
     part_far = kernel(functools.partial(partial_body, n), full, (meta_far, *far_back), [keys, keys])
     part_own = flip(part_far, near)
-    return kernel(
-        functools.partial(final_body, n),
-        jax.ShapeDtypeStruct((length, D), BF),
-        (meta, hidden, part_own, *own_back),
+    settled = kernel(
+        functools.partial(settle_body, n),
+        sds((length, D), F32),
+        (meta, hidden, *own_back),
         [keys, keys],
     )
+    return kernel(final_body, jax.ShapeDtypeStruct((length, D), BF), (settled, part_own))
 
 
 def large_group(

time: 104 us -> 104 us (level)
    pallas_call x16 -> x17, Pallas kernels: 11.1 us -> 11.2 us  [call(): run(*[pltpu.with_memory_space_constraint(x, m) for x, m in zip(xs, spaces)])]
where the time goes in v6:
time: 104 us
  waiting for transfers between devices  51 us (49%)
  starting transfers between devices  41.7 us (40%)
  Pallas kernels  11.2 us (11%)
    ppermute x20, waiting for transfers between devices, flip(): return lax.ppermute(x, 'seq', [(i, i ^ k) for i in range(n)])  38.3 us
    ppermute x20, starting transfers between devices, flip(): return lax.ppermute(x, 'seq', [(i, i ^ k) for i in range(n)])  27.6 us
    ppermute x4, waiting for transfers between devices, small_group(): f = lax.ppermute(f, 'seq', ahead)  12.7 us
    pallas_call x17, Pallas kernels, call(): run(*[pltpu.with_memory_space_constraint(x, m) for x, m in zip(xs, spaces)])  11.2 us
    ppermute x4, starting transfers between devices, small_group(): f = lax.ppermute(f, 'seq', ahead)  8.73 us
    ppermute x9, starting transfers between devices, share(): held = held + [lax.ppermute(h, 'win', pairs) for h in held]  4.91 us
  transfers between devices with their start and end apart: 36, of which 18 were waited for; matrix products, arithmetic and copies ran while one was open for 0% of the time, Pallas kernels for 6%

profile of v6, /device:TPU:0, one launch (start us, length us, event | category | flops | bytes accessed | tf_op | source)
XLA Modules:
  0.0 104.1 jit_solution(9870890815605807291)
XLA Ops:
  0.0 2.0 %shard_map.91 = (f32[512,128]{1,0:T(8,128)S(1)}, bf16[512,128]{1,0:T(8,128)(2,1)S(1)}, f32[4,128]{1,0:T(4,128)S(1)}, bf16[512,128]{1,0:T(8,128)(2,1)S(1)}) custom-call(bf16[128,1024]{1,0:T(8,128)(2,1)} %k_ref.5, bf16[128,2048]{1,0:T(8,128)(2,1)} %v_ref.5, s32[2,128]{1,0:T(2,128)} %bitcast.2, f32[2,128]{1,0:T(2,128)} %bitcast.3, bf16[2048,128]{1,0:T(8,128)(2,1)} %wown_ref.1), custom_call_target="tpu_custom_call" | custom-call | tf_op jit(solution)/shard_map/pallas_call | solution.py:34
  2.1 3.1 %collective-permute-start.4 = (bf16[512,128]{1,0:T(8,128)(2,1)S(1)}, bf16[512,128]{1,0:T(8,128)(2,1)S(1)}, u32[]{:S(2)}, u32[]{:S(2)}) collective-permute-start(bf16[512,128]{1,0:T(8,128)(2,1)S(1)} %get-tuple-element.36), channel_id=1, source_target_pairs={{0,8},{8,16},{16,24},{24,28},{28,20},{20,12},{12,4},{4,0},{1,9},{9... | collective-permute-start | bytes 393224 | tf_op jit(solution)/shard_map/ppermute | solution.py:344
  5.2 3.4 %collective-permute-done.4.refs_0_ = bf16[512,128]{1,0:T(8,128)(2,1)S(1)} collective-permute-done((bf16[512,128]{1,0:T(8,128)(2,1)S(1)}, bf16[512,128]{1,0:T(8,128)(2,1)S(1)}, u32[]{:S(2)}, u32[]{:S(2)}) %collective-permute-start.4) | collective-permute-done | bytes 131104 | tf_op jit(solution)/shard_map/ppermute | solution.py:344
  8.6 1.8 %collective-permute-start.9 = (bf16[512,128]{1,0:T(8,128)(2,1)S(1)}, bf16[512,128]{1,0:T(8,128)(2,1)S(1)}, u32[]{:S(2)}, u32[]{:S(2)}) collective-permute-start(bf16[512,128]{1,0:T(8,128)(2,1)S(1)} %collective-permute-done.4.refs_0_), channel_id=1, source_target_pairs={{0,8},{8,16},{16,24},{24,28},{28,20},{20,12},{12,4},{4,0},{1,9},{9... | collective-permute-start | bytes 393224 | tf_op jit(solution)/shard_map/ppermute | solution.py:344
  10.6 2.9 %collective-permute-done.9.refs_0_ = bf16[512,128]{1,0:T(8,128)(2,1)S(1)} collective-permute-done((bf16[512,128]{1,0:T(8,128)(2,1)S(1)}, bf16[512,128]{1,0:T(8,128)(2,1)S(1)}, u32[]{:S(2)}, u32[]{:S(2)}) %collective-permute-start.9) | collective-permute-done | bytes 131104 | tf_op jit(solution)/shard_map/ppermute | solution.py:344
  13.6 1.8 %collective-permute-start.14 = (bf16[512,128]{1,0:T(8,128)(2,1)S(1)}, bf16[512,128]{1,0:T(8,128)(2,1)S(1)}, u32[]{:S(2)}, u32[]{:S(2)}) collective-permute-start(bf16[512,128]{1,0:T(8,128)(2,1)S(1)} %collective-permute-done.9.refs_0_), channel_id=1, source_target_pairs={{0,8},{8,16},{16,24},{24,28},{28,20},{20,12},{12,4},{4,0},{1,9},{9... | collective-permute-start | bytes 393224 | tf_op jit(solution)/shard_map/ppermute | solution.py:344
  15.6 3.4 %collective-permute-done.14.refs_0_ = bf16[512,128]{1,0:T(8,128)(2,1)S(1)} collective-permute-done((bf16[512,128]{1,0:T(8,128)(2,1)S(1)}, bf16[512,128]{1,0:T(8,128)(2,1)S(1)}, u32[]{:S(2)}, u32[]{:S(2)}) %collective-permute-start.14) | collective-permute-done | bytes 131104 | tf_op jit(solution)/shard_map/ppermute | solution.py:344
  19.0 2.0 %collective-permute-start.16 = (bf16[512,128]{1,0:T(8,128)(2,1)S(1)}, bf16[512,128]{1,0:T(8,128)(2,1)S(1)}, u32[]{:S(2)}, u32[]{:S(2)}) collective-permute-start(bf16[512,128]{1,0:T(8,128)(2,1)S(1)} %collective-permute-done.14.refs_0_), channel_id=1, source_target_pairs={{0,8},{8,16},{16,24},{24,28},{28,20},{20,12},{12,4},{4,0},{1,9},{9... | collective-permute-start | bytes 393224 | tf_op jit(solution)/shard_map/ppermute | solution.py:344
  21.0 2.9 %collective-permute-done.16.refs_2_ = bf16[512,128]{1,0:T(8,128)(2,1)S(1)} collective-permute-done((bf16[512,128]{1,0:T(8,128)(2,1)S(1)}, bf16[512,128]{1,0:T(8,128)(2,1)S(1)}, u32[]{:S(2)}, u32[]{:S(2)}) %collective-permute-start.16) | collective-permute-done | bytes 131104 | tf_op jit(solution)/shard_map/ppermute | solution.py:344
  24.0 2.1 %collective-permute-start.17 = (bf16[1536,128]{1,0:T(8,128)(2,1)S(1)}, bf16[1536,128]{1,0:T(8,128)(2,1)S(1)}, u32[]{:S(2)}, u32[]{:S(2)}) collective-permute-start(bf16[1536,128]{1,0:T(8,128)(2,1)S(1)} %shard_map.100.refs_0_), channel_id=1, source_target_pairs={{0,2},{1,3},{2,0},{3,1},{4,6},{5,7},{6,4},{7,5},{8,10},{9,11},{10,... | collective-permute-start | bytes 1179656 | tf_op jit(solution)/shard_map/ppermute | solution.py:314
  26.2 2.5 %collective-permute-start.1 = (bf16[512,128]{1,0:T(8,128)(2,1)S(1)}, bf16[512,128]{1,0:T(8,128)(2,1)S(1)}, u32[]{:S(2)}, u32[]{:S(2)}) collective-permute-start(bf16[512,128]{1,0:T(8,128)(2,1)S(1)} %shard_map.94), channel_id=1, source_target_pairs={{0,8},{4,12},{8,0},{12,4},{16,24},{20,28},{24,16},{28,20},{1,9},{5... | collective-permute-start | bytes 393224 | tf_op jit(solution)/shard_map/ppermute | solution.py:293
  29.2 3.0 %collective-permute-done.1.refs_1_.refs_0_ = bf16[512,128]{1,0:T(8,128)(2,1)S(1)} collective-permute-done((bf16[512,128]{1,0:T(8,128)(2,1)S(1)}, bf16[512,128]{1,0:T(8,128)(2,1)S(1)}, u32[]{:S(2)}, u32[]{:S(2)}) %collective-permute-start.1) | collective-permute-done | bytes 131104 | tf_op jit(solution)/shard_map/ppermute | solution.py:293
  32.3 2.3 %collective-permute-start.2 = (bf16[512,128]{1,0:T(8,128)(2,1)S(1)}, bf16[512,128]{1,0:T(8,128)(2,1)S(1)}, u32[]{:S(2)}, u32[]{:S(2)}) collective-permute-start(bf16[512,128]{1,0:T(8,128)(2,1)S(1)} %shard_map.95), channel_id=1, source_target_pairs={{0,16},{4,20},{8,24},{12,28},{16,0},{20,4},{24,8},{28,12},{1,17},{... | collective-permute-start | bytes 393224 | tf_op jit(solution)/shard_map/ppermute | solution.py:293
  35.8 3.8 %collective-permute-done.2.refs_1_ = bf16[512,128]{1,0:T(8,128)(2,1)S(1)} collective-permute-done((bf16[512,128]{1,0:T(8,128)(2,1)S(1)}, bf16[512,128]{1,0:T(8,128)(2,1)S(1)}, u32[]{:S(2)}, u32[]{:S(2)}) %collective-permute-start.2) | collective-permute-done | bytes 131104 | tf_op jit(solution)/shard_map/ppermute | solution.py:293
  39.8 2.2 %collective-permute-start.3 = (bf16[512,128]{1,0:T(8,128)(2,1)S(1)}, bf16[512,128]{1,0:T(8,128)(2,1)S(1)}, u32[]{:S(2)}, u32[]{:S(2)}) collective-permute-start(bf16[512,128]{1,0:T(8,128)(2,1)S(1)} %get-tuple-element.35), channel_id=1, source_target_pairs={{0,4},{4,0},{8,12},{12,8},{16,20},{20,16},{24,28},{28,24},{1,5},{5... | collective-permute-start | bytes 393224 | tf_op jit(solution)/shard_map/ppermute | solution.py:293
  42.5 2.4 %collective-permute-done.3.po_ref = bf16[512,128]{1,0:T(8,128)(2,1)S(1)} collective-permute-done((bf16[512,128]{1,0:T(8,128)(2,1)S(1)}, bf16[512,128]{1,0:T(8,128)(2,1)S(1)}, u32[]{:S(2)}, u32[]{:S(2)}) %collective-permute-start.3) | collective-permute-done | bytes 131104 | tf_op jit(solution)/shard_map/ppermute | solution.py:293
  50.6 2.2 %collective-permute-start.28 = (bf16[128,384]{1,0:T(8,128)(2,1)S(1)}, bf16[128,384]{1,0:T(8,128)(2,1)S(1)}, u32[]{:S(2)}, u32[]{:S(2)}) collective-permute-start(bf16[128,384]{1,0:T(8,128)(2,1)S(1)} %get-tuple-element.48), channel_id=1, source_target_pairs={{0,16},{4,20},{8,24},{12,28},{16,0},{20,4},{24,8},{28,12},{1,17},{... | collective-permute-start | bytes 294920 | tf_op jit(solution)/shard_map/ppermute | solution.py:293
  53.6 10.2 %collective-permute-done.26.meta_ref = f32[4,128]{1,0:T(4,128)S(1)} collective-permute-done((f32[4,128]{1,0:T(4,128)S(1)}, f32[4,128]{1,0:T(4,128)S(1)}, u32[]{:S(2)}, u32[]{:S(2)}) %collective-permute-start.26) | collective-permute-done | bytes 2080 | tf_op jit(solution)/shard_map/ppermute | solution.py:293
  64.3 1.8 %collective-permute-start.29 = (bf16[64,1024]{1,0:T(8,128)(2,1)S(1)}, bf16[64,1024]{1,0:T(8,128)(2,1)S(1)}, u32[]{:S(2)}, u32[]{:S(2)}) collective-permute-start(bf16[64,1024]{1,0:T(8,128)(2,1)S(1)} %get-tuple-element.50), channel_id=1, source_target_pairs={{0,4},{4,0},{8,12},{12,8},{16,20},{20,16},{24,28},{28,24},{1,5},{5... | collective-permute-start | bytes 393224 | tf_op jit(solution)/shard_map/ppermute | solution.py:293
  66.1 1.8 %collective-permute-start.31 = (bf16[64,1024]{1,0:T(8,128)(2,1)S(1)}, bf16[64,1024]{1,0:T(8,128)(2,1)S(1)}, u32[]{:S(2)}, u32[]{:S(2)}) collective-permute-start(bf16[64,1024]{1,0:T(8,128)(2,1)S(1)} %get-tuple-element.52), channel_id=1, source_target_pairs={{0,12},{4,8},{8,4},{12,0},{16,28},{20,24},{24,20},{28,16},{1,13},{... | collective-permute-start | bytes 393224 | tf_op jit(solution)/shard_map/ppermute | solution.py:293
  67.9 1.9 %collective-permute-done.29.refs_1_ = bf16[64,1024]{1,0:T(8,128)(2,1)S(1)} collective-permute-done((bf16[64,1024]{1,0:T(8,128)(2,1)S(1)}, bf16[64,1024]{1,0:T(8,128)(2,1)S(1)}, u32[]{:S(2)}, u32[]{:S(2)}) %collective-permute-start.29) | collective-permute-done | bytes 131104 | tf_op jit(solution)/shard_map/ppermute | solution.py:293
  69.8 2.7 %collective-permute-done.30.refs_2_ = bf16[64,1024]{1,0:T(8,128)(2,1)S(1)} collective-permute-done((bf16[64,1024]{1,0:T(8,128)(2,1)S(1)}, bf16[64,1024]{1,0:T(8,128)(2,1)S(1)}, u32[]{:S(2)}, u32[]{:S(2)}) %collective-permute-start.30) | collective-permute-done | bytes 131104 | tf_op jit(solution)/shard_map/ppermute | solution.py:293
  75.0 1.7 %collective-permute-start.32 = (bf16[64,1024]{1,0:T(8,128)(2,1)S(1)}, bf16[64,1024]{1,0:T(8,128)(2,1)S(1)}, u32[]{:S(2)}, u32[]{:S(2)}) collective-permute-start(bf16[64,1024]{1,0:T(8,128)(2,1)S(1)} %get-tuple-element.54), channel_id=1, source_target_pairs={{0,4},{4,0},{8,12},{12,8},{16,20},{20,16},{24,28},{28,24},{1,5},{5... | collective-permute-start | bytes 393224 | tf_op jit(solution)/shard_map/ppermute | solution.py:293
  78.6 1.7 %collective-permute-start.20 = (bf16[64,1024]{1,0:T(8,128)(2,1)S(1)}, bf16[64,1024]{1,0:T(8,128)(2,1)S(1)}, u32[]{:S(2)}, u32[]{:S(2)}) collective-permute-start(bf16[64,1024]{1,0:T(8,128)(2,1)S(1)} %get-tuple-element.41), channel_id=1, source_target_pairs={{0,4},{4,0},{8,12},{12,8},{16,20},{20,16},{24,28},{28,24},{1,5},{5... | collective-permute-start | bytes 393224 | tf_op jit(solution)/shard_map/ppermute | solution.py:293
  80.5 1.7 %collective-permute-done.32.refs_1_ = bf16[64,1024]{1,0:T(8,128)(2,1)S(1)} collective-permute-done((bf16[64,1024]{1,0:T(8,128)(2,1)S(1)}, bf16[64,1024]{1,0:T(8,128)(2,1)S(1)}, u32[]{:S(2)}, u32[]{:S(2)}) %collective-permute-start.32) | collective-permute-done | bytes 131104 | tf_op jit(solution)/shard_map/ppermute | solution.py:293
  83.4 2.4 %collective-permute-done.34.refs_3_ = bf16[64,1024]{1,0:T(8,128)(2,1)S(1)} collective-permute-done((bf16[64,1024]{1,0:T(8,128)(2,1)S(1)}, bf16[64,1024]{1,0:T(8,128)(2,1)S(1)}, u32[]{:S(2)}, u32[]{:S(2)}) %collective-permute-start.34) | collective-permute-done | bytes 131104 | tf_op jit(solution)/shard_map/ppermute | solution.py:293
  86.3 2.5 %collective-permute-start.35 = (bf16[128,1024]{1,0:T(8,128)(2,1)S(1)}, bf16[128,1024]{1,0:T(8,128)(2,1)S(1)}, u32[]{:S(2)}, u32[]{:S(2)}) collective-permute-start(bf16[128,1024]{1,0:T(8,128)(2,1)S(1)} %shard_map.106), channel_id=1, source_target_pairs={{0,16},{4,20},{8,24},{12,28},{16,0},{20,4},{24,8},{28,12},{1,17},{... | collective-permute-start | bytes 786440 | tf_op jit(solution)/shard_map/ppermute | solution.py:293
  88.8 1.8 %collective-permute-done.21.refs_2_ = bf16[64,1024]{1,0:T(8,128)(2,1)S(1)} collective-permute-done((bf16[64,1024]{1,0:T(8,128)(2,1)S(1)}, bf16[64,1024]{1,0:T(8,128)(2,1)S(1)}, u32[]{:S(2)}, u32[]{:S(2)}) %collective-permute-start.21) | collective-permute-done | bytes 131104 | tf_op jit(solution)/shard_map/ppermute | solution.py:293
  93.1 2.5 %collective-permute-start.23 = (bf16[64,1024]{1,0:T(8,128)(2,1)S(1)}, bf16[64,1024]{1,0:T(8,128)(2,1)S(1)}, u32[]{:S(2)}, u32[]{:S(2)}) collective-permute-start(bf16[64,1024]{1,0:T(8,128)(2,1)S(1)} %get-tuple-element.45), channel_id=1, source_target_pairs={{0,4},{4,0},{8,12},{12,8},{16,20},{20,16},{24,28},{28,24},{1,5},{5... | collective-permute-start | bytes 393224 | tf_op jit(solution)/shard_map/ppermute | solution.py:293
  95.6 1.5 %collective-permute-start.25 = (bf16[64,1024]{1,0:T(8,128)(2,1)S(1)}, bf16[64,1024]{1,0:T(8,128)(2,1)S(1)}, u32[]{:S(2)}, u32[]{:S(2)}) collective-permute-start(bf16[64,1024]{1,0:T(8,128)(2,1)S(1)} %get-tuple-element.47), channel_id=1, source_target_pairs={{0,12},{4,8},{8,4},{12,0},{16,28},{20,24},{24,20},{28,16},{1,13},{... | collective-permute-start | bytes 393224 | tf_op jit(solution)/shard_map/ppermute | solution.py:293
  97.1 2.3 %collective-permute-done.23.refs_1_ = bf16[64,1024]{1,0:T(8,128)(2,1)S(1)} collective-permute-done((bf16[64,1024]{1,0:T(8,128)(2,1)S(1)}, bf16[64,1024]{1,0:T(8,128)(2,1)S(1)}, u32[]{:S(2)}, u32[]{:S(2)}) %collective-permute-start.23) | collective-permute-done | bytes 131104 | tf_op jit(solution)/shard_map/ppermute | solution.py:293
  100.7 2.1 %collective-permute-done.25.refs_3_ = bf16[64,1024]{1,0:T(8,128)(2,1)S(1)} collective-permute-done((bf16[64,1024]{1,0:T(8,128)(2,1)S(1)}, bf16[64,1024]{1,0:T(8,128)(2,1)S(1)}, u32[]{:S(2)}, u32[]{:S(2)}) %collective-permute-start.25) | collective-permute-done | bytes 131104 | tf_op jit(solution)/shard_map/ppermute | solution.py:293
  (71 shorter events, 21.2 us)
Async XLA Ops:
  2.1 6.5 %collective-permute-start.4 = (bf16[512,128]{1,0:T(8,128)(2,1)S(1)}, bf16[512,128]{1,0:T(8,128)(2,1)S(1)}, u32[]{:S(2)}, u32[]{:S(2)}) collective-permute-start(bf16[512,128]{1,0:T(8,128)(2,1)S(1)} %get-tuple-element.36), channel_id=1, source_target_pairs={{0,8},{8,16},{16,24},{24,28},{28,20},{20,12},{12,4},{4,0},{1,9},{9... | collective-permute-start | bytes 393224 | tf_op jit(solution)/shard_map/ppermute | solution.py:344
  5.2 5.2 %collective-permute-start.5 = (bf16[512,128]{1,0:T(8,128)(2,1)S(1)}, bf16[512,128]{1,0:T(8,128)(2,1)S(1)}, u32[]{:S(2)}, u32[]{:S(2)}) collective-permute-start(bf16[512,128]{1,0:T(8,128)(2,1)S(1)} %get-tuple-element.36), channel_id=1, source_target_pairs={{8,0},{16,8},{24,16},{28,24},{20,28},{12,20},{4,12},{0,4},{9,1},{1... | collective-permute-start | bytes 393224 | tf_op jit(solution)/shard_map/ppermute | solution.py:347
  10.4 5.0 %collective-permute-start.10 = (bf16[512,128]{1,0:T(8,128)(2,1)S(1)}, bf16[512,128]{1,0:T(8,128)(2,1)S(1)}, u32[]{:S(2)}, u32[]{:S(2)}) collective-permute-start(bf16[512,128]{1,0:T(8,128)(2,1)S(1)} %collective-permute-done.5.refs_1_), channel_id=1, source_target_pairs={{8,0},{16,8},{24,16},{28,24},{20,28},{12,20},{4,12},{0,4},{9,1},{1... | collective-permute-start | bytes 393224 | tf_op jit(solution)/shard_map/ppermute | solution.py:347
  13.6 5.4 %collective-permute-start.14 = (bf16[512,128]{1,0:T(8,128)(2,1)S(1)}, bf16[512,128]{1,0:T(8,128)(2,1)S(1)}, u32[]{:S(2)}, u32[]{:S(2)}) collective-permute-start(bf16[512,128]{1,0:T(8,128)(2,1)S(1)} %collective-permute-done.9.refs_0_), channel_id=1, source_target_pairs={{0,8},{8,16},{16,24},{24,28},{28,20},{20,12},{12,4},{4,0},{1,9},{9... | collective-permute-start | bytes 393224 | tf_op jit(solution)/shard_map/ppermute | solution.py:344
  15.4 5.6 %collective-permute-start.15 = (bf16[512,128]{1,0:T(8,128)(2,1)S(1)}, bf16[512,128]{1,0:T(8,128)(2,1)S(1)}, u32[]{:S(2)}, u32[]{:S(2)}) collective-permute-start(bf16[512,128]{1,0:T(8,128)(2,1)S(1)} %collective-permute-done.10.refs_1_), channel_id=1, source_target_pairs={{8,0},{16,8},{24,16},{28,24},{20,28},{12,20},{4,12},{0,4},{9,1},{1... | collective-permute-start | bytes 393224 | tf_op jit(solution)/shard_map/ppermute | solution.py:347
  21.0 5.2 %collective-permute-start = (bf16[512,128]{1,0:T(8,128)(2,1)S(1)}, bf16[512,128]{1,0:T(8,128)(2,1)S(1)}, u32[]{:S(2)}, u32[]{:S(2)}) collective-permute-start(bf16[512,128]{1,0:T(8,128)(2,1)S(1)} %get-tuple-element.33), channel_id=1, source_target_pairs={{0,4},{4,0},{8,12},{12,8},{16,20},{20,16},{24,28},{28,24},{1,5},{5... | collective-permute-start | bytes 393224 | tf_op jit(solution)/shard_map/ppermute | solution.py:293
  24.0 17.9 %collective-permute-start.17 = (bf16[1536,128]{1,0:T(8,128)(2,1)S(1)}, bf16[1536,128]{1,0:T(8,128)(2,1)S(1)}, u32[]{:S(2)}, u32[]{:S(2)}) collective-permute-start(bf16[1536,128]{1,0:T(8,128)(2,1)S(1)} %shard_map.100.refs_0_), channel_id=1, source_target_pairs={{0,2},{1,3},{2,0},{3,1},{4,6},{5,7},{6,4},{7,5},{8,10},{9,11},{10,... | collective-permute-start | bytes 1179656 | tf_op jit(solution)/shard_map/ppermute | solution.py:314
  26.2 6.1 %collective-permute-start.1 = (bf16[512,128]{1,0:T(8,128)(2,1)S(1)}, bf16[512,128]{1,0:T(8,128)(2,1)S(1)}, u32[]{:S(2)}, u32[]{:S(2)}) collective-permute-start(bf16[512,128]{1,0:T(8,128)(2,1)S(1)} %shard_map.94), channel_id=1, source_target_pairs={{0,8},{4,12},{8,0},{12,4},{16,24},{20,28},{24,16},{28,20},{1,9},{5... | collective-permute-start | bytes 393224 | tf_op jit(solution)/shard_map/ppermute | solution.py:293
  28.8 13.2 %collective-permute-start.6 = (bf16[1024,128]{1,0:T(8,128)(2,1)S(1)}, bf16[1024,128]{1,0:T(8,128)(2,1)S(1)}, u32[]{:S(2)}, u32[]{:S(2)}) collective-permute-start(bf16[1024,128]{1,0:T(8,128)(2,1)S(1)} %shard_map.97.refs_0_), channel_id=1, source_target_pairs={{0,2},{1,3},{2,0},{3,1},{4,6},{5,7},{6,4},{7,5},{8,10},{9,11},{10,... | collective-permute-start | bytes 786440 | tf_op jit(solution)/shard_map/ppermute | solution.py:314
  32.3 7.3 %collective-permute-start.2 = (bf16[512,128]{1,0:T(8,128)(2,1)S(1)}, bf16[512,128]{1,0:T(8,128)(2,1)S(1)}, u32[]{:S(2)}, u32[]{:S(2)}) collective-permute-start(bf16[512,128]{1,0:T(8,128)(2,1)S(1)} %shard_map.95), channel_id=1, source_target_pairs={{0,16},{4,20},{8,24},{12,28},{16,0},{20,4},{24,8},{28,12},{1,17},{... | collective-permute-start | bytes 393224 | tf_op jit(solution)/shard_map/ppermute | solution.py:293
  34.6 7.9 %collective-permute-start.7 = (bf16[1024,128]{1,0:T(8,128)(2,1)S(1)}, bf16[1024,128]{1,0:T(8,128)(2,1)S(1)}, u32[]{:S(2)}, u32[]{:S(2)}) collective-permute-start(bf16[1024,128]{1,0:T(8,128)(2,1)S(1)} %shard_map.97.refs_0_), channel_id=1, source_target_pairs={{0,1},{1,0},{2,3},{3,2},{4,5},{5,4},{6,7},{7,6},{8,9},{9,8},{10,11... | collective-permute-start | bytes 786440 | tf_op jit(solution)/shard_map/ppermute | solution.py:314
  34.6 10.3 %collective-permute-start.11 = (bf16[1024,128]{1,0:T(8,128)(2,1)S(1)}, bf16[1024,128]{1,0:T(8,128)(2,1)S(1)}, u32[]{:S(2)}, u32[]{:S(2)}) collective-permute-start(bf16[1024,128]{1,0:T(8,128)(2,1)S(1)} %shard_map.98.refs_4_), channel_id=1, source_target_pairs={{0,2},{1,3},{2,0},{3,1},{4,6},{5,7},{6,4},{7,5},{8,10},{9,11},{10,... | collective-permute-start | bytes 786440 | tf_op jit(solution)/shard_map/ppermute | solution.py:314
  39.8 5.1 %collective-permute-start.3 = (bf16[512,128]{1,0:T(8,128)(2,1)S(1)}, bf16[512,128]{1,0:T(8,128)(2,1)S(1)}, u32[]{:S(2)}, u32[]{:S(2)}) collective-permute-start(bf16[512,128]{1,0:T(8,128)(2,1)S(1)} %get-tuple-element.35), channel_id=1, source_target_pairs={{0,4},{4,0},{8,12},{12,8},{16,20},{20,16},{24,28},{28,24},{1,5},{5... | collective-permute-start | bytes 393224 | tf_op jit(solution)/shard_map/ppermute | solution.py:293
  41.9 7.8 %collective-permute-start.18 = (bf16[1536,128]{1,0:T(8,128)(2,1)S(1)}, bf16[1536,128]{1,0:T(8,128)(2,1)S(1)}, u32[]{:S(2)}, u32[]{:S(2)}) collective-permute-start(bf16[1536,128]{1,0:T(8,128)(2,1)S(1)} %shard_map.100.refs_0_), channel_id=1, source_target_pairs={{0,1},{1,0},{2,3},{3,2},{4,5},{5,4},{6,7},{7,6},{8,9},{9,8},{10,11... | collective-permute-start | bytes 1179656 | tf_op jit(solution)/shard_map/ppermute | solution.py:314
  41.9 7.8 %collective-permute-start.19 = (bf16[1536,128]{1,0:T(8,128)(2,1)S(1)}, bf16[1536,128]{1,0:T(8,128)(2,1)S(1)}, u32[]{:S(2)}, u32[]{:S(2)}) collective-permute-start(bf16[1536,128]{1,0:T(8,128)(2,1)S(1)} %collective-permute-done.17.refs_1_), channel_id=1, source_target_pairs={{0,1},{1,0},{2,3},{3,2},{4,5},{5,4},{6,7},{7,6},{8,9},{9,8},{10,11... | collective-permute-start | bytes 1179656 | tf_op jit(solution)/shard_map/ppermute | solution.py:314
  42.5 5.6 %collective-permute-start.12 = (bf16[1024,128]{1,0:T(8,128)(2,1)S(1)}, bf16[1024,128]{1,0:T(8,128)(2,1)S(1)}, u32[]{:S(2)}, u32[]{:S(2)}) collective-permute-start(bf16[1024,128]{1,0:T(8,128)(2,1)S(1)} %shard_map.98.refs_4_), channel_id=1, source_target_pairs={{0,1},{1,0},{2,3},{3,2},{4,5},{5,4},{6,7},{7,6},{8,9},{9,8},{10,11... | collective-permute-start | bytes 786440 | tf_op jit(solution)/shard_map/ppermute | solution.py:314
  48.9 14.9 %collective-permute-start.27 = (bf16[128,640]{1,0:T(8,128)(2,1)S(1)}, bf16[128,640]{1,0:T(8,128)(2,1)S(1)}, u32[]{:S(2)}, u32[]{:S(2)}) collective-permute-start(bf16[128,640]{1,0:T(8,128)(2,1)S(1)} %get-tuple-element.38.first_ref), channel_id=1, source_target_pairs={{0,16},{4,20},{8,24},{12,28},{16,0},{20,4},{24,8},{28,12},{1,17},{... | collective-permute-start | bytes 491528 | tf_op jit(solution)/shard_map/ppermute | solution.py:293
  50.6 13.2 %collective-permute-start.28 = (bf16[128,384]{1,0:T(8,128)(2,1)S(1)}, bf16[128,384]{1,0:T(8,128)(2,1)S(1)}, u32[]{:S(2)}, u32[]{:S(2)}) collective-permute-start(bf16[128,384]{1,0:T(8,128)(2,1)S(1)} %get-tuple-element.48), channel_id=1, source_target_pairs={{0,16},{4,20},{8,24},{12,28},{16,0},{20,4},{24,8},{28,12},{1,17},{... | collective-permute-start | bytes 294920 | tf_op jit(solution)/shard_map/ppermute | solution.py:293
  52.9 11.0 %collective-permute-start.26 = (f32[4,128]{1,0:T(4,128)S(1)}, f32[4,128]{1,0:T(4,128)S(1)}, u32[]{:S(2)}, u32[]{:S(2)}) collective-permute-start(f32[4,128]{1,0:T(4,128)S(1)} %get-tuple-element.31.meta_ref), channel_id=1, source_target_pairs={{0,16},{4,20},{8,24},{12,28},{16,0},{20,4},{24,8},{28,12},{1,17},{... | collective-permute-start | bytes 6152 | tf_op jit(solution)/shard_map/ppermute | solution.py:293
  64.3 5.5 %collective-permute-start.29 = (bf16[64,1024]{1,0:T(8,128)(2,1)S(1)}, bf16[64,1024]{1,0:T(8,128)(2,1)S(1)}, u32[]{:S(2)}, u32[]{:S(2)}) collective-permute-start(bf16[64,1024]{1,0:T(8,128)(2,1)S(1)} %get-tuple-element.50), channel_id=1, source_target_pairs={{0,4},{4,0},{8,12},{12,8},{16,20},{20,16},{24,28},{28,24},{1,5},{5... | collective-permute-start | bytes 393224 | tf_op jit(solution)/shard_map/ppermute | solution.py:293
  66.1 6.4 %collective-permute-start.30 = (bf16[64,1024]{1,0:T(8,128)(2,1)S(1)}, bf16[64,1024]{1,0:T(8,128)(2,1)S(1)}, u32[]{:S(2)}, u32[]{:S(2)}) collective-permute-start(bf16[64,1024]{1,0:T(8,128)(2,1)S(1)} %get-tuple-element.51), channel_id=1, source_target_pairs={{0,8},{4,12},{8,0},{12,4},{16,24},{20,28},{24,16},{28,20},{1,9},{5... | collective-permute-start | bytes 393224 | tf_op jit(solution)/shard_map/ppermute | solution.py:293
  66.1 7.7 %collective-permute-start.31 = (bf16[64,1024]{1,0:T(8,128)(2,1)S(1)}, bf16[64,1024]{1,0:T(8,128)(2,1)S(1)}, u32[]{:S(2)}, u32[]{:S(2)}) collective-permute-start(bf16[64,1024]{1,0:T(8,128)(2,1)S(1)} %get-tuple-element.52), channel_id=1, source_target_pairs={{0,12},{4,8},{8,4},{12,0},{16,28},{20,24},{24,20},{28,16},{1,13},{... | collective-permute-start | bytes 393224 | tf_op jit(solution)/shard_map/ppermute | solution.py:293
  75.0 7.2 %collective-permute-start.32 = (bf16[64,1024]{1,0:T(8,128)(2,1)S(1)}, bf16[64,1024]{1,0:T(8,128)(2,1)S(1)}, u32[]{:S(2)}, u32[]{:S(2)}) collective-permute-start(bf16[64,1024]{1,0:T(8,128)(2,1)S(1)} %get-tuple-element.54), channel_id=1, source_target_pairs={{0,4},{4,0},{8,12},{12,8},{16,20},{20,16},{24,28},{28,24},{1,5},{5... | collective-permute-start | bytes 393224 | tf_op jit(solution)/shard_map/ppermute | solution.py:293
  76.8 6.7 %collective-permute-start.33 = (bf16[64,1024]{1,0:T(8,128)(2,1)S(1)}, bf16[64,1024]{1,0:T(8,128)(2,1)S(1)}, u32[]{:S(2)}, u32[]{:S(2)}) collective-permute-start(bf16[64,1024]{1,0:T(8,128)(2,1)S(1)} %get-tuple-element.55), channel_id=1, source_target_pairs={{0,8},{4,12},{8,0},{12,4},{16,24},{20,28},{24,16},{28,20},{1,9},{5... | collective-permute-start | bytes 393224 | tf_op jit(solution)/shard_map/ppermute | solution.py:293
  77.1 8.8 %collective-permute-start.34 = (bf16[64,1024]{1,0:T(8,128)(2,1)S(1)}, bf16[64,1024]{1,0:T(8,128)(2,1)S(1)}, u32[]{:S(2)}, u32[]{:S(2)}) collective-permute-start(bf16[64,1024]{1,0:T(8,128)(2,1)S(1)} %get-tuple-element.56), channel_id=1, source_target_pairs={{0,12},{4,8},{8,4},{12,0},{16,28},{20,24},{24,20},{28,16},{1,13},{... | collective-permute-start | bytes 393224 | tf_op jit(solution)/shard_map/ppermute | solution.py:293
  78.6 10.2 %collective-permute-start.20 = (bf16[64,1024]{1,0:T(8,128)(2,1)S(1)}, bf16[64,1024]{1,0:T(8,128)(2,1)S(1)}, u32[]{:S(2)}, u32[]{:S(2)}) collective-permute-start(bf16[64,1024]{1,0:T(8,128)(2,1)S(1)} %get-tuple-element.41), channel_id=1, source_target_pairs={{0,4},{4,0},{8,12},{12,8},{16,20},{20,16},{24,28},{28,24},{1,5},{5... | collective-permute-start | bytes 393224 | tf_op jit(solution)/shard_map/ppermute | solution.py:293
  80.3 10.4 %collective-permute-start.21 = (bf16[64,1024]{1,0:T(8,128)(2,1)S(1)}, bf16[64,1024]{1,0:T(8,128)(2,1)S(1)}, u32[]{:S(2)}, u32[]{:S(2)}) collective-permute-start(bf16[64,1024]{1,0:T(8,128)(2,1)S(1)} %get-tuple-element.42), channel_id=1, source_target_pairs={{0,8},{4,12},{8,0},{12,4},{16,24},{20,28},{24,16},{28,20},{1,9},{5... | collective-permute-start | bytes 393224 | tf_op jit(solution)/shard_map/ppermute | solution.py:293
  82.3 9.6 %collective-permute-start.22 = (bf16[64,1024]{1,0:T(8,128)(2,1)S(1)}, bf16[64,1024]{1,0:T(8,128)(2,1)S(1)}, u32[]{:S(2)}, u32[]{:S(2)}) collective-permute-start(bf16[64,1024]{1,0:T(8,128)(2,1)S(1)} %get-tuple-element.43), channel_id=1, source_target_pairs={{0,12},{4,8},{8,4},{12,0},{16,28},{20,24},{24,20},{28,16},{1,13},{... | collective-permute-start | bytes 393224 | tf_op jit(solution)/shard_map/ppermute | solution.py:293
  86.3 17.0 %collective-permute-start.35 = (bf16[128,1024]{1,0:T(8,128)(2,1)S(1)}, bf16[128,1024]{1,0:T(8,128)(2,1)S(1)}, u32[]{:S(2)}, u32[]{:S(2)}) collective-permute-start(bf16[128,1024]{1,0:T(8,128)(2,1)S(1)} %shard_map.106), channel_id=1, source_target_pairs={{0,16},{4,20},{8,24},{12,28},{16,0},{20,4},{24,8},{28,12},{1,17},{... | collective-permute-start | bytes 786440 | tf_op jit(solution)/shard_map/ppermute | solution.py:293
  93.1 6.4 %collective-permute-start.23 = (bf16[64,1024]{1,0:T(8,128)(2,1)S(1)}, bf16[64,1024]{1,0:T(8,128)(2,1)S(1)}, u32[]{:S(2)}, u32[]{:S(2)}) collective-permute-start(bf16[64,1024]{1,0:T(8,128)(2,1)S(1)} %get-tuple-element.45), channel_id=1, source_target_pairs={{0,4},{4,0},{8,12},{12,8},{16,20},{20,16},{24,28},{28,24},{1,5},{5... | collective-permute-start | bytes 393224 | tf_op jit(solution)/shard_map/ppermute | solution.py:293
  95.6 5.1 %collective-permute-start.24 = (bf16[64,1024]{1,0:T(8,128)(2,1)S(1)}, bf16[64,1024]{1,0:T(8,128)(2,1)S(1)}, u32[]{:S(2)}, u32[]{:S(2)}) collective-permute-start(bf16[64,1024]{1,0:T(8,128)(2,1)S(1)} %get-tuple-element.46), channel_id=1, source_target_pairs={{0,8},{4,12},{8,0},{12,4},{16,24},{20,28},{24,16},{28,20},{1,9},{5... | collective-permute-start | bytes 393224 | tf_op jit(solution)/shard_map/ppermute | solution.py:293
  95.6 7.3 %collective-permute-start.25 = (bf16[64,1024]{1,0:T(8,128)(2,1)S(1)}, bf16[64,1024]{1,0:T(8,128)(2,1)S(1)}, u32[]{:S(2)}, u32[]{:S(2)}) collective-permute-start(bf16[64,1024]{1,0:T(8,128)(2,1)S(1)} %get-tuple-element.47), channel_id=1, source_target_pairs={{0,12},{4,8},{8,4},{12,0},{16,28},{20,24},{24,20},{28,16},{1,13},{... | collective-permute-start | bytes 393224 | tf_op jit(solution)/shard_map/ppermute | solution.py:293
  (11 other events, 147.3 us)

commit v7 on v6

--- a/solution.py
+++ b/solution.py
@@ -42,11 +42,17 @@
     return lax.dot_general(a, b, (dims, ((), ())), preferred_element_type=F32)
 
 
-def states_body(k_ref, v_ref, ids_ref, gates_ref, w_ref, mine_ref, send_ref, meta_ref, piece_ref, full, sem):
+def states_body(
+    other, k_ref, v_ref, ids_ref, gates_ref, w_ref, mine_ref, send_ref, meta_ref, piece_ref, extra_ref, full, sem
+):
     rows = piece_ref.shape[0]
-    start = pl.multiple_of(lax.axis_index("win") * rows, rows)
-    copy = pltpu.make_async_copy(w_ref.at[pl.ds(start, rows), :], piece_ref, sem)
-    copy.start()
+    w = lax.axis_index("win")
+    copies = []
+    for i, (part, dst) in enumerate(((w, piece_ref), (jnp.bitwise_xor(w, other), extra_ref))):
+        start = pl.multiple_of(part * rows, rows)
+        copies.append(pltpu.make_async_copy(w_ref.at[pl.ds(start, rows), :], dst, sem.at[i]))
+    for copy in copies:
+        copy.start()
     meta_ref[0:TOP, :] = ids_ref[...].astype(F32)
     meta_ref[TOP : 2 * TOP, :] = gates_ref[...]
     half = full.shape[0] // 2
@@ -57,7 +63,8 @@
     y = lax.rem(lax.axis_index("seq"), 2)
     mine_ref[...] = full[pl.ds(pl.multiple_of(y * half, half), half), :]
     send_ref[...] = full[pl.ds(pl.multiple_of((1 - y) * half, half), half), :].astype(BF)
-    copy.wait()
+    for copy in copies:
+        copy.wait()
 
 
 def running_body(mine_ref, *refs):
@@ -164,8 +171,10 @@
                 at += width
 
 
-def early_body(n, offsets, groups, q_ref, ia_ref, ib_ref, pm_ref, po_ref, wown_ref, res_ref, *refs):
-    packs, att, out_ref, prefix = refs[:-3], refs[-3], refs[-2], refs[-1]
+def early_body(n, offsets, groups, q_ref, ia_ref, ib_ref, pm_ref, po_ref, wown_ref, res_ref, meta_ref, *refs):
+    packs, refs = refs[: len(groups) * len(offsets)], refs[len(groups) * len(offsets) :]
+    att, out_ref = refs[:2]
+    outs, prefix, key_ref = refs[2:-2], refs[-2], refs[-1]
     s = lax.axis_index("seq")
     y = lax.rem(s, 2)
     length = q_ref.shape[0]
@@ -187,48 +196,49 @@
     own = dot(att[...], wown_ref[...]) + res_ref[:, columns(n, s, 0, width)].astype(F32)
     out_ref[:, :width] = own.astype(BF)
     project_some(n, offsets, groups, packs, att, res_ref, out_ref, width)
-
-
-def assemble(n, s, shifts, first, second, hid):
-    width = hid.shape[1] // n
+    key_ref[...] = keys_of(meta_ref[...], n)[0]
+    deal(key_ref, out_ref[...], outs, outs[0].shape[0])
+
+
+def assemble(n, s, shifts, first, second, out_ref, at):
+    width = out_ref.shape[1] // n
     cut = first.shape[1] // width
+    rows = first.shape[0]
     for i, shift in enumerate(shifts):
-        src, at = (first, i) if i < cut else (second, i - cut)
-        hid[:, columns(n, s, shift, width)] = src[:, at * width : (at + 1) * width].astype(F32)
-    h = hid[...]
-    return h, (h * lax.rsqrt(jnp.mean(h * h, axis=-1, keepdims=True) + 1e-06)).astype(BF)
-
-
-def late_body(n, offsets, groups, shifts, att_ref, first_ref, res_ref, meta_ref, *refs):
+        src, j = (first, i) if i < cut else (second, i - cut)
+        value = src[:, j * width : (j + 1) * width].astype(out_ref.dtype)
+        out_ref[at : at + rows, columns(n, s, shift, width)] = value
+
+
+def late_body(n, offsets, groups, att_ref, res_ref, meta_ref, *refs):
+    packs, refs = refs[: len(groups) * len(offsets)], refs[len(groups) * len(offsets) :]
+    out_ref, outs, key_ref = refs[0], refs[1:-1], refs[-1]
+    project_some(n, offsets, groups, packs, att_ref, res_ref, out_ref, 0)
+    key_ref[...] = keys_of(meta_ref[...], n)[0]
+    deal(key_ref, out_ref[...], outs, outs[0].shape[0])
+
+
+def deal_body(n, part_ref, meta_ref, *refs):
+    outs, key_ref = refs[:-1], refs[-1]
+    key_ref[...] = keys_of(meta_ref[...], n)[0]
+    deal(key_ref, part_ref[...], outs, outs[0].shape[0])
+
+
+def expert_body(n, shifts, sender, win_ref, wout_ref, *refs):
     near = n // 2
-    packs, refs = refs[: len(groups) * len(offsets)], refs[len(groups) * len(offsets) :]
-    second_ref, hidden_ref = refs[:2]
-    outs = refs[2 : 2 + near]
-    hid, key_ref = refs[2 + near :]
-    project_some(n, offsets, groups, packs, att_ref, res_ref, second_ref, 0)
-    h, normed = assemble(n, lax.axis_index("seq"), shifts, first_ref, second_ref, hid)
-    hidden_ref[...] = h.astype(BF)
-    key_ref[...] = keys_of(meta_ref[...], n)[0]
-    deal(key_ref, normed, outs, outs[0].shape[0])
-
-
-def deal_body(n, shifts, first_ref, second_ref, meta_ref, *refs):
-    outs, hid, key_ref = refs[:-2], refs[-2], refs[-1]
-    key_ref[...] = keys_of(meta_ref[...], n)[0]
-    sender = jnp.bitwise_xor(lax.axis_index("seq"), n // 2)
-    normed = assemble(n, sender, shifts, first_ref, second_ref, hid)[1]
-    deal(key_ref, normed, outs, outs[0].shape[0])
-
-
-def expert_body(parts, win_ref, wout_ref, *refs):
-    ins, outs = refs[:parts], refs[parts:]
-    cap = ins[0].shape[0]
-    x = jnp.concatenate([r[...] for r in ins], axis=0)
+    firsts, seconds, outs, rows_ref = refs[:near], refs[near : 2 * near], refs[2 * near : 3 * near], refs[-1]
+    cap = firsts[0].shape[0]
+    s = lax.axis_index("seq")
+    for k in range(near):
+        owner = jnp.bitwise_xor(s, k ^ sender)
+        assemble(n, owner, shifts, firsts[k], seconds[k], rows_ref, k * cap)
+    h = rows_ref[...]
+    x = (h * lax.rsqrt(jnp.mean(h * h, axis=-1, keepdims=True) + 1e-06)).astype(BF)
     act = dot(x, win_ref[0])
     gate = act[:, :HE]
     inner = (gate / (1.0 + jnp.exp(-gate)) * act[:, HE:]).astype(BF)
     rows = dot(inner, wout_ref[0]).astype(BF)
-    for k in range(parts):
+    for k in range(near):
         outs[k][...] = rows[k * cap : (k + 1) * cap, :]
 
 
@@ -257,10 +267,10 @@
     out_ref[...] = gather_rows(n, meta_ref[...], ins, key_ref, gate_ref).astype(BF)
 
 
-def settle_body(n, meta_ref, hidden_ref, *refs):
-    ins, out_ref, key_ref, gate_ref = refs[:-3], refs[-3], refs[-2], refs[-1]
-    total = gather_rows(n, meta_ref[...], ins, key_ref, gate_ref)
-    out_ref[...] = total + hidden_ref[...].astype(F32)
+def settle_body(n, shifts, meta_ref, first_ref, second_ref, *refs):
+    ins, out_ref, hid, key_ref, gate_ref = refs[:-4], refs[-4], refs[-3], refs[-2], refs[-1]
+    assemble(n, lax.axis_index("seq"), shifts, first_ref, second_ref, hid, 0)
+    out_ref[...] = gather_rows(n, meta_ref[...], ins, key_ref, gate_ref) + hid[...]
 
 
 def final_body(total_ref, other_ref, out_ref):
@@ -307,19 +317,19 @@
         offsets = offsets + [o ^ bit for o in offsets]
         bit //= 2
 
-    def share(x):
-        held = [x]
-        for k in spread:
+    def share(held):
+        for k in spread[len(held) - 1 :]:
             pairs = [(i, i ^ k) for i in range(copies)]
             held = held + [lax.ppermute(h, "win", pairs) for h in held]
         return held
 
     width = out_weight.shape[1]
-    mine, sent, meta, piece = kernel(
-        states_body,
-        (sds((half, DV), F32), sds((half, DV), BF), sds((2 * TOP, length), F32), sds((rows, width), BF)),
+    piece_buf = sds((rows, width), BF)
+    mine, sent, meta, piece, extra = kernel(
+        functools.partial(states_body, spread[0]),
+        (sds((half, DV), F32), sds((half, DV), BF), sds((2 * TOP, length), F32), piece_buf, piece_buf),
         (key_rows, value_rows, expert_ids.T, gate_values.T, out_weight),
-        [pltpu.VMEM((2 * half, DV), F32), pltpu.SemaphoreType.DMA],
+        [pltpu.VMEM((2 * half, DV), F32), pltpu.SemaphoreType.DMA((2,))],
         in_hbm=(4,),
         loads=True,
     )
@@ -346,19 +356,20 @@
         if j < near - 1:
             b = lax.ppermute(b, "seq", back)
             bs.append(b)
-    steps = [[j] for j in range(near - 2)] + [[near - 2, near - 1]]
+    extra_f = lax.ppermute(extra, "seq", ahead)
+    extra_b = lax.ppermute(extra, "seq", back)
     groups, packs = [], []
-    for js in steps:
-        shifts, xs = [], []
-        for j in js:
-            shifts.append(-(j + 1))
-            xs.append(fs[j])
-            if j < near - 1:
-                shifts.append(j + 1)
-                xs.append(bs[j])
-        groups.append(shifts)
-        pack = kernel(pack_body, sds((rows * len(xs), width), BF), xs)
-        packs += share(pack)
+    for j in range(near):
+        both = j < near - 1
+        groups.append([-(j + 1), j + 1] if both else [-(j + 1)])
+        if both:
+            buf = sds((2 * rows, width), BF)
+            held = [kernel(pack_body, buf, (fs[j], bs[j]))]
+            if j == 0:
+                held.append(kernel(pack_body, buf, (extra_f, extra_b)))
+        else:
+            held = [fs[j]]
+        packs += share(held)
 
     tokens = (queries, key_rows, value_rows)
     intra = [
@@ -368,54 +379,58 @@
     row_buf = sds((cap, D), BF)
     full = sds((length, D), BF)
     keys = pltpu.VMEM((n, length), F32)
-    early, late = groups[:-1], groups[-1:]
-    ahead_packs, last_packs = packs[:-copies], packs[-copies:]
     shifts = [0] + [x for g in groups for x in g]
-    left = len(groups[-1])
-    some = sds((length, (n - left) * width), BF)
-    rest = sds((length, left * width), BF)
-    whole = pltpu.VMEM((length, D), F32)
-    att, first = kernel(
-        functools.partial(early_body, n, offsets, early),
-        (sds((length, H * DV), BF), some),
-        (queries, *intra, prefix_mine, prefix_other, out_weight, residual, *ahead_packs),
-        [pltpu.VMEM((2 * half, DV), BF)],
-    )
-    first_far = flip(first, near)
-    second, hidden, *deal_own = kernel(
-        functools.partial(late_body, n, offsets, late, shifts),
-        (rest, full, *[row_buf] * near),
-        (att, first, residual, meta, *last_packs),
-        [whole, keys],
-    )
-    second_far = flip(second, near)
-    own_in = flips(deal_own)
-    deal_far = kernel(
-        functools.partial(deal_body, n, shifts),
-        tuple([row_buf] * near),
-        (first_far, second_far, meta_far),
-        [whole, keys],
-    )
-    far_in = flips(deal_far)
-
-    def experts(xs):
+    begun = near // 2
+    done = 1 + sum(len(g) for g in groups[:begun])
+    parts = (done * width, (n - done) * width)
+    bufs = [[sds((cap, p), BF)] * near for p in parts]
+    att, first, *own_a = kernel(
+        functools.partial(early_body, n, offsets, groups[:begun]),
+        (sds((length, H * DV), BF), sds((length, parts[0]), BF), *bufs[0]),
+        (
+            queries,
+            *intra,
+            prefix_mine,
+            prefix_other,
+            out_weight,
+            residual,
+            meta,
+            *packs[: begun * copies],
+        ),
+        [pltpu.VMEM((2 * half, DV), BF), keys],
+    )
+    second, *own_b = kernel(
+        functools.partial(late_body, n, offsets, groups[begun:]),
+        (sds((length, parts[1]), BF), *bufs[1]),
+        (att, residual, meta, *packs[begun * copies :]),
+        [keys],
+    )
+
+    def dealt(x, i):
+        return kernel(functools.partial(deal_body, n), tuple(bufs[i]), (x, meta_far), [keys])
+
+    far_a = dealt(flip(first, near), 0)
+    far_b = dealt(flip(second, near), 1)
+
+    def experts(sender, xs):
         return kernel(
-            functools.partial(expert_body, near),
+            functools.partial(expert_body, n, shifts, sender),
             tuple([row_buf] * near),
             (expert_in, expert_out, *xs),
+            [pltpu.VMEM((near * cap, D), F32)],
         )
 
-    own_out = experts(own_in)
+    own_out = experts(0, flips(own_a) + flips(own_b))
+    far_out = experts(near, flips(far_a) + flips(far_b))
     own_back = flips(own_out)
-    far_out = experts(far_in)
     far_back = flips(far_out)
     part_far = kernel(functools.partial(partial_body, n), full, (meta_far, *far_back), [keys, keys])
     part_own = flip(part_far, near)
     settled = kernel(
-        functools.partial(settle_body, n),
+        functools.partial(settle_body, n, shifts),
         sds((length, D), F32),
-        (meta, hidden, *own_back),
-        [keys, keys],
+        (meta, first, second, *own_back),
+        [pltpu.VMEM((length, D), F32), keys, keys],
     )
     return kernel(final_body, jax.ShapeDtypeStruct((length, D), BF), (settled, part_own))
 

time: 104 us -> 104 us (level)
  waiting for transfers between devices: 51 us -> 42.9 us
  starting transfers between devices: 41.7 us -> 48.9 us
    ppermute x4, waiting for transfers between devices: 12.7 us -> 5.43 us  [small_group(): f = lax.ppermute(f, 'seq', ahead)]
    ppermute x20 -> x26, waiting for transfers between devices: 38.3 us -> 33.7 us  [flip(): return lax.ppermute(x, 'seq', [(i, i ^ k) for i in range(n)])]
    ppermute x20 -> x26, starting transfers between devices: 27.6 us -> 31.8 us  [flip(): return lax.ppermute(x, 'seq', [(i, i ^ k) for i in range(n)])]
    ppermute x4, starting transfers between devices: 8.73 us -> 6.27 us  [small_group(): f = lax.ppermute(f, 'seq', ahead)]
    ppermute x3, starting transfers between devices: 0.47 us -> 2.77 us  [small_group(): b = lax.ppermute(b, 'seq', back)]
    ppermute x3, waiting for transfers between devices: 0.01 us -> 2.21 us  [small_group(): b = lax.ppermute(b, 'seq', back)]
    ppermute x0 -> x2, starting transfers between devices: none -> 2.03 us  [the longest x1 1.14 us: small_group(): extra_b = lax.ppermute(extra, 'seq', back)]
    ppermute x9 -> x11, waiting for transfers between devices: 0.02 us -> 1.28 us  [share(): held = held + [lax.ppermute(h, 'win', pairs) for h in held]]
  transfers between devices with their start and end apart: 36 -> 46, of which waited for: 18 -> 22; matrix products, arithmetic and copies ran while one was open for 0% -> 0% of each run, Pallas kernels for 6% -> 7%
where the time goes in v7:
time: 104 us
  starting transfers between devices  48.9 us (47%)
  waiting for transfers between devices  42.9 us (41%)
  Pallas kernels  12 us (12%)
    ppermute x26, waiting for transfers between devices, flip(): return lax.ppermute(x, 'seq', [(i, i ^ k) for i in range(n)])  33.7 us
    ppermute x26, starting transfers between devices, flip(): return lax.ppermute(x, 'seq', [(i, i ^ k) for i in range(n)])  31.8 us
    pallas_call x19, Pallas kernels, call(): run(*[pltpu.with_memory_space_constraint(x, m) for x, m in zip(xs, spaces)])  12 us
    ppermute x4, starting transfers between devices, small_group(): f = lax.ppermute(f, 'seq', ahead)  6.27 us
    ppermute x11, starting transfers between devices, share(): held = held + [lax.ppermute(h, 'win', pairs) for h in held]  6.08 us
    ppermute x4, waiting for transfers between devices, small_group(): f = lax.ppermute(f, 'seq', ahead)  5.43 us
    ppermute x3, starting transfers between devices, small_group(): b = lax.ppermute(b, 'seq', back)  2.77 us
    ppermute x3, waiting for transfers between devices, small_group(): b = lax.ppermute(b, 'seq', back)  2.21 us
  transfers between devices with their start and end apart: 46, of which 22 were waited for; matrix products, arithmetic and copies ran while one was open for 0% of the time, Pallas kernels for 7%

profile of v7, /device:TPU:0, one launch (start us, length us, event | category | flops | bytes accessed | tf_op | source)
XLA Modules:
  0.0 104.2 jit_solution(13069526412065979749)
XLA Ops:
  0.0 2.1 %shard_map.91 = (f32[512,128]{1,0:T(8,128)S(1)}, bf16[512,128]{1,0:T(8,128)(2,1)S(1)}, f32[4,128]{1,0:T(4,128)S(1)}, bf16[512,128]{1,0:T(8,128)(2,1)S(1)}, bf16[512,128]{1,0:T(8,128)(2,1)S(1)}) custom-call(bf16[128,1024]{1,0:T(8,128)(2,1)} %k_ref.5, bf16[128,2048]{1,0:T(8,128)(2,1)} %v_ref.5, s32[2,128]{1,0:T(2,128)} %bitcast.2, f32[2,128]{1,0:T(2,128)} %bitcast.3, ...), custom_call_target="tpu_custom_call" | custom-call | tf_op jit(solution)/shard_map/pallas_call | solution.py:34
  2.1 3.1 %collective-permute-start.4 = (bf16[512,128]{1,0:T(8,128)(2,1)S(1)}, bf16[512,128]{1,0:T(8,128)(2,1)S(1)}, u32[]{:S(2)}, u32[]{:S(2)}) collective-permute-start(bf16[512,128]{1,0:T(8,128)(2,1)S(1)} %get-tuple-element.44), channel_id=1, source_target_pairs={{0,8},{8,16},{16,24},{24,28},{28,20},{20,12},{12,4},{4,0},{1,9},{9... | collective-permute-start | bytes 393224 | tf_op jit(solution)/shard_map/ppermute | solution.py:354
  5.2 2.0 %collective-permute-start = (bf16[512,128]{1,0:T(8,128)(2,1)S(1)}, bf16[512,128]{1,0:T(8,128)(2,1)S(1)}, u32[]{:S(2)}, u32[]{:S(2)}) collective-permute-start(bf16[512,128]{1,0:T(8,128)(2,1)S(1)} %get-tuple-element.41), channel_id=1, source_target_pairs={{0,4},{4,0},{8,12},{12,8},{16,20},{20,16},{24,28},{28,24},{1,5},{5... | collective-permute-start | bytes 393224 | tf_op jit(solution)/shard_map/ppermute | solution.py:303
  7.2 2.3 %collective-permute-done.4.refs_0_ = bf16[512,128]{1,0:T(8,128)(2,1)S(1)} collective-permute-done((bf16[512,128]{1,0:T(8,128)(2,1)S(1)}, bf16[512,128]{1,0:T(8,128)(2,1)S(1)}, u32[]{:S(2)}, u32[]{:S(2)}) %collective-permute-start.4) | collective-permute-done | bytes 131104 | tf_op jit(solution)/shard_map/ppermute | solution.py:354
  16.9 1.6 %collective-permute-start.12 = (bf16[1024,128]{1,0:T(8,128)(2,1)S(1)}, bf16[1024,128]{1,0:T(8,128)(2,1)S(1)}, u32[]{:S(2)}, u32[]{:S(2)}) collective-permute-start(bf16[1024,128]{1,0:T(8,128)(2,1)S(1)} %shard_map.99.refs_4_), channel_id=1, source_target_pairs={{0,2},{1,3},{2,0},{3,1},{4,6},{5,7},{6,4},{7,5},{8,10},{9,11},{10,... | collective-permute-start | bytes 786440 | tf_op jit(solution)/shard_map/ppermute | solution.py:323
  20.3 1.6 %collective-permute-start.16 = (bf16[512,128]{1,0:T(8,128)(2,1)S(1)}, bf16[512,128]{1,0:T(8,128)(2,1)S(1)}, u32[]{:S(2)}, u32[]{:S(2)}) collective-permute-start(bf16[512,128]{1,0:T(8,128)(2,1)S(1)} %collective-permute-done.11.refs_1_), channel_id=1, source_target_pairs={{8,0},{16,8},{24,16},{28,24},{20,28},{12,20},{4,12},{0,4},{9,1},{1... | collective-permute-start | bytes 393224 | tf_op jit(solution)/shard_map/ppermute | solution.py:357
  21.9 1.6 %collective-permute-start.2 = (bf16[512,128]{1,0:T(8,128)(2,1)S(1)}, bf16[512,128]{1,0:T(8,128)(2,1)S(1)}, u32[]{:S(2)}, u32[]{:S(2)}) collective-permute-start(bf16[512,128]{1,0:T(8,128)(2,1)S(1)} %shard_map.95), channel_id=1, source_target_pairs={{0,16},{4,20},{8,24},{12,28},{16,0},{20,4},{24,8},{28,12},{1,17},{... | collective-permute-start | bytes 393224 | tf_op jit(solution)/shard_map/ppermute | solution.py:303
  23.5 2.2 %collective-permute-done.16.refs_1_ = bf16[512,128]{1,0:T(8,128)(2,1)S(1)} collective-permute-done((bf16[512,128]{1,0:T(8,128)(2,1)S(1)}, bf16[512,128]{1,0:T(8,128)(2,1)S(1)}, u32[]{:S(2)}, u32[]{:S(2)}) %collective-permute-start.16) | collective-permute-done | bytes 131104 | tf_op jit(solution)/shard_map/ppermute | solution.py:357
  25.8 2.1 %collective-permute-start.17 = (bf16[1024,128]{1,0:T(8,128)(2,1)S(1)}, bf16[1024,128]{1,0:T(8,128)(2,1)S(1)}, u32[]{:S(2)}, u32[]{:S(2)}) collective-permute-start(bf16[1024,128]{1,0:T(8,128)(2,1)S(1)} %shard_map.101.refs_0_), channel_id=1, source_target_pairs={{0,2},{1,3},{2,0},{3,1},{4,6},{5,7},{6,4},{7,5},{8,10},{9,11},{10,... | collective-permute-start | bytes 786440 | tf_op jit(solution)/shard_map/ppermute | solution.py:323
  27.8 4.0 %collective-permute-done.2.refs_1_ = bf16[512,128]{1,0:T(8,128)(2,1)S(1)} collective-permute-done((bf16[512,128]{1,0:T(8,128)(2,1)S(1)}, bf16[512,128]{1,0:T(8,128)(2,1)S(1)}, u32[]{:S(2)}, u32[]{:S(2)}) %collective-permute-start.2) | collective-permute-done | bytes 131104 | tf_op jit(solution)/shard_map/ppermute | solution.py:303
  33.9 5.1 %collective-permute-done.3.po_ref = bf16[512,128]{1,0:T(8,128)(2,1)S(1)} collective-permute-done((bf16[512,128]{1,0:T(8,128)(2,1)S(1)}, bf16[512,128]{1,0:T(8,128)(2,1)S(1)}, u32[]{:S(2)}, u32[]{:S(2)}) %collective-permute-start.3) | collective-permute-done | bytes 131104 | tf_op jit(solution)/shard_map/ppermute | solution.py:303
  38.9 1.8 %collective-permute-done.20.refs_4_ = bf16[512,128]{1,0:T(8,128)(2,1)S(1)} collective-permute-done((bf16[512,128]{1,0:T(8,128)(2,1)S(1)}, bf16[512,128]{1,0:T(8,128)(2,1)S(1)}, u32[]{:S(2)}, u32[]{:S(2)}) %collective-permute-start.20) | collective-permute-done | bytes 131104 | tf_op jit(solution)/shard_map/ppermute | solution.py:354
  41.8 1.3 %shard_map.92.ia_ref = f32[128,1024]{1,0:T(8,128)S(1)} custom-call(bf16[128,1024]{1,0:T(8,128)(2,1)S(1)} %copy-done.4, bf16[128,1024]{1,0:T(8,128)(2,1)S(1)} %copy-done.3, bf16[128,2048]{1,0:T(8,128)(2,1)S(1)} %copy-done.1), custom_call_target="tpu_custom_call" | custom-call | tf_op jit(solution)/shard_map/pallas_call | solution.py:34
  43.1 1.3 %shard_map.93.ib_ref = f32[128,1024]{1,0:T(8,128)S(1)} custom-call(bf16[128,1024]{1,0:T(8,128)(2,1)S(1)} %copy-done.4, bf16[128,1024]{1,0:T(8,128)(2,1)S(1)} %copy-done.3, bf16[128,2048]{1,0:T(8,128)(2,1)S(1)} %copy-done.1), custom_call_target="tpu_custom_call" | custom-call | tf_op jit(solution)/shard_map/pallas_call | solution.py:34
  48.2 2.6 %collective-permute-start.38 = (bf16[128,384]{1,0:T(8,128)(2,1)S(1)}, bf16[128,384]{1,0:T(8,128)(2,1)S(1)}, u32[]{:S(2)}, u32[]{:S(2)}) collective-permute-start(bf16[128,384]{1,0:T(8,128)(2,1)S(1)} %get-tuple-element.48.second_ref), channel_id=1, source_target_pairs={{0,16},{4,20},{8,24},{12,28},{16,0},{20,4},{24,8},{28,12},{1,17},{... | collective-permute-start | bytes 294920 | tf_op jit(solution)/shard_map/ppermute | solution.py:303
  51.2 8.8 %collective-permute-done.33.meta_ref = f32[4,128]{1,0:T(4,128)S(1)} collective-permute-done((f32[4,128]{1,0:T(4,128)S(1)}, f32[4,128]{1,0:T(4,128)S(1)}, u32[]{:S(2)}, u32[]{:S(2)}) %collective-permute-start.33) | collective-permute-done | bytes 2080 | tf_op jit(solution)/shard_map/ppermute | solution.py:303
  60.9 3.0 %collective-permute-start.37 = (bf16[64,640]{1,0:T(8,128)(2,1)S(1)}, bf16[64,640]{1,0:T(8,128)(2,1)S(1)}, u32[]{:S(2)}, u32[]{:S(2)}) collective-permute-start(bf16[64,640]{1,0:T(8,128)(2,1)S(1)} %get-tuple-element.64), channel_id=1, source_target_pairs={{0,12},{4,8},{8,4},{12,0},{16,28},{20,24},{24,20},{28,16},{1,13},{... | collective-permute-start | bytes 245768 | tf_op jit(solution)/shard_map/ppermute | solution.py:303
  64.9 2.9 %collective-permute-start.41 = (bf16[64,384]{1,0:T(8,128)(2,1)S(1)}, bf16[64,384]{1,0:T(8,128)(2,1)S(1)}, u32[]{:S(2)}, u32[]{:S(2)}) collective-permute-start(bf16[64,384]{1,0:T(8,128)(2,1)S(1)} %get-tuple-element.68), channel_id=1, source_target_pairs={{0,12},{4,8},{8,4},{12,0},{16,28},{20,24},{24,20},{28,16},{1,13},{... | collective-permute-start | bytes 147464 | tf_op jit(solution)/shard_map/ppermute | solution.py:303
  69.1 1.3 %collective-permute-done.41.refs_7_ = bf16[64,384]{1,0:T(8,128)(2,1)S(1)} collective-permute-done((bf16[64,384]{1,0:T(8,128)(2,1)S(1)}, bf16[64,384]{1,0:T(8,128)(2,1)S(1)}, u32[]{:S(2)}, u32[]{:S(2)}) %collective-permute-start.41) | collective-permute-done | bytes 49184 | tf_op jit(solution)/shard_map/ppermute | solution.py:303
  70.4 1.5 %shard_map.107 = (bf16[64,1024]{1,0:T(8,128)(2,1)S(1)}, bf16[64,1024]{1,0:T(8,128)(2,1)S(1)}, bf16[64,1024]{1,0:T(8,128)(2,1)S(1)}, bf16[64,1024]{1,0:T(8,128)(2,1)S(1)}) custom-call(bf16[1,1024,768]{2,1,0:T(8,128)(2,1)S(1)} %copy-done, bf16[1,384,1024]{2,1,0:T(8,128)(2,1)S(1)} %copy-done.2, bf16[64,640]{1,0:T(8,128)(2,1)S(1)} %get-tuple-element.61.refs_0_, ...), custom_call_target="tpu_custom_call" | custom-call | tf_op jit(solution)/shard_map/pallas_call | solution.py:34
  72.8 2.0 %collective-permute-start.43 = (bf16[64,1024]{1,0:T(8,128)(2,1)S(1)}, bf16[64,1024]{1,0:T(8,128)(2,1)S(1)}, u32[]{:S(2)}, u32[]{:S(2)}) collective-permute-start(bf16[64,1024]{1,0:T(8,128)(2,1)S(1)} %get-tuple-element.71), channel_id=1, source_target_pairs={{0,8},{4,12},{8,0},{12,4},{16,24},{20,28},{24,16},{28,20},{1,9},{5... | collective-permute-start | bytes 393224 | tf_op jit(solution)/shard_map/ppermute | solution.py:303
  76.3 2.0 %collective-permute-start.25 = (bf16[64,640]{1,0:T(8,128)(2,1)S(1)}, bf16[64,640]{1,0:T(8,128)(2,1)S(1)}, u32[]{:S(2)}, u32[]{:S(2)}) collective-permute-start(bf16[64,640]{1,0:T(8,128)(2,1)S(1)} %get-tuple-element.51), channel_id=1, source_target_pairs={{0,8},{4,12},{8,0},{12,4},{16,24},{20,28},{24,16},{28,20},{1,9},{5... | collective-permute-start | bytes 245768 | tf_op jit(solution)/shard_map/ppermute | solution.py:303
  79.1 1.7 %collective-permute-done.44.refs_3_ = bf16[64,1024]{1,0:T(8,128)(2,1)S(1)} collective-permute-done((bf16[64,1024]{1,0:T(8,128)(2,1)S(1)}, bf16[64,1024]{1,0:T(8,128)(2,1)S(1)}, u32[]{:S(2)}, u32[]{:S(2)}) %collective-permute-start.44) | collective-permute-done | bytes 131104 | tf_op jit(solution)/shard_map/ppermute | solution.py:303
  82.4 1.3 %collective-permute-start.26 = (bf16[64,640]{1,0:T(8,128)(2,1)S(1)}, bf16[64,640]{1,0:T(8,128)(2,1)S(1)}, u32[]{:S(2)}, u32[]{:S(2)}) collective-permute-start(bf16[64,640]{1,0:T(8,128)(2,1)S(1)} %get-tuple-element.52), channel_id=1, source_target_pairs={{0,12},{4,8},{8,4},{12,0},{16,28},{20,24},{24,20},{28,16},{1,13},{... | collective-permute-start | bytes 245768 | tf_op jit(solution)/shard_map/ppermute | solution.py:303
  83.7 3.1 %collective-permute-start.27 = (bf16[64,384]{1,0:T(8,128)(2,1)S(1)}, bf16[64,384]{1,0:T(8,128)(2,1)S(1)}, u32[]{:S(2)}, u32[]{:S(2)}) collective-permute-start(bf16[64,384]{1,0:T(8,128)(2,1)S(1)} %get-tuple-element.54), channel_id=1, source_target_pairs={{0,4},{4,0},{8,12},{12,8},{16,20},{20,16},{24,28},{28,24},{1,5},{5... | collective-permute-start | bytes 147464 | tf_op jit(solution)/shard_map/ppermute | solution.py:303
  86.9 1.5 %collective-permute-start.29 = (bf16[64,384]{1,0:T(8,128)(2,1)S(1)}, bf16[64,384]{1,0:T(8,128)(2,1)S(1)}, u32[]{:S(2)}, u32[]{:S(2)}) collective-permute-start(bf16[64,384]{1,0:T(8,128)(2,1)S(1)} %get-tuple-element.56), channel_id=1, source_target_pairs={{0,12},{4,8},{8,4},{12,0},{16,28},{20,24},{24,20},{28,16},{1,13},{... | collective-permute-start | bytes 147464 | tf_op jit(solution)/shard_map/ppermute | solution.py:303
  88.9 4.1 %collective-permute-done.28.refs_6_ = bf16[64,384]{1,0:T(8,128)(2,1)S(1)} collective-permute-done((bf16[64,384]{1,0:T(8,128)(2,1)S(1)}, bf16[64,384]{1,0:T(8,128)(2,1)S(1)}, u32[]{:S(2)}, u32[]{:S(2)}) %collective-permute-start.28) | collective-permute-done | bytes 49184 | tf_op jit(solution)/shard_map/ppermute | solution.py:303
  93.6 1.4 %shard_map.103 = (bf16[64,1024]{1,0:T(8,128)(2,1)S(1)}, bf16[64,1024]{1,0:T(8,128)(2,1)S(1)}, bf16[64,1024]{1,0:T(8,128)(2,1)S(1)}, bf16[64,1024]{1,0:T(8,128)(2,1)S(1)}) custom-call(bf16[1,1024,768]{2,1,0:T(8,128)(2,1)S(1)} %copy-done, bf16[1,384,1024]{2,1,0:T(8,128)(2,1)S(1)} %copy-done.2, bf16[64,640]{1,0:T(8,128)(2,1)S(1)} %get-tuple-element.49.refs_0_, ...), custom_call_target="tpu_custom_call" | custom-call | tf_op jit(solution)/shard_map/pallas_call | solution.py:34
  95.1 1.9 %collective-permute-start.30 = (bf16[64,1024]{1,0:T(8,128)(2,1)S(1)}, bf16[64,1024]{1,0:T(8,128)(2,1)S(1)}, u32[]{:S(2)}, u32[]{:S(2)}) collective-permute-start(bf16[64,1024]{1,0:T(8,128)(2,1)S(1)} %get-tuple-element.58), channel_id=1, source_target_pairs={{0,4},{4,0},{8,12},{12,8},{16,20},{20,16},{24,28},{28,24},{1,5},{5... | collective-permute-start | bytes 393224 | tf_op jit(solution)/shard_map/ppermute | solution.py:303
  97.0 1.6 %collective-permute-start.32 = (bf16[64,1024]{1,0:T(8,128)(2,1)S(1)}, bf16[64,1024]{1,0:T(8,128)(2,1)S(1)}, u32[]{:S(2)}, u32[]{:S(2)}) collective-permute-start(bf16[64,1024]{1,0:T(8,128)(2,1)S(1)} %get-tuple-element.60), channel_id=1, source_target_pairs={{0,12},{4,8},{8,4},{12,0},{16,28},{20,24},{24,20},{28,16},{1,13},{... | collective-permute-start | bytes 393224 | tf_op jit(solution)/shard_map/ppermute | solution.py:303
  98.6 1.5 %collective-permute-done.30.refs_1_ = bf16[64,1024]{1,0:T(8,128)(2,1)S(1)} collective-permute-done((bf16[64,1024]{1,0:T(8,128)(2,1)S(1)}, bf16[64,1024]{1,0:T(8,128)(2,1)S(1)}, u32[]{:S(2)}, u32[]{:S(2)}) %collective-permute-start.30) | collective-permute-done | bytes 131104 | tf_op jit(solution)/shard_map/ppermute | solution.py:303
  100.1 1.9 %collective-permute-done.31.refs_2_ = bf16[64,1024]{1,0:T(8,128)(2,1)S(1)} collective-permute-done((bf16[64,1024]{1,0:T(8,128)(2,1)S(1)}, bf16[64,1024]{1,0:T(8,128)(2,1)S(1)}, u32[]{:S(2)}, u32[]{:S(2)}) %collective-permute-start.31) | collective-permute-done | bytes 131104 | tf_op jit(solution)/shard_map/ppermute | solution.py:303
  (93 shorter events, 27.7 us)
Async XLA Ops:
  2.1 7.4 %collective-permute-start.4 = (bf16[512,128]{1,0:T(8,128)(2,1)S(1)}, bf16[512,128]{1,0:T(8,128)(2,1)S(1)}, u32[]{:S(2)}, u32[]{:S(2)}) collective-permute-start(bf16[512,128]{1,0:T(8,128)(2,1)S(1)} %get-tuple-element.44), channel_id=1, source_target_pairs={{0,8},{8,16},{16,24},{24,28},{28,20},{20,12},{12,4},{4,0},{1,9},{9... | collective-permute-start | bytes 393224 | tf_op jit(solution)/shard_map/ppermute | solution.py:354
  5.2 8.4 %collective-permute-start = (bf16[512,128]{1,0:T(8,128)(2,1)S(1)}, bf16[512,128]{1,0:T(8,128)(2,1)S(1)}, u32[]{:S(2)}, u32[]{:S(2)}) collective-permute-start(bf16[512,128]{1,0:T(8,128)(2,1)S(1)} %get-tuple-element.41), channel_id=1, source_target_pairs={{0,4},{4,0},{8,12},{12,8},{16,20},{20,16},{24,28},{28,24},{1,5},{5... | collective-permute-start | bytes 393224 | tf_op jit(solution)/shard_map/ppermute | solution.py:303
  9.5 6.4 %collective-permute-start.10 = (bf16[512,128]{1,0:T(8,128)(2,1)S(1)}, bf16[512,128]{1,0:T(8,128)(2,1)S(1)}, u32[]{:S(2)}, u32[]{:S(2)}) collective-permute-start(bf16[512,128]{1,0:T(8,128)(2,1)S(1)} %collective-permute-done.4.refs_0_), channel_id=1, source_target_pairs={{0,8},{8,16},{16,24},{24,28},{28,20},{20,12},{12,4},{4,0},{1,9},{9... | collective-permute-start | bytes 393224 | tf_op jit(solution)/shard_map/ppermute | solution.py:354
  10.5 6.4 %collective-permute-start.11 = (bf16[512,128]{1,0:T(8,128)(2,1)S(1)}, bf16[512,128]{1,0:T(8,128)(2,1)S(1)}, u32[]{:S(2)}, u32[]{:S(2)}) collective-permute-start(bf16[512,128]{1,0:T(8,128)(2,1)S(1)} %collective-permute-done.5.refs_1_), channel_id=1, source_target_pairs={{8,0},{16,8},{24,16},{28,24},{20,28},{12,20},{4,12},{0,4},{9,1},{1... | collective-permute-start | bytes 393224 | tf_op jit(solution)/shard_map/ppermute | solution.py:357
  11.6 6.9 %collective-permute-start.6 = (bf16[512,128]{1,0:T(8,128)(2,1)S(1)}, bf16[512,128]{1,0:T(8,128)(2,1)S(1)}, u32[]{:S(2)}, u32[]{:S(2)}) collective-permute-start(bf16[512,128]{1,0:T(8,128)(2,1)S(1)} %get-tuple-element.45), channel_id=1, source_target_pairs={{0,8},{8,16},{16,24},{24,28},{28,20},{20,12},{12,4},{4,0},{1,9},{9... | collective-permute-start | bytes 393224 | tf_op jit(solution)/shard_map/ppermute | solution.py:359
  12.5 6.4 %collective-permute-start.7 = (bf16[512,128]{1,0:T(8,128)(2,1)S(1)}, bf16[512,128]{1,0:T(8,128)(2,1)S(1)}, u32[]{:S(2)}, u32[]{:S(2)}) collective-permute-start(bf16[512,128]{1,0:T(8,128)(2,1)S(1)} %get-tuple-element.45), channel_id=1, source_target_pairs={{8,0},{16,8},{24,16},{28,24},{20,28},{12,20},{4,12},{0,4},{9,1},{1... | collective-permute-start | bytes 393224 | tf_op jit(solution)/shard_map/ppermute | solution.py:360
  13.7 6.6 %collective-permute-start.1 = (bf16[512,128]{1,0:T(8,128)(2,1)S(1)}, bf16[512,128]{1,0:T(8,128)(2,1)S(1)}, u32[]{:S(2)}, u32[]{:S(2)}) collective-permute-start(bf16[512,128]{1,0:T(8,128)(2,1)S(1)} %shard_map.94), channel_id=1, source_target_pairs={{0,8},{4,12},{8,0},{12,4},{16,24},{20,28},{24,16},{28,20},{1,9},{5... | collective-permute-start | bytes 393224 | tf_op jit(solution)/shard_map/ppermute | solution.py:303
  15.9 6.0 %collective-permute-start.15 = (bf16[512,128]{1,0:T(8,128)(2,1)S(1)}, bf16[512,128]{1,0:T(8,128)(2,1)S(1)}, u32[]{:S(2)}, u32[]{:S(2)}) collective-permute-start(bf16[512,128]{1,0:T(8,128)(2,1)S(1)} %collective-permute-done.10.refs_0_), channel_id=1, source_target_pairs={{0,8},{8,16},{16,24},{24,28},{28,20},{20,12},{12,4},{4,0},{1,9},{9... | collective-permute-start | bytes 393224 | tf_op jit(solution)/shard_map/ppermute | solution.py:354
  16.9 15.0 %collective-permute-start.12 = (bf16[1024,128]{1,0:T(8,128)(2,1)S(1)}, bf16[1024,128]{1,0:T(8,128)(2,1)S(1)}, u32[]{:S(2)}, u32[]{:S(2)}) collective-permute-start(bf16[1024,128]{1,0:T(8,128)(2,1)S(1)} %shard_map.99.refs_4_), channel_id=1, source_target_pairs={{0,2},{1,3},{2,0},{3,1},{4,6},{5,7},{6,4},{7,5},{8,10},{9,11},{10,... | collective-permute-start | bytes 786440 | tf_op jit(solution)/shard_map/ppermute | solution.py:323
  18.5 14.0 %collective-permute-start.8 = (bf16[1024,128]{1,0:T(8,128)(2,1)S(1)}, bf16[1024,128]{1,0:T(8,128)(2,1)S(1)}, u32[]{:S(2)}, u32[]{:S(2)}) collective-permute-start(bf16[1024,128]{1,0:T(8,128)(2,1)S(1)} %shard_map.97.refs_0_), channel_id=1, source_target_pairs={{0,1},{1,0},{2,3},{3,2},{4,5},{5,4},{6,7},{7,6},{8,9},{9,8},{10,11... | collective-permute-start | bytes 786440 | tf_op jit(solution)/shard_map/ppermute | solution.py:323
  18.9 13.7 %collective-permute-start.9 = (bf16[1024,128]{1,0:T(8,128)(2,1)S(1)}, bf16[1024,128]{1,0:T(8,128)(2,1)S(1)}, u32[]{:S(2)}, u32[]{:S(2)}) collective-permute-start(bf16[1024,128]{1,0:T(8,128)(2,1)S(1)} %shard_map.98.refs_1_), channel_id=1, source_target_pairs={{0,1},{1,0},{2,3},{3,2},{4,5},{5,4},{6,7},{7,6},{8,9},{9,8},{10,11... | collective-permute-start | bytes 786440 | tf_op jit(solution)/shard_map/ppermute | solution.py:323
  21.9 9.9 %collective-permute-start.2 = (bf16[512,128]{1,0:T(8,128)(2,1)S(1)}, bf16[512,128]{1,0:T(8,128)(2,1)S(1)}, u32[]{:S(2)}, u32[]{:S(2)}) collective-permute-start(bf16[512,128]{1,0:T(8,128)(2,1)S(1)} %shard_map.95), channel_id=1, source_target_pairs={{0,16},{4,20},{8,24},{12,28},{16,0},{20,4},{24,8},{28,12},{1,17},{... | collective-permute-start | bytes 393224 | tf_op jit(solution)/shard_map/ppermute | solution.py:303
  25.8 16.0 %collective-permute-start.17 = (bf16[1024,128]{1,0:T(8,128)(2,1)S(1)}, bf16[1024,128]{1,0:T(8,128)(2,1)S(1)}, u32[]{:S(2)}, u32[]{:S(2)}) collective-permute-start(bf16[1024,128]{1,0:T(8,128)(2,1)S(1)} %shard_map.101.refs_0_), channel_id=1, source_target_pairs={{0,2},{1,3},{2,0},{3,1},{4,6},{5,7},{6,4},{7,5},{8,10},{9,11},{10,... | collective-permute-start | bytes 786440 | tf_op jit(solution)/shard_map/ppermute | solution.py:323
  31.8 12.6 %collective-permute-start.13 = (bf16[1024,128]{1,0:T(8,128)(2,1)S(1)}, bf16[1024,128]{1,0:T(8,128)(2,1)S(1)}, u32[]{:S(2)}, u32[]{:S(2)}) collective-permute-start(bf16[1024,128]{1,0:T(8,128)(2,1)S(1)} %shard_map.99.refs_4_), channel_id=1, source_target_pairs={{0,1},{1,0},{2,3},{3,2},{4,5},{5,4},{6,7},{7,6},{8,9},{9,8},{10,11... | collective-permute-start | bytes 786440 | tf_op jit(solution)/shard_map/ppermute | solution.py:323
  31.9 12.6 %collective-permute-start.14 = (bf16[1024,128]{1,0:T(8,128)(2,1)S(1)}, bf16[1024,128]{1,0:T(8,128)(2,1)S(1)}, u32[]{:S(2)}, u32[]{:S(2)}) collective-permute-start(bf16[1024,128]{1,0:T(8,128)(2,1)S(1)} %collective-permute-done.12.refs_5_), channel_id=1, source_target_pairs={{0,1},{1,0},{2,3},{3,2},{4,5},{5,4},{6,7},{7,6},{8,9},{9,8},{10,11... | collective-permute-start | bytes 786440 | tf_op jit(solution)/shard_map/ppermute | solution.py:323
  32.5 6.4 %collective-permute-start.3 = (bf16[512,128]{1,0:T(8,128)(2,1)S(1)}, bf16[512,128]{1,0:T(8,128)(2,1)S(1)}, u32[]{:S(2)}, u32[]{:S(2)}) collective-permute-start(bf16[512,128]{1,0:T(8,128)(2,1)S(1)} %get-tuple-element.43), channel_id=1, source_target_pairs={{0,4},{4,0},{8,12},{12,8},{16,20},{20,16},{24,28},{28,24},{1,5},{5... | collective-permute-start | bytes 393224 | tf_op jit(solution)/shard_map/ppermute | solution.py:303
  32.6 8.2 %collective-permute-start.20 = (bf16[512,128]{1,0:T(8,128)(2,1)S(1)}, bf16[512,128]{1,0:T(8,128)(2,1)S(1)}, u32[]{:S(2)}, u32[]{:S(2)}) collective-permute-start(bf16[512,128]{1,0:T(8,128)(2,1)S(1)} %collective-permute-done.15.refs_0_), channel_id=1, source_target_pairs={{0,8},{8,16},{16,24},{24,28},{28,20},{20,12},{12,4},{4,0},{1,9},{9... | collective-permute-start | bytes 393224 | tf_op jit(solution)/shard_map/ppermute | solution.py:354
  38.9 7.3 %collective-permute-start.18 = (bf16[1024,128]{1,0:T(8,128)(2,1)S(1)}, bf16[1024,128]{1,0:T(8,128)(2,1)S(1)}, u32[]{:S(2)}, u32[]{:S(2)}) collective-permute-start(bf16[1024,128]{1,0:T(8,128)(2,1)S(1)} %shard_map.101.refs_0_), channel_id=1, source_target_pairs={{0,1},{1,0},{2,3},{3,2},{4,5},{5,4},{6,7},{7,6},{8,9},{9,8},{10,11... | collective-permute-start | bytes 786440 | tf_op jit(solution)/shard_map/ppermute | solution.py:323
  45.6 14.4 %collective-permute-start.34 = (bf16[128,640]{1,0:T(8,128)(2,1)S(1)}, bf16[128,640]{1,0:T(8,128)(2,1)S(1)}, u32[]{:S(2)}, u32[]{:S(2)}) collective-permute-start(bf16[128,640]{1,0:T(8,128)(2,1)S(1)} %get-tuple-element.46.first_ref), channel_id=1, source_target_pairs={{0,16},{4,20},{8,24},{12,28},{16,0},{20,4},{24,8},{28,12},{1,17},{... | collective-permute-start | bytes 491528 | tf_op jit(solution)/shard_map/ppermute | solution.py:303
  48.2 15.7 %collective-permute-start.38 = (bf16[128,384]{1,0:T(8,128)(2,1)S(1)}, bf16[128,384]{1,0:T(8,128)(2,1)S(1)}, u32[]{:S(2)}, u32[]{:S(2)}) collective-permute-start(bf16[128,384]{1,0:T(8,128)(2,1)S(1)} %get-tuple-element.48.second_ref), channel_id=1, source_target_pairs={{0,16},{4,20},{8,24},{12,28},{16,0},{20,4},{24,8},{28,12},{1,17},{... | collective-permute-start | bytes 294920 | tf_op jit(solution)/shard_map/ppermute | solution.py:303
  50.8 9.1 %collective-permute-start.33 = (f32[4,128]{1,0:T(4,128)S(1)}, f32[4,128]{1,0:T(4,128)S(1)}, u32[]{:S(2)}, u32[]{:S(2)}) collective-permute-start(f32[4,128]{1,0:T(4,128)S(1)} %get-tuple-element.39.meta_ref), channel_id=1, source_target_pairs={{0,16},{4,20},{8,24},{12,28},{16,0},{20,4},{24,8},{28,12},{1,17},{... | collective-permute-start | bytes 6152 | tf_op jit(solution)/shard_map/ppermute | solution.py:303
  60.9 6.9 %collective-permute-start.36 = (bf16[64,640]{1,0:T(8,128)(2,1)S(1)}, bf16[64,640]{1,0:T(8,128)(2,1)S(1)}, u32[]{:S(2)}, u32[]{:S(2)}) collective-permute-start(bf16[64,640]{1,0:T(8,128)(2,1)S(1)} %get-tuple-element.63), channel_id=1, source_target_pairs={{0,8},{4,12},{8,0},{12,4},{16,24},{20,28},{24,16},{28,20},{1,9},{5... | collective-permute-start | bytes 245768 | tf_op jit(solution)/shard_map/ppermute | solution.py:303
  60.9 7.3 %collective-permute-start.37 = (bf16[64,640]{1,0:T(8,128)(2,1)S(1)}, bf16[64,640]{1,0:T(8,128)(2,1)S(1)}, u32[]{:S(2)}, u32[]{:S(2)}) collective-permute-start(bf16[64,640]{1,0:T(8,128)(2,1)S(1)} %get-tuple-element.64), channel_id=1, source_target_pairs={{0,12},{4,8},{8,4},{12,0},{16,28},{20,24},{24,20},{28,16},{1,13},{... | collective-permute-start | bytes 245768 | tf_op jit(solution)/shard_map/ppermute | solution.py:303
  71.8 7.3 %collective-permute-start.42 = (bf16[64,1024]{1,0:T(8,128)(2,1)S(1)}, bf16[64,1024]{1,0:T(8,128)(2,1)S(1)}, u32[]{:S(2)}, u32[]{:S(2)}) collective-permute-start(bf16[64,1024]{1,0:T(8,128)(2,1)S(1)} %get-tuple-element.70), channel_id=1, source_target_pairs={{0,4},{4,0},{8,12},{12,8},{16,20},{20,16},{24,28},{28,24},{1,5},{5... | collective-permute-start | bytes 393224 | tf_op jit(solution)/shard_map/ppermute | solution.py:303
  72.8 6.3 %collective-permute-start.43 = (bf16[64,1024]{1,0:T(8,128)(2,1)S(1)}, bf16[64,1024]{1,0:T(8,128)(2,1)S(1)}, u32[]{:S(2)}, u32[]{:S(2)}) collective-permute-start(bf16[64,1024]{1,0:T(8,128)(2,1)S(1)} %get-tuple-element.71), channel_id=1, source_target_pairs={{0,8},{4,12},{8,0},{12,4},{16,24},{20,28},{24,16},{28,20},{1,9},{5... | collective-permute-start | bytes 393224 | tf_op jit(solution)/shard_map/ppermute | solution.py:303
  74.9 6.0 %collective-permute-start.44 = (bf16[64,1024]{1,0:T(8,128)(2,1)S(1)}, bf16[64,1024]{1,0:T(8,128)(2,1)S(1)}, u32[]{:S(2)}, u32[]{:S(2)}) collective-permute-start(bf16[64,1024]{1,0:T(8,128)(2,1)S(1)} %get-tuple-element.72), channel_id=1, source_target_pairs={{0,12},{4,8},{8,4},{12,0},{16,28},{20,24},{24,20},{28,16},{1,13},{... | collective-permute-start | bytes 393224 | tf_op jit(solution)/shard_map/ppermute | solution.py:303
  75.4 11.5 %collective-permute-start.24 = (bf16[64,640]{1,0:T(8,128)(2,1)S(1)}, bf16[64,640]{1,0:T(8,128)(2,1)S(1)}, u32[]{:S(2)}, u32[]{:S(2)}) collective-permute-start(bf16[64,640]{1,0:T(8,128)(2,1)S(1)} %get-tuple-element.50), channel_id=1, source_target_pairs={{0,4},{4,0},{8,12},{12,8},{16,20},{20,16},{24,28},{28,24},{1,5},{5... | collective-permute-start | bytes 245768 | tf_op jit(solution)/shard_map/ppermute | solution.py:303
  76.3 10.5 %collective-permute-start.25 = (bf16[64,640]{1,0:T(8,128)(2,1)S(1)}, bf16[64,640]{1,0:T(8,128)(2,1)S(1)}, u32[]{:S(2)}, u32[]{:S(2)}) collective-permute-start(bf16[64,640]{1,0:T(8,128)(2,1)S(1)} %get-tuple-element.51), channel_id=1, source_target_pairs={{0,8},{4,12},{8,0},{12,4},{16,24},{20,28},{24,16},{28,20},{1,9},{5... | collective-permute-start | bytes 245768 | tf_op jit(solution)/shard_map/ppermute | solution.py:303
  81.3 22.2 %collective-permute-start.45 = (bf16[128,1024]{1,0:T(8,128)(2,1)S(1)}, bf16[128,1024]{1,0:T(8,128)(2,1)S(1)}, u32[]{:S(2)}, u32[]{:S(2)}) collective-permute-start(bf16[128,1024]{1,0:T(8,128)(2,1)S(1)} %shard_map.108), channel_id=1, source_target_pairs={{0,16},{4,20},{8,24},{12,28},{16,0},{20,4},{24,8},{28,12},{1,17},{... | collective-permute-start | bytes 786440 | tf_op jit(solution)/shard_map/ppermute | solution.py:303
  86.8 6.1 %collective-permute-start.28 = (bf16[64,384]{1,0:T(8,128)(2,1)S(1)}, bf16[64,384]{1,0:T(8,128)(2,1)S(1)}, u32[]{:S(2)}, u32[]{:S(2)}) collective-permute-start(bf16[64,384]{1,0:T(8,128)(2,1)S(1)} %get-tuple-element.55), channel_id=1, source_target_pairs={{0,8},{4,12},{8,0},{12,4},{16,24},{20,28},{24,16},{28,20},{1,9},{5... | collective-permute-start | bytes 147464 | tf_op jit(solution)/shard_map/ppermute | solution.py:303
  86.9 6.8 %collective-permute-start.29 = (bf16[64,384]{1,0:T(8,128)(2,1)S(1)}, bf16[64,384]{1,0:T(8,128)(2,1)S(1)}, u32[]{:S(2)}, u32[]{:S(2)}) collective-permute-start(bf16[64,384]{1,0:T(8,128)(2,1)S(1)} %get-tuple-element.56), channel_id=1, source_target_pairs={{0,12},{4,8},{8,4},{12,0},{16,28},{20,24},{24,20},{28,16},{1,13},{... | collective-permute-start | bytes 147464 | tf_op jit(solution)/shard_map/ppermute | solution.py:303
  97.0 6.0 %collective-permute-start.32 = (bf16[64,1024]{1,0:T(8,128)(2,1)S(1)}, bf16[64,1024]{1,0:T(8,128)(2,1)S(1)}, u32[]{:S(2)}, u32[]{:S(2)}) collective-permute-start(bf16[64,1024]{1,0:T(8,128)(2,1)S(1)} %get-tuple-element.60), channel_id=1, source_target_pairs={{0,12},{4,8},{8,4},{12,0},{16,28},{20,24},{24,20},{28,16},{1,13},{... | collective-permute-start | bytes 393224 | tf_op jit(solution)/shard_map/ppermute | solution.py:303
  (21 other events, 213.5 us)
